TPU v7x, 256 devices: a whole 4x4x8 slice. The times are simulated.
256 devices in a mesh: tm: 8 (over y, x_hi), lon: 32 (over x_lo, z, core).
Axes of the slice: x: 4 (x_hi: 2, x_lo: 2; x = x_hi * 2 + x_lo), y: 4, z: 8, core: 2. Of those that a mesh axis runs over, the one named last changes fastest.
Arguments:
- frames: bfloat16 [64, 16, 24, 4096], P(None, 'tm', None, 'lon'), may hold values from -6 to 6
- cotangent: bfloat16 [64, 16, 24, 4096], P(None, 'tm', None, 'lon'), may hold values from -6 to 6
- w_space: bfloat16 [3, 3, 64, 64], replicated, may hold values from -0.25 to 0.25
- w_time: bfloat16 [3, 64, 64], replicated, may hold values from -0.4375 to 0.4375
Outputs:
- grad_frames: bfloat16 [64, 16, 24, 4096], P(None, 'tm', None, 'lon')
- grad_space: float32 [3, 3, 64, 64], replicated
- grad_time: float32 [3, 64, 64], replicated
All inputs are finite; a program needn't handle non-finite values.
Results may differ from a plain program's by a relative error of at most 0.0049.
Values may be sent and summed in bfloat16 or wider, within the bound.
No kernel may reach another device: no remote copies, remote signals or barrier semaphores. Data moves between devices by JAX's collectives and lax.ppermute only.
A program may use at most 64 MiB of HBM per device.

v0:
```python
import math

import jax
import jax.numpy as jnp
from jax import lax
from jax.sharding import PartitionSpec as P


def padded_2(cells, sides, width):
    for axis, dim in sides:
        count = lax.axis_size(axis)
        head = lax.slice_in_dim(cells, 0, width, axis=dim)
        tail = lax.slice_in_dim(cells, cells.shape[dim] - width, cells.shape[dim], axis=dim)
        cells = jnp.concatenate(
            [
                lax.ppermute(tail, axis, [(i, (i + 1) % count) for i in range(count)]),
                cells,
                lax.ppermute(head, axis, [((i + 1) % count, i) for i in range(count)]),
            ],
            axis=dim,
        )
    return cells


def from_behind(value, axis, steps):
    count = lax.axis_size(axis)
    first, last = (max(0, -steps), min(count, count - steps))
    return lax.ppermute(value, axis, [(source, source + steps) for source in range(first, last)])


def silu_slope(pre):
    sigmoid_value = jax.nn.sigmoid(pre)
    return sigmoid_value * (1.0 + pre * (1.0 - sigmoid_value))


def pad_rows(field):
    return jnp.pad(field, ((0, 0), (0, 0), (1, 1), (0, 0)))


def body(frames, cotangent, w_space, w_time):
    channels, frame_count, lat_rows, lon_cols = frames.shape
    contract_last = (((1,), (1,)), ((), ()))
    contract_first = (((0,), (0,)), ((), ()))
    padded = pad_rows(padded_2(frames, (("lon", 3),), 1))
    later_frames = from_behind(cotangent, "tm", -1)
    later_ext = jnp.concatenate([cotangent, later_frames], axis=1)
    pre = None
    for i in range(3):
        for j in range(3):
            window = padded[:, :, i : i + lat_rows, j : j + lon_cols].reshape(channels, -1)
            term = jnp.dot(w_space[i, j], window, preferred_element_type=jnp.float32)
            pre = term if pre is None else pre + term
    act = jax.nn.silu(pre).astype(jnp.bfloat16)
    upstream = None
    for k in range(3):
        later_k = later_ext[:, k : k + frame_count].reshape(channels, -1)
        term = lax.dot_general(
            w_time[k], later_k, contract_first, preferred_element_type=jnp.float32
        )
        upstream = term if upstream is None else upstream + term
    tm_terms = []
    act_grid = act.reshape(channels, frame_count, lat_rows, lon_cols)
    earlier = from_behind(act_grid, "tm", 1)
    act_ext = jnp.concatenate([earlier, act_grid], axis=1)
    cot_flat = cotangent.reshape(channels, -1)
    for k in range(3):
        window = act_ext[:, 2 - k : 2 - k + frame_count].reshape(channels, -1)
        tm_terms.append(
            lax.dot_general(cot_flat, window, contract_last, preferred_element_type=jnp.float32)
        )
    grad_tm = jnp.stack(tm_terms)
    dpre = (upstream * silu_slope(pre)).astype(jnp.bfloat16)
    dpre_grid = dpre.reshape(channels, frame_count, lat_rows, lon_cols)
    dpad = pad_rows(padded_2(dpre_grid, (("lon", 3),), 1))
    sp_terms = []
    for i in range(3):
        for j in range(3):
            window = padded[:, :, i : i + lat_rows, j : j + lon_cols].reshape(channels, -1)
            sp_terms.append(
                lax.dot_general(dpre, window, contract_last, preferred_element_type=jnp.float32)
            )
    grad_sp = jnp.stack(sp_terms).reshape(3, 3, channels, channels)
    back = None
    for i in range(3):
        for j in range(3):
            window = dpad[:, :, 2 - i : 2 - i + lat_rows, 2 - j : 2 - j + lon_cols].reshape(
                channels, -1
            )
            term = lax.dot_general(
                w_space[i, j], window, contract_first, preferred_element_type=jnp.float32
            )
            back = term if back is None else back + term
    grad_frames = back.astype(jnp.bfloat16).reshape(channels, frame_count, lat_rows, lon_cols)
    grad_sp, grad_tm = lax.psum((grad_sp, grad_tm), ("tm", "lon"))
    total_cells = frame_count * lax.axis_size("tm") * lat_rows * lon_cols * lax.axis_size("lon")
    scale = 1.0 / math.sqrt(total_cells)
    return (grad_frames, grad_sp * scale, grad_tm * scale)


def solution(mesh):
    return jax.shard_map(
        body,
        mesh=mesh,
        in_specs=(P(None, "tm", None, "lon"), P(None, "tm", None, "lon"), P(), P()),
        out_specs=(P(None, "tm", None, "lon"), P(), P()),
        check_vma=False,
    )
```

profile of v0, /device:TPU:1, one launch (start us, length us, event | category | flops | bytes accessed | tf_op | source)
XLA Modules:
  0.0 309.6 jit_solution(8349422694415326540)
XLA Ops:
  7.2 1.7 fusion.141
  9.0 0.7 copy.31
  9.7 3.1 collective-permute-start.1
  12.7 0.7 copy.32
  13.7 1.5 collective-permute-start
  15.2 0.7 copy.14
  15.9 0.7 collective-permute-done.2
  16.6 0.7 copy.15
  17.3 1.9 fusion.13
  19.1 0.9 pad_maximum_fusion.3
  20.0 1.8 fusion.139
  21.8 0.4 fusion.65
  22.1 0.4 convolution_bitcast_fusion
  22.9 0.4 convolution_bitcast_fusion.2
  23.2 0.4 convolution_add_fusion.2
  23.6 0.4 convolution_add_fusion.1
  23.9 0.4 fusion
  24.7 0.8 multiply_convert_fusion
  25.6 1.1 copy.24
  26.7 5.7 %collective-permute-start.5 = (bf16[64,2,24,128]{3,0,2,1:T(8,128)(2,1)}, bf16[64,2,24,128]{3,0,2,1:T(8,128)(2,1)}, u32[]{:S(2)}, u32[]{:S(2)}) collective-permute-start(bf16[64,2,24,128]{3,0,2,1:T(8,128)(2,1)} %copy.24), channel_id=1, source_target_pairs={{0,32},{32,64},{64,96},{96,128},{128,160},{160,192},{192,224},{1,3... | collective-permute-start | bytes 2359304 | tf_op jit(solution)/shard_map/ppermute | solution.py:28
  32.4 0.4 convolution_bitcast_fusion.6
  32.8 1.1 pad_maximum_fusion.4
  33.9 0.4 convolution_bitcast_fusion.4
  34.3 0.4 convolution_add_fusion.13
  34.7 1.9 fusion.7
  36.6 0.4 fusion.27
  37.0 0.4 fusion.26
  37.3 0.4 fusion.25
  37.7 0.4 fusion.24
  38.1 0.4 fusion.23
  38.5 0.4 fusion.22
  38.8 0.4 fusion.21
  39.6 0.4 fusion.20
  40.0 0.7 copy-done.10
  40.7 0.7 copy.33
  41.4 5.8 %collective-permute-start.3 = (bf16[64,2,24,1]{0,2,3,1:T(8,128)(2,1)S(1)}, bf16[64,2,24,1]{0,2,3,1:T(8,128)(2,1)S(1)}, u32[]{:S(2)}, u32[]{:S(2)}) collective-permute-start(bf16[64,2,24,1]{0,2,3,1:T(8,128)(2,1)S(1)} %copy.33), channel_id=1, source_target_pairs={{0,1},{1,2},{2,3},{3,4},{4,5},{5,6},{6,7},{7,8},{8,9},{9,10},{10,1... | collective-permute-start | bytes 18440 | tf_op jit(solution)/shard_map/ppermute | solution.py:16
  47.2 0.7 copy.34
  47.9 2.1 fusion.19
  50.1 0.7 copy.20
  50.8 0.6 collective-permute-done.4
  51.3 0.7 copy.21
  52.0 0.9 copy-done.2
  52.9 2.0 pad_maximum_fusion
  54.9 3.3 %select_maximum_fusion = bf16[64,2,26,130]{3,2,1,0:T(8,128)(2,1)S(1)} fusion(bf16[64,2,24,1]{3,2,1,0:T(8,128)(2,1)} %copy-done.2, bf16[64,2,24,128]{3,2,1,0:T(8,128)(2,1)S(1)} %bitcast.272, bf16[64,2,24,1]{3,2,1,0:T(8,128)(2,1)} %copy-done.1), kind=kLoop, calls=%fused_computation.30 | loop fusion | flops 5191680 | bytes 1664000 | tf_op jit(solution)/shard_map/concatenate | solution.py:14
  58.3 1.5 fusion.28
  59.7 1.5 convolution_bitcast_fusion.5
  61.3 82.8 %psum.15 = f32[3,64,64]{1,2,0:T(8,128)S(1)} all-reduce(f32[3,64,64]{1,2,0:T(8,128)S(1)} %pad_maximum_fusion.5), channel_id=1, replica_groups=mesh['tm'=8,'lon'=32] {'tm','lon'}, use_global_device_ids=true, to_apply=%region_1.2 | all-reduce | flops 12288 | bytes 98304 | tf_op jit(solution)/shard_map/psum | solution.py:94
  144.1 1.8 fusion.138
  145.8 0.4 fusion.45
  146.2 0.4 convolution_add_fusion.10
  146.7 0.4 convolution_add_fusion.9
  147.1 0.7 copy-done.8
  147.8 0.4 convolution_add_fusion.8
  148.2 0.7 copy-done.4
  148.9 0.4 convolution_add_fusion.7
  149.4 0.7 copy-done.7
  150.1 0.4 convolution_add_fusion.6
  150.5 0.4 convolution_add_fusion.5
  150.9 0.4 convolution_add_fusion.4
  151.3 0.4 fusion.18
  151.8 0.7 copy.28
  152.5 1.0 copy.56
  153.5 147.6 %all-reduce.4.cloned.1.call-done = f32[3,3,64,64]{3,2,1,0:T(8,128)} async-done(((f32[3,3,64,64]{3,2,1,0:T(8,128)}), f32[3,3,64,64]{3,2,1,0:T(8,128)}) %all-reduce.4.cloned.1.call-update) | async-done | bytes 147472 | tf_op jit(solution)/shard_map/psum | solution.py:94
  301.1 1.7 broadcast_multiply_fusion
  (34 shorter events, 1.7 us)
Async XLA Ops:
  7.2 293.9 %all-reduce.4.cloned.1.call-start = ((), (), s32[]{:S(2)}) async-start(), calls=%async_computation | async-start | bytes 589824 | tf_op jit(solution)/shard_map/psum | solution.py:94
  8.9 4.8 %copy-start.5 = (bf16[64,2,24,128]{3,2,1,0:T(8,128)(2,1)S(1)}, bf16[64,2,24,128]{3,2,1,0:T(8,128)(2,1)}, u32[]{:S(2)}) copy-start(bf16[64,2,24,128]{3,2,1,0:T(8,128)(2,1)} %param.5) | copy-start | bytes 2359300
  9.0 8.3 %copy-start = (bf16[64,2,24,128]{3,2,1,0:T(8,128)(2,1)S(1)}, bf16[64,2,24,128]{3,2,1,0:T(8,128)(2,1)}, u32[]{:S(2)}) copy-start(bf16[64,2,24,128]{3,2,1,0:T(8,128)(2,1)} %param.4) | copy-start | bytes 2359300
  9.7 5.5 %collective-permute-start.1 = (bf16[64,2,24,1]{0,2,3,1:T(8,128)(2,1)S(1)}, bf16[64,2,24,1]{0,2,3,1:T(8,128)(2,1)S(1)}, u32[]{:S(2)}, u32[]{:S(2)}) collective-permute-start(bf16[64,2,24,1]{0,2,3,1:T(8,128)(2,1)S(1)} %copy.31), channel_id=1, source_target_pairs={{0,1},{1,2},{2,3},{3,4},{4,5},{5,6},{6,7},{7,8},{8,9},{9,10},{10,1... | collective-permute-start | bytes 18440 | tf_op jit(solution)/shard_map/ppermute | solution.py:16
  13.4 3.2 %collective-permute-start.2 = (bf16[64,2,24,1]{0,2,3,1:T(8,128)(2,1)S(1)}, bf16[64,2,24,1]{0,2,3,1:T(8,128)(2,1)S(1)}, u32[]{:S(2)}, u32[]{:S(2)}) collective-permute-start(bf16[64,2,24,1]{0,2,3,1:T(8,128)(2,1)S(1)} %copy.32), channel_id=1, source_target_pairs={{1,0},{2,1},{3,2},{4,3},{5,4},{6,5},{7,6},{8,7},{9,8},{10,9},{11,1... | collective-permute-start | bytes 18440 | tf_op jit(solution)/shard_map/ppermute | solution.py:18
  13.7 19.1 %collective-permute-start = (bf16[64,2,24,128]{3,2,1,0:T(8,128)(2,1)S(1)}, bf16[64,2,24,128]{3,2,1,0:T(8,128)(2,1)}, u32[]{:S(2)}, u32[]{:S(2)}) collective-permute-start(bf16[64,2,24,128]{3,2,1,0:T(8,128)(2,1)S(1)} %copy-done.5), channel_id=1, source_target_pairs={{32,0},{64,32},{96,64},{128,96},{160,128},{192,160},{224,192},{33,... | collective-permute-start | bytes 2359304 | tf_op jit(solution)/shard_map/ppermute | solution.py:28
  20.0 1.8 copy-start.9
  26.7 31.5 %collective-permute-start.5 = (bf16[64,2,24,128]{3,0,2,1:T(8,128)(2,1)}, bf16[64,2,24,128]{3,0,2,1:T(8,128)(2,1)}, u32[]{:S(2)}, u32[]{:S(2)}) collective-permute-start(bf16[64,2,24,128]{3,0,2,1:T(8,128)(2,1)} %copy.24), channel_id=1, source_target_pairs={{0,32},{32,64},{64,96},{96,128},{128,160},{160,192},{192,224},{1,3... | collective-permute-start | bytes 2359304 | tf_op jit(solution)/shard_map/ppermute | solution.py:28
  32.7 1.1 copy-start.11
  36.6 3.0 copy-start.3
  40.0 0.7 copy-start.10
  41.4 8.7 %collective-permute-start.3 = (bf16[64,2,24,1]{0,2,3,1:T(8,128)(2,1)S(1)}, bf16[64,2,24,1]{0,2,3,1:T(8,128)(2,1)S(1)}, u32[]{:S(2)}, u32[]{:S(2)}) collective-permute-start(bf16[64,2,24,1]{0,2,3,1:T(8,128)(2,1)S(1)} %copy.33), channel_id=1, source_target_pairs={{0,1},{1,2},{2,3},{3,4},{4,5},{5,6},{6,7},{7,8},{8,9},{9,10},{10,1... | collective-permute-start | bytes 18440 | tf_op jit(solution)/shard_map/ppermute | solution.py:16
  47.9 3.5 %collective-permute-start.4 = (bf16[64,2,24,1]{0,2,3,1:T(8,128)(2,1)S(1)}, bf16[64,2,24,1]{0,2,3,1:T(8,128)(2,1)S(1)}, u32[]{:S(2)}, u32[]{:S(2)}) collective-permute-start(bf16[64,2,24,1]{0,2,3,1:T(8,128)(2,1)S(1)} %copy.34), channel_id=1, source_target_pairs={{1,0},{2,1},{3,2},{4,3},{5,4},{6,5},{7,6},{8,7},{9,8},{10,9},{11,1... | collective-permute-start | bytes 18440 | tf_op jit(solution)/shard_map/ppermute | solution.py:18
  50.8 1.3 copy-start.1
  52.0 0.9 copy-start.2
  54.9 3.3 %copy-start.6 = (bf16[64,2,24,128]{3,2,1,0:T(8,128)(2,1)S(1)}, bf16[64,2,24,128]{3,2,1,0:T(8,128)(2,1)}, u32[]{:S(2)}) copy-start(bf16[64,2,24,128]{3,2,1,0:T(8,128)(2,1)} %param.5) | copy-start | bytes 2359300
  146.7 1.1 copy-start.8
  147.8 1.1 copy-start.4
  148.9 1.1 copy-start.7
Sparse Core Ops, SparseCore 0:
  50.2 250.8 all-reduce.3
where the time goes:
time: 310 us
  waiting for transfers between devices  149 us (48%)
  blocking collectives  82.8 us (27%)
  matrix products  18.4 us (6%)
  local copies, waits for them, and re-layouts  17.8 us (6%)
  starting transfers between devices  16.4 us (5%)
  between operations  14.5 us (5%)
  other arithmetic  10.8 us (3%)
    psum x1, waiting for transfers between devices, body(): grad_sp, grad_tm = lax.psum((grad_sp, grad_tm), ('tm', 'lon'))  148 us
    psum x1, blocking collectives, body(): grad_sp, grad_tm = lax.psum((grad_sp, grad_tm), ('tm', 'lon'))  82.8 us
    ppermute x2, starting transfers between devices, padded_2(): lax.ppermute(tail, axis, [(i, (i + 1) % count) for i in range(count)])  8.86 us
    unnamed x32, local copies, waits for them, and re-layouts  8.46 us
    concatenate x4, other arithmetic, padded_2(): jnp.concatenate([lax.ppermute(tail, axis, [(i, (i + 1) % count) for i in...  8.03 us
    ppermute x2, starting transfers between devices, from_behind(): lax.ppermute(value, axis, [(source, source + steps) for source in range(f...  7.12 us
  transfers between devices with their start and end apart: 7, of which 3 were waited for; matrix products, arithmetic and copies ran while one was open for 13% of the time, Pallas kernels for 0%

commit v1 on v0

v1 whole, which is shorter than its diff:
```python
import math

import jax
import jax.numpy as jnp
import numpy as np
from jax import lax
from jax.experimental import pallas as pl
from jax.experimental.pallas import tpu as pltpu
from jax.sharding import Mesh
from jax.sharding import PartitionSpec as P

AXES = ("y", "xh", "xl", "z", "c")
TM = ("y", "xh")
LON = ("xl", "z", "c")
PLANE = ("y", "xh", "xl")
LINE = ("z", "c")
F32 = jnp.float32
BF16 = jnp.bfloat16
ROWS = 8
VMEM_LIMIT = 48 * 1024 * 1024


def dot_nt(a, b):
    return lax.dot_general(a, b, (((1,), (1,)), ((), ())), preferred_element_type=F32)


def lane_taps(slab, left, right, at):
    width = slab.shape[1]
    lane = lax.broadcasted_iota(jnp.int32, slab.shape, 1)
    wide = slab.astype(F32)
    before = jnp.where(lane == 0, pltpu.roll(left, lax.rem(width - at, width), 1), pltpu.roll(wide, 1, 1))
    after = jnp.where(lane == width - 1, pltpu.roll(right, width - 1 - at, 1), pltpu.roll(wide, width - 1, 1))
    return before.astype(BF16), slab, after.astype(BF16)


def forward_kernel(x_ref, left_ref, right_ref, w_ref, x3_ref, act_ref, slope_ref, y_ref):
    frames, rows, chans, cols = x_ref.shape
    left = left_ref[...].astype(F32)
    right = right_ref[...].astype(F32)
    weight = w_ref[...]
    zero = jnp.zeros((3 * chans, cols), F32)
    y_ref[0] = zero
    y_ref[rows + 1] = zero
    for f in range(frames):

        @pl.loop(0, rows // ROWS)
        def _(g):
            wide = []
            for r in range(ROWS):
                h = g * ROWS + r
                x3 = jnp.concatenate(lane_taps(x_ref[f, h], left, right, f * rows + h), axis=0)
                x3_ref[f, h] = x3
                wide.append(x3)
            y = jnp.dot(weight, jnp.concatenate(wide, axis=1), preferred_element_type=F32)
            for r in range(ROWS):
                y_ref[g * ROWS + r + 1] = y[:, r * cols : (r + 1) * cols]

        @pl.loop(0, rows // ROWS)
        def _(g):
            for r in range(ROWS):
                h = g * ROWS + r
                pre = (
                    y_ref[h, 0:chans]
                    + y_ref[h + 1, chans : 2 * chans]
                    + y_ref[h + 2, 2 * chans : 3 * chans]
                )
                s = 1.0 / (1.0 + jnp.exp(-pre))
                act_ref[f, h] = (pre * s).astype(BF16)
                slope_ref[f, h] = s * (1.0 + pre * (1.0 - s))


def grads_kernel(c0_ref, c1_ref, c2_ref, act_ref, slope_ref, x3_ref, w_ref, base_ref,
                 d_ref, first_ref, last_ref, sum_ref, d_scr):
    rows, chans, cols = d_ref.shape
    weight = w_ref[...]
    lane = lax.broadcasted_iota(jnp.int32, (chans, cols), 1)
    d_scr[0] = jnp.zeros((chans, cols), BF16)
    d_scr[rows + 1] = jnp.zeros((chans, cols), BF16)
    first = jnp.zeros((chans, cols), F32)
    last = jnp.zeros((chans, cols), F32)
    t_sum = jnp.zeros((3 * chans, chans), F32)
    for g in range(rows // ROWS):
        hs = range(g * ROWS, (g + 1) * ROWS)
        cot = jnp.concatenate(
            [jnp.concatenate([ref[h] for h in hs], axis=1) for ref in (c0_ref, c1_ref, c2_ref)], axis=0
        )
        up = jnp.dot(weight, cot, preferred_element_type=F32)
        for r, h in enumerate(hs):
            d = (up[:, r * cols : (r + 1) * cols] * slope_ref[h]).astype(BF16)
            d_ref[h] = d
            d_scr[h + 1] = d
            wide = d.astype(F32)
            first = jnp.where(lane == h, pltpu.roll(wide, h, 1), first)
            last = jnp.where(lane == h, pltpu.roll(wide, (h + 1) % cols, 1), last)
        act = jnp.concatenate([act_ref[h] for h in hs], axis=1)
        t_sum = t_sum + dot_nt(cot, act)
    first_ref[...] = first.astype(BF16)
    last_ref[...] = last.astype(BF16)
    g_sum = jnp.zeros((3 * chans, 3 * chans), F32)
    for g in range(rows // ROWS):
        hs = range(g * ROWS, (g + 1) * ROWS)
        d3 = jnp.concatenate(
            [jnp.concatenate([d_scr[h - i + 2] for h in hs], axis=1) for i in range(3)], axis=0
        )
        x3 = jnp.concatenate([x3_ref[h] for h in hs], axis=1)
        g_sum = g_sum + dot_nt(d3, x3)
    both = jnp.concatenate([g_sum, t_sum], axis=1)
    half = both.shape[1] // 2
    sum_ref[0] = base_ref[0] + both[:, :half]
    sum_ref[1] = base_ref[1] + both[:, half:]


def back_kernel(d_ref, left_ref, right_ref, w_ref, out_ref, z_ref):
    rows, chans, cols = d_ref.shape
    left = left_ref[...].astype(F32)
    right = right_ref[...].astype(F32)
    weight = w_ref[...]
    zero = jnp.zeros((3 * chans, cols), F32)
    z_ref[0] = zero
    z_ref[rows + 1] = zero

    @pl.loop(0, rows // ROWS)
    def _(g):
        wide = []
        for r in range(ROWS):
            h = g * ROWS + r
            before, same, after = lane_taps(d_ref[h], left, right, h)
            wide.append(jnp.concatenate([after, same, before], axis=0))
        z = jnp.dot(weight, jnp.concatenate(wide, axis=1), preferred_element_type=F32)
        for r in range(ROWS):
            z_ref[g * ROWS + r + 1] = z[:, r * cols : (r + 1) * cols]

    @pl.loop(0, rows // ROWS)
    def _(g):
        for r in range(ROWS):
            h = g * ROWS + r
            out = (
                z_ref[h + 2, 0:chans]
                + z_ref[h + 1, chans : 2 * chans]
                + z_ref[h, 2 * chans : 3 * chans]
            )
            out_ref[h] = out.astype(BF16)


def in_vmem(count):
    return [pl.BlockSpec(memory_space=pltpu.VMEM)] * count


def call(kernel, args, outs, scratch, flops):
    return pl.pallas_call(
        kernel,
        out_shape=outs,
        in_specs=in_vmem(len(args)),
        out_specs=tuple(in_vmem(len(outs))),
        scratch_shapes=scratch,
        compiler_params=pltpu.CompilerParams(vmem_limit_bytes=VMEM_LIMIT),
        cost_estimate=pl.CostEstimate(flops=flops, transcendentals=0, bytes_accessed=4_000_000),
    )(*args)


def exchange(cells, axes):
    return lax.all_to_all(cells, axes, 0, 0, tiled=True)


def spread(cells, axes):
    count = lax.axis_size(axes)
    return exchange(jnp.broadcast_to(cells[None], (count,) + cells.shape), axes)


def sum_over_all(cells):
    count = lax.axis_size(PLANE)
    parts = exchange(cells.reshape(count, -1, cells.shape[-1]), PLANE).sum(0)
    parts = spread(parts, LINE).sum(0)
    return spread(parts, PLANE).reshape(cells.shape)


def edge_swap(first, last):
    count = lax.axis_size(LON)
    left = lax.ppermute(last, LON, [(i, (i + 1) % count) for i in range(count)])
    right = lax.ppermute(first, LON, [((i + 1) % count, i) for i in range(count)])
    return left, right


def body(frames, cotangent, w_space, w_time):
    chans, nf, rows, cols = frames.shape
    shape = jax.ShapeDtypeStruct
    steps = lax.axis_size(TM)
    slabs = (rows, chans, cols)
    cot = [jnp.transpose(cotangent[:, f], (1, 0, 2)) for f in range(nf)]
    cot += [lax.ppermute(c, TM, [(i, i - 1) for i in range(1, steps)]) for c in cot]

    edge = lambda w: jnp.pad(frames[:, :, :, w].reshape(chans, nf * rows), ((0, 0), (0, cols - nf * rows)))
    left, right = edge_swap(edge(0), edge(cols - 1))
    field = jnp.transpose(frames, (1, 2, 0, 3))
    w_fwd = jnp.transpose(w_space, (0, 2, 1, 3)).reshape(3 * chans, 3 * chans)
    w_bwd = jnp.transpose(w_space, (0, 3, 1, 2)).reshape(3 * chans, 3 * chans)
    w_up = jnp.transpose(w_time, (2, 0, 1)).reshape(chans, 3 * chans)
    x3, act, slope = call(
        forward_kernel,
        (field, left, right, w_fwd),
        (
            shape((nf, rows, 3 * chans, cols), BF16),
            shape((nf,) + slabs, BF16),
            shape((nf,) + slabs, F32),
        ),
        [pltpu.VMEM((rows + 2, 3 * chans, cols), F32)],
        4_000_000_000,
    )
    total = jnp.zeros((2, 3 * chans, 2 * chans), F32)
    pieces = []
    for f in range(nf):
        dpre, first, last, total = call(
            grads_kernel,
            (cot[f], cot[f + 1], cot[f + 2], act[f], slope[f], x3[f], w_up, total),
            (
                shape(slabs, BF16),
                shape((chans, cols), BF16),
                shape((chans, cols), BF16),
                shape((2, 3 * chans, 2 * chans), F32),
            ),
            [pltpu.VMEM((rows + 2, chans, cols), BF16)],
            4_000_000_000,
        )
        d_left, d_right = edge_swap(first, last)
        (out,) = call(
            back_kernel,
            (dpre, d_left, d_right, w_bwd),
            (shape(slabs, BF16),),
            [pltpu.VMEM((rows + 2, 3 * chans, cols), F32)],
            2_000_000_000,
        )
        pieces.append(jnp.transpose(out, (1, 0, 2)))
    grad_frames = jnp.stack(pieces, axis=1)
    total = sum_over_all(total.reshape(-1, 2 * chans)).reshape(2, 3 * chans, 2 * chans)
    cells = nf * steps * rows * cols * lax.axis_size(LON)
    both = jnp.concatenate([total[0], total[1]], axis=1) * (1.0 / math.sqrt(cells))
    grad_sp = jnp.transpose(both[:, : 3 * chans].reshape(3, chans, 3, chans), (0, 2, 1, 3))
    grad_tm = both[:, 3 * chans :].reshape(3, chans, chans)
    return grad_frames, grad_sp, grad_tm


def solution(mesh):
    fine = Mesh(np.asarray(mesh.devices).reshape(4, 2, 2, 8, 2), AXES)
    field = P(None, TM, None, LON)
    return jax.shard_map(
        body,
        mesh=fine,
        in_specs=(field, field, P(), P()),
        out_specs=(field, P(), P()),
        check_vma=False,
    )
```

time: 310 us -> 81.7 us (0.26)
  waiting for transfers between devices: 149 us -> 19.7 us
  blocking collectives: 82.8 us -> 14.6 us
  matrix products: 18.4 us -> 0 us
  between operations: 14.5 us -> 0.92 us
  starting transfers between devices: 16.4 us -> 28.1 us
  other arithmetic: 10.8 us -> 0.14 us
  Pallas kernels: 0 us -> 8.5 us
  local copies, waits for them, and re-layouts: 17.8 us -> 9.3 us
    psum x1 -> x0, waiting for transfers between devices: 148 us -> none  [body(): grad_sp, grad_tm = lax.psum((grad_sp, grad_tm), ('tm', 'lon'))]
    psum x1 -> x0, blocking collectives: 82.8 us -> none  [body(): grad_sp, grad_tm = lax.psum((grad_sp, grad_tm), ('tm', 'lon'))]
    dot_general x33 -> x0, matrix products: 18.4 us -> none  [the longest x9 5 us: body(): lax.dot_general(dpre, window, contract_last, preferred_element_type=jnp.f...]
    all_to_all x0 -> x2, starting transfers between devices: none -> 17.9 us  [exchange(): return lax.all_to_all(cells, axes, 0, 0, tiled=True)]
    all_to_all x0 -> x1, blocking collectives: none -> 14.6 us  [exchange(): return lax.all_to_all(cells, axes, 0, 0, tiled=True)]
    ppermute x6 -> x8, waiting for transfers between devices: 1.3 us -> 12.2 us  [the longest x2 9.55 us: body(): lax.ppermute(c, TM, [(i, i - 1) for i in range(1, steps)])]
    concatenate x5 -> x0, other arithmetic: 9.11 us -> none  [the longest x4 8.03 us: padded_2(): jnp.concatenate([lax.ppermute(tail, axis, [(i, (i + 1) % count) for i in...]
    pallas_call x0 -> x5, Pallas kernels: none -> 8.5 us  [call(): pl.pallas_call(kernel, out_shape=outs, in_specs=in_vmem(len(args)), out_s...]
  transfers between devices with their start and end apart: 7 -> 10, of which waited for: 3 -> 5; matrix products, arithmetic and copies ran while one was open for 13% -> 6% of each run, Pallas kernels for 0% -> 9%
where the time goes in v1:
time: 81.7 us; the launch traced here: 81.2 us
  starting transfers between devices  28.1 us (34%)
  waiting for transfers between devices  19.7 us (24%)
  blocking collectives  14.6 us (18%)
  local copies, waits for them, and re-layouts  9.3 us (11%)
  Pallas kernels  8.5 us (10%)
  between operations  0.92 us (1%)
    all_to_all x2, starting transfers between devices, exchange(): return lax.all_to_all(cells, axes, 0, 0, tiled=True)  17.9 us
    all_to_all x1, blocking collectives, exchange(): return lax.all_to_all(cells, axes, 0, 0, tiled=True)  14.6 us
    ppermute x2, waiting for transfers between devices, body(): lax.ppermute(c, TM, [(i, i - 1) for i in range(1, steps)])  9.55 us
    pallas_call x5, Pallas kernels, call(): pl.pallas_call(kernel, out_shape=outs, in_specs=in_vmem(len(args)), out_s...  8.5 us
    all_to_all x2, waiting for transfers between devices, exchange(): return lax.all_to_all(cells, axes, 0, 0, tiled=True)  7.44 us
    ppermute x3, starting transfers between devices, edge_swap(): left = lax.ppermute(last, LON, [(i, (i + 1) % count) for i in range(count)])  6.55 us
    unnamed x15, local copies, waits for them, and re-layouts  3.88 us
    ppermute x3, waiting for transfers between devices, edge_swap(): lax.ppermute(first, LON, [((i + 1) % count, i) for i in range(count)])  2.69 us
  transfers between devices with their start and end apart: 10, of which 5 were waited for; matrix products, arithmetic and copies ran while one was open for 6% of the time, Pallas kernels for 9%

profile of v1, /device:TPU:1, one launch (start us, length us, event | category | flops | bytes accessed | tf_op | source)
XLA Modules:
  0.0 81.2 jit_solution(5471723475306548781)
XLA Ops:
  0.6 1.7 %fusion = (bf16[64,2,24,1]{3,2,1,0:T(8,128)(2,1)S(1)}, bf16[64,2,24,1]{3,2,1,0:T(8,128)(2,1)S(1)}) fusion(bf16[64,2,24,128]{3,2,1,0:T(8,128)(2,1)} %param.4), kind=kLoop, calls=%fused_computation.11 | loop fusion | bytes 24576 | tf_op jit(solution)/shard_map/slice | solution.py:192
  2.4 0.0 copy-start.1
  2.4 0.7 copy.42
  3.1 0.1 copy.31
  3.2 3.1 %collective-permute-start.1 = (bf16[64,128]{1,0:T(8,128)(2,1)S(1)}, bf16[64,128]{1,0:T(8,128)(2,1)S(1)}, u32[]{:S(2)}, u32[]{:S(2)}) collective-permute-start(bf16[64,128]{1,0:T(8,128)(2,1)S(1)} %pad.7), channel_id=1, source_target_pairs={{0,1},{1,2},{2,3},{3,4},{4,5},{5,6},{6,7},{7,8},{8,9},{9,10},{10,1... | collective-permute-start | bytes 49160 | tf_op jit(solution)/shard_map/ppermute | solution.py:179
  6.3 0.7 copy.43
  7.0 0.1 copy.33
  7.1 0.0 copy-start
  7.1 0.3 collective-permute-start.2
  7.4 0.0 copy-done.1
  7.4 0.1 fusion.1
  7.5 0.0 copy-start.2
  7.5 0.1 copy.49
  7.6 0.0 copy-start.3
  7.6 1.3 %collective-permute-start = (bf16[24,64,128]{2,1,0:T(8,128)(2,1)S(1)}, bf16[24,64,128]{2,1,0:T(8,128)(2,1)S(1)}, u32[]{:S(2)}, u32[]{:S(2)}) collective-permute-start(bf16[24,64,128]{2,1,0:T(8,128)(2,1)S(1)} %bitcast.48), channel_id=1, source_target_pairs={{32,0},{64,32},{96,64},{128,96},{160,128},{192,160},{224,192},{33,... | collective-permute-start | bytes 1179656 | tf_op jit(solution)/shard_map/ppermute | solution.py:190
  8.9 0.1 copy.48
  9.0 1.3 %collective-permute-start.5 = (bf16[24,64,128]{2,1,0:T(8,128)(2,1)S(1)}, bf16[24,64,128]{2,1,0:T(8,128)(2,1)S(1)}, u32[]{:S(2)}, u32[]{:S(2)}) collective-permute-start(bf16[24,64,128]{2,1,0:T(8,128)(2,1)S(1)} %bitcast.45), channel_id=1, source_target_pairs={{32,0},{64,32},{96,64},{128,96},{160,128},{192,160},{224,192},{33,... | collective-permute-start | bytes 1179656 | tf_op jit(solution)/shard_map/ppermute | solution.py:190
  10.3 0.0 copy-done
  10.3 0.2 copy.47
  10.5 0.0 copy-done.2
  10.5 0.1 copy.34
  10.7 0.2 reshape.27.w_ref
  10.8 0.0 copy-done.3
  10.8 0.1 copy.35.w_ref
  10.9 0.0 collective-permute-done.1.left_ref
  10.9 0.0 collective-permute-done.2.right_ref
  11.0 3.2 %shard_map.67 = (bf16[2,24,192,128]{3,2,1,0:T(8,128)(2,1)S(1)}, bf16[2,24,64,128]{3,2,1,0:T(8,128)(2,1)S(1)}, f32[2,24,64,128]{3,2,1,0:T(8,128)S(1)}) custom-call(bf16[2,24,64,128]{3,2,1,0:T(8,128)(2,1)S(1)} %bitcast.44, bf16[64,128]{1,0:T(8,128)(2,1)S(1)} %collective-permute-done.1.left_ref, bf16[64,128]{1,0:T(8,128)(2,1)S(1)} %collective-permute-done.2.right_ref, ...), custom_call_target="tpu_custom_call" | custom-call | flops 4000000000 | bytes 4000000 | tf_op jit(solution)/shard_map/pallas_call | solution.py:150
  14.2 0.2 slice_bitcast_fusion.1
  14.3 0.2 slice_bitcast_fusion.3
  14.5 0.1 slice_bitcast_fusion.5
  14.5 3.1 %collective-permute-done.c2_ref.c1_ref = bf16[24,64,128]{2,1,0:T(8,128)(2,1)S(1)} collective-permute-done((bf16[24,64,128]{2,1,0:T(8,128)(2,1)S(1)}, bf16[24,64,128]{2,1,0:T(8,128)(2,1)S(1)}, u32[]{:S(2)}, u32[]{:S(2)}) %collective-permute-start) | collective-permute-done | bytes 393248 | tf_op jit(solution)/shard_map/ppermute | solution.py:190
  17.7 1.3 %shard_map.68 = (bf16[24,64,128]{2,1,0:T(8,128)(2,1)S(1)}, bf16[64,128]{1,0:T(8,128)(2,1)S(1)}, bf16[64,128]{1,0:T(8,128)(2,1)S(1)}, f32[2,192,128]{2,1,0:T(8,128)S(1)}) custom-call(bf16[24,64,128]{2,1,0:T(8,128)(2,1)S(1)} %bitcast.49, bf16[24,64,128]{2,1,0:T(8,128)(2,1)S(1)} %bitcast.46, bf16[24,64,128]{2,1,0:T(8,128)(2,1)S(1)} %collective-permute-done.c2_ref.c1_ref, ...), custom_call_target="tpu_custom_call" | custom-call | flops 4000000000 | bytes 4000000 | tf_op jit(solution)/shard_map/pallas_call | solution.py:150
  19.0 6.5 %collective-permute-done.5.c2_ref = bf16[24,64,128]{2,1,0:T(8,128)(2,1)S(1)} collective-permute-done((bf16[24,64,128]{2,1,0:T(8,128)(2,1)S(1)}, bf16[24,64,128]{2,1,0:T(8,128)(2,1)S(1)}, u32[]{:S(2)}, u32[]{:S(2)}) %collective-permute-start.5) | collective-permute-done | bytes 393248 | tf_op jit(solution)/shard_map/ppermute | solution.py:190
  25.4 1.3 %shard_map.70 = (bf16[24,64,128]{2,1,0:T(8,128)(2,1)S(1)}, bf16[64,128]{1,0:T(8,128)(2,1)S(1)}, bf16[64,128]{1,0:T(8,128)(2,1)S(1)}, f32[2,192,128]{2,1,0:T(8,128)S(1)}) custom-call(bf16[24,64,128]{2,1,0:T(8,128)(2,1)S(1)} %bitcast.47, bf16[24,64,128]{2,1,0:T(8,128)(2,1)S(1)} %collective-permute-done.c2_ref.c1_ref, ...), custom_call_target="tpu_custom_call" | custom-call | flops 4000000000 | bytes 4000000 | tf_op jit(solution)/shard_map/pallas_call | solution.py:150
  26.7 14.6 %all_to_all.15 = f32[16,24,128]{2,1,0:T(8,128)S(1)} all-to-all(f32[16,24,128]{2,1,0:T(8,128)S(1)} %bitcast.52), channel_id=1, replica_groups=mesh['y'=4,'xh'=2,'xl'=2,'z'=8,'c'=2] {'y','xh','xl'}, dimensions={0} | all-to-all | bytes 393216 | tf_op jit(solution)/shard_map/all_to_all | solution.py:162
  41.4 0.7 broadcast_in_dim.7
  42.1 14.3 %all-to-all-start.1 = ((f32[16,24,128]{2,1,0:T(8,128)}), f32[16,24,128]{2,1,0:T(8,128)S(1)}, u32[]{:S(2)}, u32[]{:S(2)}) async-start(f32[16,24,128]{2,1,0:T(8,128)} %broadcast_in_dim.7), calls=%async_computation.1 | async-start | bytes 393216 | tf_op jit(solution)/shard_map/all_to_all | solution.py:162
  56.4 1.6 %collective-permute-start.6 = (bf16[64,128]{1,0:T(8,128)(2,1)S(1)}, bf16[64,128]{1,0:T(8,128)(2,1)S(1)}, u32[]{:S(2)}, u32[]{:S(2)}) collective-permute-start(bf16[64,128]{1,0:T(8,128)(2,1)S(1)} %get-tuple-element.22), channel_id=1, source_target_pairs={{0,1},{1,2},{2,3},{3,4},{4,5},{5,6},{6,7},{7,8},{8,9},{9,10},{10,1... | collective-permute-start | bytes 49160 | tf_op jit(solution)/shard_map/ppermute | solution.py:179
  58.1 0.0 collective-permute-start.7
  58.1 0.2 copy.36
  58.3 0.2 reshape.29.w_ref
  58.4 1.8 %collective-permute-start.3 = (bf16[64,128]{1,0:T(8,128)(2,1)S(1)}, bf16[64,128]{1,0:T(8,128)(2,1)S(1)}, u32[]{:S(2)}, u32[]{:S(2)}) collective-permute-start(bf16[64,128]{1,0:T(8,128)(2,1)S(1)} %get-tuple-element.18), channel_id=1, source_target_pairs={{0,1},{1,2},{2,3},{3,4},{4,5},{5,6},{6,7},{7,8},{8,9},{9,10},{10,1... | collective-permute-start | bytes 49160 | tf_op jit(solution)/shard_map/ppermute | solution.py:179
  60.2 0.7 collective-permute-start.4
  61.0 0.0 collective-permute-done.6.left_ref
  61.0 2.7 %collective-permute-done.7.right_ref = bf16[64,128]{1,0:T(8,128)(2,1)S(1)} collective-permute-done((bf16[64,128]{1,0:T(8,128)(2,1)S(1)}, bf16[64,128]{1,0:T(8,128)(2,1)S(1)}, u32[]{:S(2)}, u32[]{:S(2)}) %collective-permute-start.7) | collective-permute-done | bytes 16416 | tf_op jit(solution)/shard_map/ppermute | solution.py:180
  63.7 1.3 %shard_map.71 = bf16[24,64,128]{2,1,0:T(8,128)(2,1)S(1)} custom-call(bf16[24,64,128]{2,1,0:T(8,128)(2,1)S(1)} %get-tuple-element.21.d_ref, bf16[64,128]{1,0:T(8,128)(2,1)S(1)} %collective-permute-done.6.left_ref, bf16[64,128]{1,0:T(8,128)(2,1)S(1)} %collective-permute-done.7.right_ref, bf16[192,192]{1,0:T(8,128)(2,1)S(1)} %reshape.29.w_ref), custom_call_target="tpu_custom_call" | custom-call | flops 2000000000 | bytes 4000000 | tf_op jit(solution)/shard_map/pallas_call | solution.py:150
  65.0 2.1 %all-to-all-done.1 = f32[16,24,128]{2,1,0:T(8,128)S(1)} async-done(((f32[16,24,128]{2,1,0:T(8,128)}), f32[16,24,128]{2,1,0:T(8,128)S(1)}, u32[]{:S(2)}, u32[]{:S(2)}) %all-to-all-start.1) | async-done | bytes 196640 | tf_op jit(solution)/shard_map/all_to_all | solution.py:162
  67.1 0.7 broadcast_in_dim.8
  67.8 3.5 %all-to-all-start.2 = ((f32[16,24,128]{2,1,0:T(8,128)}), f32[16,24,128]{2,1,0:T(8,128)S(1)}, u32[]{:S(2)}, u32[]{:S(2)}) async-start(f32[16,24,128]{2,1,0:T(8,128)} %broadcast_in_dim.8), calls=%async_computation.2 | async-start | bytes 393216 | tf_op jit(solution)/shard_map/all_to_all | solution.py:162
  71.4 0.0 collective-permute-done.3.left_ref
  71.4 0.0 collective-permute-done.4.right_ref
  71.4 1.3 %shard_map.69 = bf16[24,64,128]{2,1,0:T(8,128)(2,1)S(1)} custom-call(bf16[24,64,128]{2,1,0:T(8,128)(2,1)S(1)} %get-tuple-element.17.d_ref, bf16[64,128]{1,0:T(8,128)(2,1)S(1)} %collective-permute-done.3.left_ref, bf16[64,128]{1,0:T(8,128)(2,1)S(1)} %collective-permute-done.4.right_ref, bf16[192,192]{1,0:T(8,128)(2,1)S(1)} %reshape.29.w_ref), custom_call_target="tpu_custom_call" | custom-call | flops 2000000000 | bytes 4000000 | tf_op jit(solution)/shard_map/pallas_call | solution.py:150
  72.7 0.1 pad_maximum_fusion
  72.8 1.4 %copy.38 = bf16[64,2,24,128]{3,2,1,0:T(8,128)(2,1)} copy(bf16[64,2,24,128]{3,0,2,1:T(8,128)(2,1)S(1)} %pad_maximum_fusion) | data formatting | bytes 1572864
  74.2 5.3 %all-to-all-done.2 = f32[16,24,128]{2,1,0:T(8,128)S(1)} async-done(((f32[16,24,128]{2,1,0:T(8,128)}), f32[16,24,128]{2,1,0:T(8,128)S(1)}, u32[]{:S(2)}, u32[]{:S(2)}) %all-to-all-start.2) | async-done | bytes 196640 | tf_op jit(solution)/shard_map/all_to_all | solution.py:162
  79.6 0.7 slice.61
  80.3 0.2 reshape.30
  80.5 0.7 copy.39
  (7 shorter events, 0.1 us)
Async XLA Ops:
  2.4 5.0 %copy-start.1 = (bf16[64,2,24,128]{3,2,1,0:T(8,128)(2,1)S(1)}, bf16[64,2,24,128]{3,2,1,0:T(8,128)(2,1)}, u32[]{:S(2)}) copy-start(bf16[64,2,24,128]{3,2,1,0:T(8,128)(2,1)} %param.5) | copy-start | bytes 2359300
  3.2 7.7 %collective-permute-start.1 = (bf16[64,128]{1,0:T(8,128)(2,1)S(1)}, bf16[64,128]{1,0:T(8,128)(2,1)S(1)}, u32[]{:S(2)}, u32[]{:S(2)}) collective-permute-start(bf16[64,128]{1,0:T(8,128)(2,1)S(1)} %pad.7), channel_id=1, source_target_pairs={{0,1},{1,2},{2,3},{3,4},{4,5},{5,6},{6,7},{7,8},{8,9},{9,10},{10,1... | collective-permute-start | bytes 49160 | tf_op jit(solution)/shard_map/ppermute | solution.py:179
  7.1 3.2 %copy-start = (bf16[64,2,24,128]{3,2,1,0:T(8,128)(2,1)S(1)}, bf16[64,2,24,128]{3,2,1,0:T(8,128)(2,1)}, u32[]{:S(2)}) copy-start(bf16[64,2,24,128]{3,2,1,0:T(8,128)(2,1)} %param.4) | copy-start | bytes 2359300
  7.1 3.8 %collective-permute-start.2 = (bf16[64,128]{1,0:T(8,128)(2,1)S(1)}, bf16[64,128]{1,0:T(8,128)(2,1)S(1)}, u32[]{:S(2)}, u32[]{:S(2)}) collective-permute-start(bf16[64,128]{1,0:T(8,128)(2,1)S(1)} %pad.8), channel_id=1, source_target_pairs={{1,0},{2,1},{3,2},{4,3},{5,4},{6,5},{7,6},{8,7},{9,8},{10,9},{11,1... | collective-permute-start | bytes 49160 | tf_op jit(solution)/shard_map/ppermute | solution.py:180
  7.5 3.0 %copy-start.2 = (bf16[3,3,64,64]{3,2,1,0:T(8,128)(2,1)S(1)}, bf16[3,3,64,64]{3,2,1,0:T(8,128)(2,1)}, u32[]{:S(2)}) copy-start(bf16[3,3,64,64]{3,2,1,0:T(8,128)(2,1)} %param.6) | copy-start | bytes 221188
  7.6 3.2 %copy-start.3 = (bf16[3,64,64]{2,1,0:T(8,128)(2,1)S(1)}, bf16[3,64,64]{2,1,0:T(8,128)(2,1)}, u32[]{:S(2)}) copy-start(bf16[3,64,64]{2,1,0:T(8,128)(2,1)} %param.7) | copy-start | bytes 73732
  7.6 10.0 %collective-permute-start = (bf16[24,64,128]{2,1,0:T(8,128)(2,1)S(1)}, bf16[24,64,128]{2,1,0:T(8,128)(2,1)S(1)}, u32[]{:S(2)}, u32[]{:S(2)}) collective-permute-start(bf16[24,64,128]{2,1,0:T(8,128)(2,1)S(1)} %bitcast.48), channel_id=1, source_target_pairs={{32,0},{64,32},{96,64},{128,96},{160,128},{192,160},{224,192},{33,... | collective-permute-start | bytes 1179656 | tf_op jit(solution)/shard_map/ppermute | solution.py:190
  9.0 16.4 %collective-permute-start.5 = (bf16[24,64,128]{2,1,0:T(8,128)(2,1)S(1)}, bf16[24,64,128]{2,1,0:T(8,128)(2,1)S(1)}, u32[]{:S(2)}, u32[]{:S(2)}) collective-permute-start(bf16[24,64,128]{2,1,0:T(8,128)(2,1)S(1)} %bitcast.45), channel_id=1, source_target_pairs={{32,0},{64,32},{96,64},{128,96},{160,128},{192,160},{224,192},{33,... | collective-permute-start | bytes 1179656 | tf_op jit(solution)/shard_map/ppermute | solution.py:190
  42.1 25.0 %all-to-all-start.1 = ((f32[16,24,128]{2,1,0:T(8,128)}), f32[16,24,128]{2,1,0:T(8,128)S(1)}, u32[]{:S(2)}, u32[]{:S(2)}) async-start(f32[16,24,128]{2,1,0:T(8,128)} %broadcast_in_dim.7), calls=%async_computation.1 | async-start | bytes 393216 | tf_op jit(solution)/shard_map/all_to_all | solution.py:162
  56.4 4.5 %collective-permute-start.6 = (bf16[64,128]{1,0:T(8,128)(2,1)S(1)}, bf16[64,128]{1,0:T(8,128)(2,1)S(1)}, u32[]{:S(2)}, u32[]{:S(2)}) collective-permute-start(bf16[64,128]{1,0:T(8,128)(2,1)S(1)} %get-tuple-element.22), channel_id=1, source_target_pairs={{0,1},{1,2},{2,3},{3,4},{4,5},{5,6},{6,7},{7,8},{8,9},{9,10},{10,1... | collective-permute-start | bytes 49160 | tf_op jit(solution)/shard_map/ppermute | solution.py:179
  58.1 5.6 %collective-permute-start.7 = (bf16[64,128]{1,0:T(8,128)(2,1)S(1)}, bf16[64,128]{1,0:T(8,128)(2,1)S(1)}, u32[]{:S(2)}, u32[]{:S(2)}) collective-permute-start(bf16[64,128]{1,0:T(8,128)(2,1)S(1)} %get-tuple-element.23), channel_id=1, source_target_pairs={{1,0},{2,1},{3,2},{4,3},{5,4},{6,5},{7,6},{8,7},{9,8},{10,9},{11,1... | collective-permute-start | bytes 49160 | tf_op jit(solution)/shard_map/ppermute | solution.py:180
  58.4 12.9 %collective-permute-start.3 = (bf16[64,128]{1,0:T(8,128)(2,1)S(1)}, bf16[64,128]{1,0:T(8,128)(2,1)S(1)}, u32[]{:S(2)}, u32[]{:S(2)}) collective-permute-start(bf16[64,128]{1,0:T(8,128)(2,1)S(1)} %get-tuple-element.18), channel_id=1, source_target_pairs={{0,1},{1,2},{2,3},{3,4},{4,5},{5,6},{6,7},{7,8},{8,9},{9,10},{10,1... | collective-permute-start | bytes 49160 | tf_op jit(solution)/shard_map/ppermute | solution.py:179
  60.2 11.1 %collective-permute-start.4 = (bf16[64,128]{1,0:T(8,128)(2,1)S(1)}, bf16[64,128]{1,0:T(8,128)(2,1)S(1)}, u32[]{:S(2)}, u32[]{:S(2)}) collective-permute-start(bf16[64,128]{1,0:T(8,128)(2,1)S(1)} %get-tuple-element.19), channel_id=1, source_target_pairs={{1,0},{2,1},{3,2},{4,3},{5,4},{6,5},{7,6},{8,7},{9,8},{10,9},{11,1... | collective-permute-start | bytes 49160 | tf_op jit(solution)/shard_map/ppermute | solution.py:180
  67.8 11.7 %all-to-all-start.2 = ((f32[16,24,128]{2,1,0:T(8,128)}), f32[16,24,128]{2,1,0:T(8,128)S(1)}, u32[]{:S(2)}, u32[]{:S(2)}) async-start(f32[16,24,128]{2,1,0:T(8,128)} %broadcast_in_dim.8), calls=%async_computation.2 | async-start | bytes 393216 | tf_op jit(solution)/shard_map/all_to_all | solution.py:162

commit v2 on v1

v2 whole, which is shorter than its diff:
```python
import functools
import math

import jax
import jax.numpy as jnp
import numpy as np
from jax import lax
from jax.experimental import pallas as pl
from jax.experimental.pallas import tpu as pltpu
from jax.sharding import Mesh
from jax.sharding import PartitionSpec as P

AXES = ("y", "xh", "xl", "z", "c")
TM = ("y", "xh")
LON = ("xl", "z", "c")
PLANE = ("y", "xh", "xl")
LINE = ("z", "c")
F32 = jnp.float32
BF16 = jnp.bfloat16
ROWS = 8
GAP = 32
VMEM_LIMIT = 16 * 1024 * 1024


def dot_nt(a, b):
    return lax.dot_general(a, b, (((1,), (1,)), ((), ())), preferred_element_type=F32)


def lane_of(f, h):
    return f * GAP + h


def lane_taps(slab, edge, at):
    width = slab.shape[1]
    lane = lax.broadcasted_iota(jnp.int32, slab.shape, 1)
    wide = slab.astype(F32)
    before = jnp.where(lane == 0, pltpu.roll(edge, width - at, 1), pltpu.roll(wide, 1, 1))
    after = jnp.where(lane == width - 1, pltpu.roll(edge, width // 2 - 1 - at, 1), pltpu.roll(wide, width - 1, 1))
    return before.astype(BF16), slab, after.astype(BF16)


def edge_kernel(x_ref, c0_ref, c1_ref, right_ref, left_ref, own_ref):
    frames, rows, chans, cols = x_ref.shape
    lane = lax.broadcasted_iota(jnp.int32, (chans, cols), 1)
    sums = (jnp.zeros((chans, cols), F32),) * 6
    for f, c_ref in enumerate((c0_ref, c1_ref)):

        def step(g, sums, f=f, c_ref=c_ref):
            for r in range(ROWS):
                h = g * ROWS + r
                at = lane_of(f, h)
                here, beside = lane == at, lane == at + 1
                wide = x_ref[f, h].astype(F32)
                low = pltpu.roll(wide, at, 1)
                high = pltpu.roll(wide, at + 2, 1)
                cot = c_ref[h].astype(F32)
                vals = (low, low, high, high, pltpu.roll(cot, at, 1), pltpu.roll(cot, at + 1, 1))
                masks = (here, beside, here, beside, here, here)
                sums = tuple(jnp.where(m, v, s) for m, v, s in zip(masks, vals, sums))
            return sums

        sums = lax.fori_loop(0, rows // ROWS, step, sums)
    first, second, before_last, last, cot_first, cot_last = sums
    half = cols // 2
    last = pltpu.roll(last, cols - 1, 1)
    right_ref[0:chans] = before_last.astype(BF16)
    right_ref[chans : 2 * chans] = last.astype(BF16)
    right_ref[2 * chans : 3 * chans] = cot_last.astype(BF16)
    left_ref[0:chans] = pltpu.roll(first, half, 1).astype(BF16)
    left_ref[chans : 2 * chans] = pltpu.roll(second, half - 1, 1).astype(BF16)
    left_ref[2 * chans : 3 * chans] = pltpu.roll(cot_first, half, 1).astype(BF16)
    own_ref[...] = (first + pltpu.roll(last, half, 1)).astype(BF16)


def silu_parts(pre):
    s = 1.0 / (1.0 + jnp.exp(-pre))
    return pre * s, s * (1.0 + pre * (1.0 - s))


def forward_kernel(x_ref, from_left_ref, from_right_ref, own_ref, w_ref, x3_ref, act_ref, slope_ref, edge_slope_ref, y_ref):
    frames, rows, chans, cols = x_ref.shape
    weight = w_ref[...]
    left_half = lax.broadcasted_iota(jnp.int32, (chans, cols), 1) < cols // 2
    own = own_ref[...].astype(F32)
    taps = [
        jnp.where(left_half, a.astype(F32), b.astype(F32))
        for a, b in (
            (from_left_ref[0:chans], own),
            (from_left_ref[chans : 2 * chans], from_right_ref[0:chans]),
            (own, from_right_ref[chans : 2 * chans]),
        )
    ]
    edge = taps[1]
    ye = jnp.dot(weight, jnp.concatenate(taps, axis=0).astype(BF16), preferred_element_type=F32)
    pre = (
        pltpu.roll(ye[0:chans], 1, 1)
        + ye[chans : 2 * chans]
        + pltpu.roll(ye[2 * chans : 3 * chans], cols - 1, 1)
    )
    edge_slope_ref[...] = silu_parts(pre)[1]
    zero = jnp.zeros((3 * chans, cols), F32)
    y_ref[0] = zero
    y_ref[rows + 1] = zero
    for f in range(frames):

        @pl.loop(0, rows // ROWS)
        def _(g):
            wide = []
            for r in range(ROWS):
                h = g * ROWS + r
                x3 = jnp.concatenate(lane_taps(x_ref[f, h], edge, lane_of(f, h)), axis=0)
                x3_ref[f, h] = x3
                wide.append(x3)
            y = jnp.dot(weight, jnp.concatenate(wide, axis=1), preferred_element_type=F32)
            for r in range(ROWS):
                y_ref[g * ROWS + r + 1] = y[:, r * cols : (r + 1) * cols]

        @pl.loop(0, rows // ROWS)
        def _(g):
            for r in range(ROWS):
                h = g * ROWS + r
                pre = (
                    y_ref[h, 0:chans]
                    + y_ref[h + 1, chans : 2 * chans]
                    + y_ref[h + 2, 2 * chans : 3 * chans]
                )
                act, slope = silu_parts(pre)
                act_ref[f, h] = act.astype(BF16)
                slope_ref[f, h] = slope


def grads_kernel(f, c0_ref, c1_ref, c2_ref, act_ref, slope_ref, x3_ref, w_ref, base_ref, d_ref, sum_ref, d_scr):
    rows, chans, cols = d_ref.shape
    weight = w_ref[...]
    d_scr[0] = jnp.zeros((chans, cols), BF16)
    d_scr[rows + 1] = jnp.zeros((chans, cols), BF16)
    t_sum = jnp.zeros((3 * chans, chans), F32)
    for g in range(rows // ROWS):
        hs = range(g * ROWS, (g + 1) * ROWS)
        cot = jnp.concatenate(
            [jnp.concatenate([ref[h] for h in hs], axis=1) for ref in (c0_ref, c1_ref, c2_ref)], axis=0
        )
        up = jnp.dot(weight, cot, preferred_element_type=F32)
        for r, h in enumerate(hs):
            d = (up[:, r * cols : (r + 1) * cols] * slope_ref[f, h]).astype(BF16)
            d_ref[h] = d
            d_scr[h + 1] = d
        act = jnp.concatenate([act_ref[f, h] for h in hs], axis=1)
        t_sum = t_sum + dot_nt(cot, act)
    g_sum = jnp.zeros((3 * chans, 3 * chans), F32)
    for g in range(rows // ROWS):
        hs = range(g * ROWS, (g + 1) * ROWS)
        d3 = jnp.concatenate(
            [jnp.concatenate([d_scr[h - i + 2] for h in hs], axis=1) for i in range(3)], axis=0
        )
        x3 = jnp.concatenate([x3_ref[f, h] for h in hs], axis=1)
        g_sum = g_sum + dot_nt(d3, x3)
    both = jnp.concatenate([g_sum, t_sum], axis=1)
    half = both.shape[1] // 2
    if f == 0:
        sum_ref[0] = both[:, :half]
        sum_ref[1] = both[:, half:]
    else:
        sum_ref[0] = base_ref[0] + both[:, :half]
        sum_ref[1] = base_ref[1] + both[:, half:]


def back_kernel(d0_ref, d1_ref, near_left_ref, near_right_ref, far_left_ref, far_right_ref, slope_ref, w_up_ref, w_ref,
                out0_ref, out1_ref, z_ref):
    rows, chans, cols = d0_ref.shape
    weight = w_ref[...]
    lane = lax.broadcasted_iota(jnp.int32, (chans, cols), 1)
    left_half = lane < cols // 2
    near = jnp.where(left_half, near_left_ref[...].astype(F32), near_right_ref[...].astype(F32))
    far = jnp.where(left_half, far_left_ref[...].astype(F32), far_right_ref[...].astype(F32))
    mixed = jnp.where(lane % (2 * GAP) < GAP, pltpu.roll(near, cols - GAP, 1), pltpu.roll(far, GAP, 1))
    cot = jnp.concatenate([near, mixed, far], axis=0).astype(BF16)
    up = jnp.dot(w_up_ref[...], cot, preferred_element_type=F32)
    edge = (up * slope_ref[...]).astype(BF16).astype(F32)
    zero = jnp.zeros((3 * chans, cols), F32)
    z_ref[0] = zero
    z_ref[rows + 1] = zero
    for f, (d_ref, out_ref) in enumerate(((d0_ref, out0_ref), (d1_ref, out1_ref))):

        @pl.loop(0, rows // ROWS)
        def _(g):
            wide = []
            for r in range(ROWS):
                h = g * ROWS + r
                before, same, after = lane_taps(d_ref[h], edge, lane_of(f, h))
                wide.append(jnp.concatenate([after, same, before], axis=0))
            z = jnp.dot(weight, jnp.concatenate(wide, axis=1), preferred_element_type=F32)
            for r in range(ROWS):
                z_ref[g * ROWS + r + 1] = z[:, r * cols : (r + 1) * cols]

        @pl.loop(0, rows // ROWS)
        def _(g):
            for r in range(ROWS):
                h = g * ROWS + r
                out = (
                    z_ref[h + 2, 0:chans]
                    + z_ref[h + 1, chans : 2 * chans]
                    + z_ref[h, 2 * chans : 3 * chans]
                )
                out_ref[h] = out.astype(BF16)


def finish_kernel(scale, sum_ref, space_ref, time_ref):
    taps, chans = time_ref.shape[:2]
    for i in range(taps):
        rows = slice(i * chans, (i + 1) * chans)
        low = sum_ref[0, rows, :] * scale
        high = sum_ref[1, rows, :] * scale
        space_ref[i, 0] = low[:, :chans]
        space_ref[i, 1] = low[:, chans:]
        space_ref[i, 2] = high[:, :chans]
        time_ref[i] = high[:, chans:]


def in_vmem(count):
    return [pl.BlockSpec(memory_space=pltpu.VMEM)] * count


def call(kernel, args, outs, scratch, flops):
    return pl.pallas_call(
        kernel,
        out_shape=outs,
        in_specs=in_vmem(len(args)),
        out_specs=tuple(in_vmem(len(outs))),
        scratch_shapes=scratch,
        compiler_params=pltpu.CompilerParams(vmem_limit_bytes=VMEM_LIMIT),
        cost_estimate=pl.CostEstimate(flops=flops, transcendentals=0, bytes_accessed=flops // 1000),
    )(*args)


def exchange(cells, axes):
    return lax.all_to_all(cells, axes, 0, 0, tiled=True)


def spread(cells, axes):
    count = lax.axis_size(axes)
    return exchange(jnp.broadcast_to(cells[None], (count,) + cells.shape), axes)


def sum_over_all(cells):
    count = lax.axis_size(PLANE)
    parts = exchange(cells.reshape(count, -1, cells.shape[-1]), PLANE).sum(0)
    parts = spread(parts, LINE).sum(0)
    return spread(parts, PLANE).reshape(cells.shape)


def shifted(cells, tm_step, lon_step):
    blocks, sectors = lax.axis_size(TM), lax.axis_size(LON)
    pairs = [
        ((t + tm_step) * sectors + (s + lon_step) % sectors, t * sectors + s)
        for t in range(blocks - tm_step)
        for s in range(sectors)
    ]
    return lax.ppermute(cells, TM + LON, pairs)


def body(frames, cotangent, w_space, w_time):
    chans, nf, rows, cols = frames.shape
    shape = jax.ShapeDtypeStruct
    slabs = (rows, chans, cols)
    edge = shape((chans, cols), BF16)
    edges = shape((3 * chans, cols), BF16)
    sums = shape((2, 3 * chans, 2 * chans), F32)
    cot = [jnp.transpose(cotangent[:, f], (1, 0, 2)) for f in range(nf)]
    cot[0], cot[1], frames = lax.optimization_barrier((cot[0], cot[1], frames))
    cot += [shifted(c, 1, 0) for c in cot]

    field = jnp.transpose(frames, (1, 2, 0, 3))
    to_right, to_left, own = call(edge_kernel, (field, cot[0], cot[1]), (edges, edges, edge), [], 10_000_000)
    from_left, from_right = shifted(to_right, 0, -1), shifted(to_left, 0, 1)
    far_left = shifted(to_right[2 * chans :], 1, -1)
    far_right = shifted(to_left[2 * chans :], 1, 1)
    w_fwd = jnp.transpose(w_space, (0, 2, 1, 3)).reshape(3 * chans, 3 * chans)
    w_bwd = jnp.transpose(w_space, (0, 3, 1, 2)).reshape(3 * chans, 3 * chans)
    w_up = jnp.transpose(w_time, (2, 0, 1)).reshape(chans, 3 * chans)
    x3, act, slope, edge_slope = call(
        forward_kernel,
        (field, from_left, from_right, own, w_fwd),
        (
            shape((nf, rows, 3 * chans, cols), BF16),
            shape((nf,) + slabs, BF16),
            shape((nf,) + slabs, F32),
            shape((chans, cols), F32),
        ),
        [pltpu.VMEM((rows + 2, 3 * chans, cols), F32)],
        10_000_000,
    )
    total = jnp.zeros((1, 8, 128), F32)
    dpre = []
    for f in range(nf):
        d, total = call(
            functools.partial(grads_kernel, f),
            (cot[f], cot[f + 1], cot[f + 2], act, slope, x3, w_up, total),
            (shape(slabs, BF16), sums),
            [pltpu.VMEM((rows + 2, chans, cols), BF16)],
            4_000_000_000,
        )
        dpre.append(d)
    total, far_left, far_right = lax.optimization_barrier((total, far_left, far_right))
    near = (from_left[2 * chans :], from_right[2 * chans :])
    out = call(
        back_kernel,
        (dpre[0], dpre[1], *near, far_left, far_right, edge_slope, w_up, w_bwd),
        (shape(slabs, BF16), shape(slabs, BF16)),
        [pltpu.VMEM((rows + 2, 3 * chans, cols), F32)],
        4_000_000_000,
    )
    grad_frames = jnp.stack([jnp.transpose(o, (1, 0, 2)) for o in out], axis=1)
    cells = nf * lax.axis_size(TM) * rows * cols * lax.axis_size(LON)
    total = sum_over_all(total.reshape(-1, 2 * chans)).reshape(sums.shape)
    grad_sp, grad_tm = call(
        functools.partial(finish_kernel, 1.0 / math.sqrt(cells)),
        (total,),
        (shape(w_space.shape, F32), shape(w_time.shape, F32)),
        [],
        1_000_000,
    )
    return grad_frames, grad_sp, grad_tm


def solution(mesh):
    fine = Mesh(np.asarray(mesh.devices).reshape(4, 2, 2, 8, 2), AXES)
    field = P(None, TM, None, LON)
    return jax.shard_map(
        body,
        mesh=fine,
        in_specs=(field, field, P(), P()),
        out_specs=(field, P(), P()),
        check_vma=False,
    )
```

time: 81.7 us -> 79.6 us (0.974)
  starting transfers between devices: 28.1 us -> 23.4 us
  local copies, waits for them, and re-layouts: 9.3 us -> 5.18 us
  Pallas kernels: 8.5 us -> 11.2 us
  blocking collectives: 14.6 us -> 16.9 us
  waiting for transfers between devices: 19.7 us -> 21.5 us
    all_to_all x2, waiting for transfers between devices: 7.44 us -> 13.6 us  [exchange(): return lax.all_to_all(cells, axes, 0, 0, tiled=True)]
    ppermute x8 -> x6, waiting for transfers between devices: 12.2 us -> 7.81 us  [shifted(): return lax.ppermute(cells, TM + LON, pairs)]
    all_to_all x2, starting transfers between devices: 17.9 us -> 14.9 us  [exchange(): return lax.all_to_all(cells, axes, 0, 0, tiled=True)]
    pallas_call x5 -> x6, Pallas kernels: 8.5 us -> 11.2 us  [call(): pl.pallas_call(kernel, out_shape=outs, in_specs=in_vmem(len(args)), out_s...]
    slice x3 -> x4, local copies, waits for them, and re-layouts: 2.49 us -> 0.01 us  [the longest x2 0.01 us: body(): near = (from_left[2 * chans:], from_right[2 * chans:])]
    unnamed x15 -> x7, local copies, waits for them, and re-layouts: 3.88 us -> 1.41 us
    all_to_all x1, blocking collectives: 14.6 us -> 16.9 us  [exchange(): return lax.all_to_all(cells, axes, 0, 0, tiled=True)]
    ppermute x8 -> x6, starting transfers between devices: 10.2 us -> 8.56 us  [shifted(): return lax.ppermute(cells, TM + LON, pairs)]
  transfers between devices with their start and end apart: 10 -> 8, of which waited for: 5 -> 4; matrix products, arithmetic and copies ran while one was open for 6% -> 3% of each run, Pallas kernels for 9% -> 13%
where the time goes in v2:
time: 79.6 us; the launch traced here: 79.1 us
  starting transfers between devices  23.4 us (29%)
  waiting for transfers between devices  21.5 us (27%)
  blocking collectives  16.9 us (21%)
  Pallas kernels  11.2 us (14%)
  local copies, waits for them, and re-layouts  5.18 us (7%)
  between operations  0.86 us (1%)
    all_to_all x1, blocking collectives, exchange(): return lax.all_to_all(cells, axes, 0, 0, tiled=True)  16.9 us
    all_to_all x2, starting transfers between devices, exchange(): return lax.all_to_all(cells, axes, 0, 0, tiled=True)  14.9 us
    all_to_all x2, waiting for transfers between devices, exchange(): return lax.all_to_all(cells, axes, 0, 0, tiled=True)  13.6 us
    pallas_call x6, Pallas kernels, call(): pl.pallas_call(kernel, out_shape=outs, in_specs=in_vmem(len(args)), out_s...  11.2 us
    ppermute x6, starting transfers between devices, shifted(): return lax.ppermute(cells, TM + LON, pairs)  8.56 us
    ppermute x6, waiting for transfers between devices, shifted(): return lax.ppermute(cells, TM + LON, pairs)  7.81 us
  transfers between devices with their start and end apart: 8, of which 4 were waited for; matrix products, arithmetic and copies ran while one was open for 3% of the time, Pallas kernels for 13%

profile of v2, /device:TPU:1, one launch (start us, length us, event | category | flops | bytes accessed | tf_op | source)
XLA Modules:
  0.0 79.1 jit_solution(17294900980851530621)
XLA Ops:
  0.6 0.0 copy-start
  0.6 1.3 %fusion = (bf16[64,1,24,128]{3,2,1,0:T(8,128)(2,1)S(1)}, bf16[64,1,24,128]{3,2,1,0:T(8,128)(2,1)S(1)}) fusion(bf16[64,2,24,128]{3,2,1,0:T(8,128)(2,1)} %param.5), kind=kLoop, calls=%fused_computation.4 | loop fusion | bytes 1572864 | tf_op jit(solution)/shard_map/slice | solution.py:269
  1.9 0.0 copy-start.1
  1.9 0.0 copy-start.2
  1.9 0.2 copy_bitcast_fusion.1
  2.1 1.3 %collective-permute-start = (bf16[24,64,128]{2,1,0:T(8,128)(2,1)S(1)}, bf16[24,64,128]{2,1,0:T(8,128)(2,1)S(1)}, u32[]{:S(2)}, u32[]{:S(2)}) collective-permute-start(bf16[24,64,128]{2,1,0:T(8,128)(2,1)S(1)} %get-tuple-element.24.c0_ref), channel_id=1, source_target_pairs={{32,0},{33,1},{34,2},{35,3},{36,4},{37,5},{38,6},{39,7},{40,8},{41... | collective-permute-start | bytes 1179656 | tf_op jit(solution)/shard_map/ppermute | solution.py:259
  3.4 0.0 copy-done
  3.4 0.2 copy.37
  3.7 1.4 %shard_map.67 = (bf16[192,128]{1,0:T(8,128)(2,1)S(1)}, bf16[192,128]{1,0:T(8,128)(2,1)S(1)}, bf16[64,128]{1,0:T(8,128)(2,1)S(1)}) custom-call(bf16[2,24,64,128]{3,2,1,0:T(8,128)(2,1)S(1)} %bitcast.24, bf16[24,64,128]{2,1,0:T(8,128)(2,1)S(1)} %get-tuple-element.24.c0_ref, bf16[24,64,128]{2,1,0:T(8,128)(2,1)S(1)} %get-tuple-element.25.c1_ref.c0_ref), custom_call_target="tpu_custom_call" | custom-call | flops 10000000 | bytes 10000 | tf_op jit(solution)/shard_map/pallas_call | solution.py:225
  5.1 3.1 %collective-permute-start.1 = (bf16[192,128]{1,0:T(8,128)(2,1)S(1)}, bf16[192,128]{1,0:T(8,128)(2,1)S(1)}, u32[]{:S(2)}, u32[]{:S(2)}) collective-permute-start(bf16[192,128]{1,0:T(8,128)(2,1)S(1)} %get-tuple-element.27), channel_id=1, source_target_pairs={{31,0},{0,1},{1,2},{2,3},{3,4},{4,5},{5,6},{6,7},{7,8},{8,9},{9,10... | collective-permute-start | bytes 147464 | tf_op jit(solution)/shard_map/ppermute | solution.py:259
  8.2 0.3 collective-permute-start.2
  8.5 1.3 %collective-permute-start.3 = (bf16[24,64,128]{2,1,0:T(8,128)(2,1)S(1)}, bf16[24,64,128]{2,1,0:T(8,128)(2,1)S(1)}, u32[]{:S(2)}, u32[]{:S(2)}) collective-permute-start(bf16[24,64,128]{2,1,0:T(8,128)(2,1)S(1)} %get-tuple-element.25.c1_ref.c0_ref), channel_id=1, source_target_pairs={{32,0},{33,1},{34,2},{35,3},{36,4},{37,5},{38,6},{39,7},{40,8},{41... | collective-permute-start | bytes 1179656 | tf_op jit(solution)/shard_map/ppermute | solution.py:259
  9.8 1.3 %collective-permute-start.4 = (bf16[64,128]{1,0:T(8,128)(2,1)S(1)}, bf16[64,128]{1,0:T(8,128)(2,1)S(1)}, u32[]{:S(2)}, u32[]{:S(2)}) collective-permute-start(bf16[64,128]{1,0:T(8,128)(2,1)S(1)} %slice.22), channel_id=1, source_target_pairs={{63,0},{32,1},{33,2},{34,3},{35,4},{36,5},{37,6},{38,7},{39,8},{40... | collective-permute-start | bytes 49160 | tf_op jit(solution)/shard_map/ppermute | solution.py:259
  11.1 0.0 copy-done.1
  11.1 0.1 copy.26
  11.3 0.2 reshape.17.w_ref
  11.4 0.0 copy-done.2
  11.4 0.1 copy.27.w_ref.w_up_ref
  11.5 0.0 collective-permute-done.1.from_left_ref
  11.5 1.3 %collective-permute-start.5 = (bf16[64,128]{1,0:T(8,128)(2,1)S(1)}, bf16[64,128]{1,0:T(8,128)(2,1)S(1)}, u32[]{:S(2)}, u32[]{:S(2)}) collective-permute-start(bf16[64,128]{1,0:T(8,128)(2,1)S(1)} %slice.23), channel_id=1, source_target_pairs={{33,0},{34,1},{35,2},{36,3},{37,4},{38,5},{39,6},{40,7},{41,8},{42... | collective-permute-start | bytes 49160 | tf_op jit(solution)/shard_map/ppermute | solution.py:259
  12.8 0.0 collective-permute-done.2.from_right_ref
  12.8 3.4 %shard_map.68 = (bf16[2,24,192,128]{3,2,1,0:T(8,128)(2,1)S(1)}, bf16[2,24,64,128]{3,2,1,0:T(8,128)(2,1)S(1)}, f32[2,24,64,128]{3,2,1,0:T(8,128)S(1)}, f32[64,128]{1,0:T(8,128)S(1)}) custom-call(bf16[2,24,64,128]{3,2,1,0:T(8,128)(2,1)S(1)} %bitcast.25, bf16[192,128]{1,0:T(8,128)(2,1)S(1)} %collective-permute-done.1.from_left_ref, ...), custom_call_target="tpu_custom_call" | custom-call | flops 10000000 | bytes 10000 | tf_op jit(solution)/shard_map/pallas_call | solution.py:225
  16.2 0.0 collective-permute-done.c2_ref.c1_ref
  16.3 1.3 %shard_map.69 = (bf16[24,64,128]{2,1,0:T(8,128)(2,1)S(1)}, f32[2,192,128]{2,1,0:T(8,128)S(1)}) custom-call(bf16[24,64,128]{2,1,0:T(8,128)(2,1)S(1)} %get-tuple-element.24.c0_ref, bf16[24,64,128]{2,1,0:T(8,128)(2,1)S(1)} %get-tuple-element.25.c1_ref.c0_ref, bf16[24,64,128]{2,1,0:T(8,128)(2,1)S(1)} %collective-permute-done.c2_ref.c1_ref, ...), custom_call_target="tpu_custom_call" | custom-call | flops 4000000000 | bytes 4000000 | tf_op jit(solution)/shard_map/pallas_call | solution.py:225
  17.6 6.2 %collective-permute-done.3.c2_ref = bf16[24,64,128]{2,1,0:T(8,128)(2,1)S(1)} collective-permute-done((bf16[24,64,128]{2,1,0:T(8,128)(2,1)S(1)}, bf16[24,64,128]{2,1,0:T(8,128)(2,1)S(1)}, u32[]{:S(2)}, u32[]{:S(2)}) %collective-permute-start.3) | collective-permute-done | bytes 393248 | tf_op jit(solution)/shard_map/ppermute | solution.py:259
  23.8 1.3 %shard_map.70 = (bf16[24,64,128]{2,1,0:T(8,128)(2,1)S(1)}, f32[2,192,128]{2,1,0:T(8,128)S(1)}) custom-call(bf16[24,64,128]{2,1,0:T(8,128)(2,1)S(1)} %get-tuple-element.25.c1_ref.c0_ref, bf16[24,64,128]{2,1,0:T(8,128)(2,1)S(1)} %collective-permute-done.c2_ref.c1_ref, bf16[24,64,128]{2,1,0:T(8,128)(2,1)S(1)} %collective-permute-done.3.c2_ref, ...), custom_call_target="tpu_custom_call" | custom-call | flops 4000000000 | bytes 4000000 | tf_op jit(solution)/shard_map/pallas_call | solution.py:225
  25.1 1.6 %collective-permute-done.4.far_left_ref = bf16[64,128]{1,0:T(8,128)(2,1)S(1)} collective-permute-done((bf16[64,128]{1,0:T(8,128)(2,1)S(1)}, bf16[64,128]{1,0:T(8,128)(2,1)S(1)}, u32[]{:S(2)}, u32[]{:S(2)}) %collective-permute-start.4) | collective-permute-done | bytes 16416 | tf_op jit(solution)/shard_map/ppermute | solution.py:259
  26.7 0.0 collective-permute-done.5.far_right_ref
  26.7 16.9 %all_to_all.15 = f32[16,24,128]{2,1,0:T(8,128)S(1)} all-to-all(f32[16,24,128]{2,1,0:T(8,128)S(1)} %bitcast.29), channel_id=1, replica_groups=mesh['y'=4,'xh'=2,'xl'=2,'z'=8,'c'=2] {'y','xh','xl'}, dimensions={0} | all-to-all | bytes 393216 | tf_op jit(solution)/shard_map/all_to_all | solution.py:237
  43.6 0.7 broadcast_in_dim.7
  44.3 11.4 %all-to-all-start.1 = ((f32[16,24,128]{2,1,0:T(8,128)}), f32[16,24,128]{2,1,0:T(8,128)S(1)}, u32[]{:S(2)}, u32[]{:S(2)}) async-start(f32[16,24,128]{2,1,0:T(8,128)} %broadcast_in_dim.7), calls=%async_computation.1 | async-start | bytes 393216 | tf_op jit(solution)/shard_map/all_to_all | solution.py:237
  55.7 0.2 copy.29
  55.8 0.2 reshape.19.w_ref
  56.0 10.0 %all-to-all-done.1 = f32[16,24,128]{2,1,0:T(8,128)S(1)} async-done(((f32[16,24,128]{2,1,0:T(8,128)}), f32[16,24,128]{2,1,0:T(8,128)S(1)}, u32[]{:S(2)}, u32[]{:S(2)}) %all-to-all-start.1) | async-done | bytes 196640 | tf_op jit(solution)/shard_map/all_to_all | solution.py:237
  66.0 0.7 broadcast_in_dim.8
  66.7 3.5 %all-to-all-start.2 = ((f32[16,24,128]{2,1,0:T(8,128)}), f32[16,24,128]{2,1,0:T(8,128)S(1)}, u32[]{:S(2)}, u32[]{:S(2)}) async-start(f32[16,24,128]{2,1,0:T(8,128)} %broadcast_in_dim.8), calls=%async_computation.2 | async-start | bytes 393216 | tf_op jit(solution)/shard_map/all_to_all | solution.py:237
  70.2 2.9 %shard_map.71 = (bf16[24,64,128]{2,1,0:T(8,128)(2,1)S(1)}, bf16[24,64,128]{2,1,0:T(8,128)(2,1)S(1)}) custom-call(bf16[24,64,128]{2,1,0:T(8,128)(2,1)S(1)} %get-tuple-element.33.d0_ref, bf16[24,64,128]{2,1,0:T(8,128)(2,1)S(1)} %get-tuple-element.35.d1_ref, bf16[64,128]{1,0:T(8,128)(2,1)S(1)} %slice.24.near_left_ref, ...), custom_call_target="tpu_custom_call" | custom-call | flops 4000000000 | bytes 4000000 | tf_op jit(solution)/shard_map/pallas_call | solution.py:225
  73.1 0.1 pad_maximum_fusion
  73.2 1.4 %copy.31 = bf16[64,2,24,128]{3,2,1,0:T(8,128)(2,1)} copy(bf16[64,2,24,128]{3,0,2,1:T(8,128)(2,1)S(1)} %pad_maximum_fusion) | data formatting | bytes 1572864
  74.6 3.7 %all-to-all-done.2 = f32[16,24,128]{2,1,0:T(8,128)S(1)} async-done(((f32[16,24,128]{2,1,0:T(8,128)}), f32[16,24,128]{2,1,0:T(8,128)S(1)}, u32[]{:S(2)}, u32[]{:S(2)}) %all-to-all-start.2) | async-done | bytes 196640 | tf_op jit(solution)/shard_map/all_to_all | solution.py:237
  78.3 0.8 %shard_map.72 = (f32[3,3,64,64]{3,2,1,0:T(8,128)}, f32[3,64,64]{2,1,0:T(8,128)}) custom-call(f32[2,192,128]{2,1,0:T(8,128)S(1)} %bitcast.26), custom_call_target="tpu_custom_call" | custom-call | flops 1000000 | bytes 1000 | tf_op jit(solution)/shard_map/pallas_call | solution.py:225
  (7 shorter events, 0.1 us)
Async XLA Ops:
  0.6 2.8 %copy-start = (bf16[64,2,24,128]{3,2,1,0:T(8,128)(2,1)S(1)}, bf16[64,2,24,128]{3,2,1,0:T(8,128)(2,1)}, u32[]{:S(2)}) copy-start(bf16[64,2,24,128]{3,2,1,0:T(8,128)(2,1)} %param.4) | copy-start | bytes 2359300
  1.9 9.2 %copy-start.1 = (bf16[3,3,64,64]{3,2,1,0:T(8,128)(2,1)S(1)}, bf16[3,3,64,64]{3,2,1,0:T(8,128)(2,1)}, u32[]{:S(2)}) copy-start(bf16[3,3,64,64]{3,2,1,0:T(8,128)(2,1)} %param.6) | copy-start | bytes 221188
  1.9 9.5 %copy-start.2 = (bf16[3,64,64]{2,1,0:T(8,128)(2,1)S(1)}, bf16[3,64,64]{2,1,0:T(8,128)(2,1)}, u32[]{:S(2)}) copy-start(bf16[3,64,64]{2,1,0:T(8,128)(2,1)} %param.7) | copy-start | bytes 73732
  2.1 14.1 %collective-permute-start = (bf16[24,64,128]{2,1,0:T(8,128)(2,1)S(1)}, bf16[24,64,128]{2,1,0:T(8,128)(2,1)S(1)}, u32[]{:S(2)}, u32[]{:S(2)}) collective-permute-start(bf16[24,64,128]{2,1,0:T(8,128)(2,1)S(1)} %get-tuple-element.24.c0_ref), channel_id=1, source_target_pairs={{32,0},{33,1},{34,2},{35,3},{36,4},{37,5},{38,6},{39,7},{40,8},{41... | collective-permute-start | bytes 1179656 | tf_op jit(solution)/shard_map/ppermute | solution.py:259
  5.1 6.4 %collective-permute-start.1 = (bf16[192,128]{1,0:T(8,128)(2,1)S(1)}, bf16[192,128]{1,0:T(8,128)(2,1)S(1)}, u32[]{:S(2)}, u32[]{:S(2)}) collective-permute-start(bf16[192,128]{1,0:T(8,128)(2,1)S(1)} %get-tuple-element.27), channel_id=1, source_target_pairs={{31,0},{0,1},{1,2},{2,3},{3,4},{4,5},{5,6},{6,7},{7,8},{8,9},{9,10... | collective-permute-start | bytes 147464 | tf_op jit(solution)/shard_map/ppermute | solution.py:259
  8.2 4.6 %collective-permute-start.2 = (bf16[192,128]{1,0:T(8,128)(2,1)S(1)}, bf16[192,128]{1,0:T(8,128)(2,1)S(1)}, u32[]{:S(2)}, u32[]{:S(2)}) collective-permute-start(bf16[192,128]{1,0:T(8,128)(2,1)S(1)} %get-tuple-element.28), channel_id=1, source_target_pairs={{1,0},{2,1},{3,2},{4,3},{5,4},{6,5},{7,6},{8,7},{9,8},{10,9},{11,1... | collective-permute-start | bytes 147464 | tf_op jit(solution)/shard_map/ppermute | solution.py:259
  8.5 15.3 %collective-permute-start.3 = (bf16[24,64,128]{2,1,0:T(8,128)(2,1)S(1)}, bf16[24,64,128]{2,1,0:T(8,128)(2,1)S(1)}, u32[]{:S(2)}, u32[]{:S(2)}) collective-permute-start(bf16[24,64,128]{2,1,0:T(8,128)(2,1)S(1)} %get-tuple-element.25.c1_ref.c0_ref), channel_id=1, source_target_pairs={{32,0},{33,1},{34,2},{35,3},{36,4},{37,5},{38,6},{39,7},{40,8},{41... | collective-permute-start | bytes 1179656 | tf_op jit(solution)/shard_map/ppermute | solution.py:259
  9.8 16.9 %collective-permute-start.4 = (bf16[64,128]{1,0:T(8,128)(2,1)S(1)}, bf16[64,128]{1,0:T(8,128)(2,1)S(1)}, u32[]{:S(2)}, u32[]{:S(2)}) collective-permute-start(bf16[64,128]{1,0:T(8,128)(2,1)S(1)} %slice.22), channel_id=1, source_target_pairs={{63,0},{32,1},{33,2},{34,3},{35,4},{36,5},{37,6},{38,7},{39,8},{40... | collective-permute-start | bytes 49160 | tf_op jit(solution)/shard_map/ppermute | solution.py:259
  11.5 15.2 %collective-permute-start.5 = (bf16[64,128]{1,0:T(8,128)(2,1)S(1)}, bf16[64,128]{1,0:T(8,128)(2,1)S(1)}, u32[]{:S(2)}, u32[]{:S(2)}) collective-permute-start(bf16[64,128]{1,0:T(8,128)(2,1)S(1)} %slice.23), channel_id=1, source_target_pairs={{33,0},{34,1},{35,2},{36,3},{37,4},{38,5},{39,6},{40,7},{41,8},{42... | collective-permute-start | bytes 49160 | tf_op jit(solution)/shard_map/ppermute | solution.py:259
  44.3 21.7 %all-to-all-start.1 = ((f32[16,24,128]{2,1,0:T(8,128)}), f32[16,24,128]{2,1,0:T(8,128)S(1)}, u32[]{:S(2)}, u32[]{:S(2)}) async-start(f32[16,24,128]{2,1,0:T(8,128)} %broadcast_in_dim.7), calls=%async_computation.1 | async-start | bytes 393216 | tf_op jit(solution)/shard_map/all_to_all | solution.py:237
  66.7 11.5 %all-to-all-start.2 = ((f32[16,24,128]{2,1,0:T(8,128)}), f32[16,24,128]{2,1,0:T(8,128)S(1)}, u32[]{:S(2)}, u32[]{:S(2)}) async-start(f32[16,24,128]{2,1,0:T(8,128)} %broadcast_in_dim.8), calls=%async_computation.2 | async-start | bytes 393216 | tf_op jit(solution)/shard_map/all_to_all | solution.py:237

commit v3 on v2

--- a/solution.py
+++ b/solution.py
@@ -19,6 +19,7 @@
 BF16 = jnp.bfloat16
 ROWS = 8
 GAP = 32
+HEAD = 12
 VMEM_LIMIT = 16 * 1024 * 1024
 
 
@@ -129,7 +130,18 @@
                 slope_ref[f, h] = slope
 
 
-def grads_kernel(f, c0_ref, c1_ref, c2_ref, act_ref, slope_ref, x3_ref, w_ref, base_ref, d_ref, sum_ref, d_scr):
+def grads_kernel(f, *refs):
+    if f == 0:
+        c0_ref, c1_ref, later_ref, act_ref, slope_ref, x3_ref, w_ref, d_ref, sum_ref, d_scr = refs
+    else:
+        c0_ref, c1_ref, later_ref, rest_ref, act_ref, slope_ref, x3_ref, w_ref, base_ref, d_ref, sum_ref, d_scr = refs
+
+    def cotangent(frame, h):
+        if frame < 2:
+            return (c0_ref, c1_ref)[frame][h]
+        at = (frame - 2) * rows + h
+        return later_ref[at] if at < rows + HEAD else rest_ref[at - rows - HEAD]
+
     rows, chans, cols = d_ref.shape
     weight = w_ref[...]
     d_scr[0] = jnp.zeros((chans, cols), BF16)
@@ -138,7 +150,7 @@
     for g in range(rows // ROWS):
         hs = range(g * ROWS, (g + 1) * ROWS)
         cot = jnp.concatenate(
-            [jnp.concatenate([ref[h] for h in hs], axis=1) for ref in (c0_ref, c1_ref, c2_ref)], axis=0
+            [jnp.concatenate([cotangent(f + k, h) for h in hs], axis=1) for k in range(3)], axis=0
         )
         up = jnp.dot(weight, cot, preferred_element_type=F32)
         for r, h in enumerate(hs):
@@ -165,14 +177,12 @@
         sum_ref[1] = base_ref[1] + both[:, half:]
 
 
-def back_kernel(d0_ref, d1_ref, near_left_ref, near_right_ref, far_left_ref, far_right_ref, slope_ref, w_up_ref, w_ref,
-                out0_ref, out1_ref, z_ref):
+def back_kernel(d0_ref, d1_ref, near_ref, far_ref, slope_ref, w_up_ref, w_ref, out0_ref, out1_ref, z_ref):
     rows, chans, cols = d0_ref.shape
     weight = w_ref[...]
     lane = lax.broadcasted_iota(jnp.int32, (chans, cols), 1)
-    left_half = lane < cols // 2
-    near = jnp.where(left_half, near_left_ref[...].astype(F32), near_right_ref[...].astype(F32))
-    far = jnp.where(left_half, far_left_ref[...].astype(F32), far_right_ref[...].astype(F32))
+    near = near_ref[...].astype(F32)
+    far = far_ref[rows - HEAD].astype(F32)
     mixed = jnp.where(lane % (2 * GAP) < GAP, pltpu.roll(near, cols - GAP, 1), pltpu.roll(far, GAP, 1))
     cot = jnp.concatenate([near, mixed, far], axis=0).astype(BF16)
     up = jnp.dot(w_up_ref[...], cot, preferred_element_type=F32)
@@ -267,14 +277,15 @@
     edges = shape((3 * chans, cols), BF16)
     sums = shape((2, 3 * chans, 2 * chans), F32)
     cot = [jnp.transpose(cotangent[:, f], (1, 0, 2)) for f in range(nf)]
-    cot[0], cot[1], frames = lax.optimization_barrier((cot[0], cot[1], frames))
-    cot += [shifted(c, 1, 0) for c in cot]
+    head = jnp.concatenate([cot[0], cot[1][:HEAD]], axis=0)
+    head, frames = lax.optimization_barrier((head, frames))
+    later = shifted(head, 1, 0)
 
     field = jnp.transpose(frames, (1, 2, 0, 3))
     to_right, to_left, own = call(edge_kernel, (field, cot[0], cot[1]), (edges, edges, edge), [], 10_000_000)
     from_left, from_right = shifted(to_right, 0, -1), shifted(to_left, 0, 1)
-    far_left = shifted(to_right[2 * chans :], 1, -1)
-    far_right = shifted(to_left[2 * chans :], 1, 1)
+    near = from_left[2 * chans :] + from_right[2 * chans :]
+    rest = shifted(jnp.concatenate([cot[1][HEAD:], near[None]], axis=0), 1, 0)
     w_fwd = jnp.transpose(w_space, (0, 2, 1, 3)).reshape(3 * chans, 3 * chans)
     w_bwd = jnp.transpose(w_space, (0, 3, 1, 2)).reshape(3 * chans, 3 * chans)
     w_up = jnp.transpose(w_time, (2, 0, 1)).reshape(chans, 3 * chans)
@@ -290,22 +301,20 @@
         [pltpu.VMEM((rows + 2, 3 * chans, cols), F32)],
         10_000_000,
     )
-    total = jnp.zeros((1, 8, 128), F32)
     dpre = []
     for f in range(nf):
         d, total = call(
             functools.partial(grads_kernel, f),
-            (cot[f], cot[f + 1], cot[f + 2], act, slope, x3, w_up, total),
+            (cot[0], cot[1], later, rest, act, slope, x3, w_up, total) if f else (cot[0], cot[1], later, act, slope, x3, w_up),
             (shape(slabs, BF16), sums),
             [pltpu.VMEM((rows + 2, chans, cols), BF16)],
             4_000_000_000,
         )
         dpre.append(d)
-    total, far_left, far_right = lax.optimization_barrier((total, far_left, far_right))
-    near = (from_left[2 * chans :], from_right[2 * chans :])
+    total, near, w_bwd = lax.optimization_barrier((total, near, w_bwd))
     out = call(
         back_kernel,
-        (dpre[0], dpre[1], *near, far_left, far_right, edge_slope, w_up, w_bwd),
+        (dpre[0], dpre[1], near, rest, edge_slope, w_up, w_bwd),
         (shape(slabs, BF16), shape(slabs, BF16)),
         [pltpu.VMEM((rows + 2, 3 * chans, cols), F32)],
         4_000_000_000,

time: 79.6 us -> 77.2 us (0.970)
  blocking collectives: 16.9 us -> 37.9 us
  starting transfers between devices: 23.4 us -> 9.5 us
  waiting for transfers between devices: 21.5 us -> 12 us
  other arithmetic: 0.12 us -> 1.01 us
    all_to_all x1 -> x2, blocking collectives: 16.9 us -> 37.9 us  [exchange(): return lax.all_to_all(cells, axes, 0, 0, tiled=True)]
    all_to_all x2 -> x1, starting transfers between devices: 14.9 us -> 3.52 us  [exchange(): return lax.all_to_all(cells, axes, 0, 0, tiled=True)]
    all_to_all x2 -> x1, waiting for transfers between devices: 13.6 us -> 3.67 us  [exchange(): return lax.all_to_all(cells, axes, 0, 0, tiled=True)]
    ppermute x6 -> x4, starting transfers between devices: 8.56 us -> 5.98 us  [shifted(): return lax.ppermute(cells, TM + LON, pairs)]
    concatenate x0 -> x2, other arithmetic: none -> 0.89 us  [the longest x1 0.87 us: body(): head = jnp.concatenate([cot[0], cot[1][:HEAD]], axis=0)]
    ppermute x6 -> x4, waiting for transfers between devices: 7.81 us -> 8.36 us  [shifted(): return lax.ppermute(cells, TM + LON, pairs)]
  transfers between devices with their start and end apart: 8 -> 5, of which waited for: 4 -> 5; matrix products, arithmetic and copies ran while one was open for 3% -> 3% of each run, Pallas kernels for 13% -> 12%
where the time goes in v3:
time: 77.2 us; the launch traced here: 76.9 us
  blocking collectives  37.9 us (49%)
  waiting for transfers between devices  12 us (16%)
  Pallas kernels  11.2 us (15%)
  starting transfers between devices  9.5 us (12%)
  local copies, waits for them, and re-layouts  4.52 us (6%)
  other arithmetic  1.01 us (1%)
  between operations  0.8 us (1%)
    all_to_all x2, blocking collectives, exchange(): return lax.all_to_all(cells, axes, 0, 0, tiled=True)  37.9 us
    pallas_call x6, Pallas kernels, call(): pl.pallas_call(kernel, out_shape=outs, in_specs=in_vmem(len(args)), out_s...  11.2 us
    ppermute x4, waiting for transfers between devices, shifted(): return lax.ppermute(cells, TM + LON, pairs)  8.36 us
    ppermute x4, starting transfers between devices, shifted(): return lax.ppermute(cells, TM + LON, pairs)  5.98 us
    all_to_all x1, waiting for transfers between devices, exchange(): return lax.all_to_all(cells, axes, 0, 0, tiled=True)  3.67 us
    all_to_all x1, starting transfers between devices, exchange(): return lax.all_to_all(cells, axes, 0, 0, tiled=True)  3.52 us
  transfers between devices with their start and end apart: 5, of which 5 were waited for; matrix products, arithmetic and copies ran while one was open for 3% of the time, Pallas kernels for 12%

profile of v3, /device:TPU:1, one launch (start us, length us, event | category | flops | bytes accessed | tf_op | source)
XLA Modules:
  0.0 76.9 jit_solution(11218001071188744390)
XLA Ops:
  0.6 0.0 copy-start
  0.6 1.3 %fusion = (bf16[64,1,24,128]{3,2,1,0:T(8,128)(2,1)S(1)}, bf16[64,1,24,128]{3,2,1,0:T(8,128)(2,1)S(1)}) fusion(bf16[64,2,24,128]{3,2,1,0:T(8,128)(2,1)} %param.5), kind=kLoop, calls=%fused_computation.7 | loop fusion | bytes 1572864 | tf_op jit(solution)/shard_map/slice | solution.py:279
  1.9 0.2 copy_bitcast_fusion.1
  2.1 0.0 copy-start.1
  2.2 0.0 copy-start.2
  2.2 0.9 %pad_maximum_fusion.1 = bf16[36,64,128]{2,1,0:T(8,128)(2,1)} fusion(bf16[12,64,128]{2,1,0:T(8,128)(2,1)S(1)} %get-tuple-element.55, bf16[24,64,128]{2,1,0:T(8,128)(2,1)S(1)} %get-tuple-element.57.c0_ref.refs_0_), kind=kLoop, calls=%fused_computation.2 | loop fusion | flops 294912 | bytes 1179648 | tf_op jit(solution)/shard_map/concatenate | solution.py:280
  3.0 1.3 %collective-permute-start = (bf16[36,64,128]{2,1,0:T(8,128)(2,1)}, bf16[36,64,128]{2,1,0:T(8,128)(2,1)S(1)}, u32[]{:S(2)}, u32[]{:S(2)}) collective-permute-start(bf16[36,64,128]{2,1,0:T(8,128)(2,1)} %pad_maximum_fusion.1), channel_id=1, source_target_pairs={{32,0},{33,1},{34,2},{35,3},{36,4},{37,5},{38,6},{39,7},{40,8},{41... | collective-permute-start | bytes 1769480 | tf_op jit(solution)/shard_map/ppermute | solution.py:269
  4.3 0.0 copy-done
  4.3 0.2 copy.37
  4.6 1.4 %shard_map.67 = (bf16[192,128]{1,0:T(8,128)(2,1)S(1)}, bf16[192,128]{1,0:T(8,128)(2,1)S(1)}, bf16[64,128]{1,0:T(8,128)(2,1)S(1)}) custom-call(bf16[2,24,64,128]{3,2,1,0:T(8,128)(2,1)S(1)} %bitcast.25, bf16[24,64,128]{2,1,0:T(8,128)(2,1)S(1)} %get-tuple-element.57.c0_ref.refs_0_, bf16[24,64,128]{2,1,0:T(8,128)(2,1)S(1)} %get-tuple-element.56.c1_ref.refs_1_), custom_call_target="tpu_custom_call" | custom-call | flops 10000000 | bytes 10000 | tf_op jit(solution)/shard_map/pallas_call | solution.py:235
  6.0 3.1 %collective-permute-start.1 = (bf16[192,128]{1,0:T(8,128)(2,1)S(1)}, bf16[192,128]{1,0:T(8,128)(2,1)S(1)}, u32[]{:S(2)}, u32[]{:S(2)}) collective-permute-start(bf16[192,128]{1,0:T(8,128)(2,1)S(1)} %get-tuple-element.25), channel_id=1, source_target_pairs={{31,0},{0,1},{1,2},{2,3},{3,4},{4,5},{5,6},{6,7},{7,8},{8,9},{9,10... | collective-permute-start | bytes 147464 | tf_op jit(solution)/shard_map/ppermute | solution.py:269
  9.1 0.3 collective-permute-start.2
  9.4 0.0 copy-done.1
  9.4 0.1 copy.26
  9.5 0.2 reshape.17.w_ref
  9.7 0.0 copy-done.2
  9.7 0.1 copy.27.refs_6_.refs_7_.w_up_ref
  9.8 0.2 copy.29
  10.0 0.2 reshape.19.w_ref
  10.1 0.1 collective-permute-done.1.from_left_ref
  10.3 2.3 %collective-permute-done.2.from_right_ref = bf16[192,128]{1,0:T(8,128)(2,1)S(1)} collective-permute-done((bf16[192,128]{1,0:T(8,128)(2,1)S(1)}, bf16[192,128]{1,0:T(8,128)(2,1)S(1)}, u32[]{:S(2)}, u32[]{:S(2)}) %collective-permute-start.2) | collective-permute-done | bytes 49184 | tf_op jit(solution)/shard_map/ppermute | solution.py:269
  12.6 1.3 %collective-permute-start.3 = (bf16[13,64,128]{2,1,0:T(8,128)(2,1)S(1)}, bf16[13,64,128]{2,1,0:T(8,128)(2,1)S(1)}, u32[]{:S(2)}, u32[]{:S(2)}) collective-permute-start(bf16[13,64,128]{2,1,0:T(8,128)(2,1)S(1)} %pad_maximum_fusion.2), channel_id=1, source_target_pairs={{32,0},{33,1},{34,2},{35,3},{36,4},{37,5},{38,6},{39,7},{40,8},{41... | collective-permute-start | bytes 638984 | tf_op jit(solution)/shard_map/ppermute | solution.py:269
  13.9 3.4 %shard_map.68 = (bf16[2,24,192,128]{3,2,1,0:T(8,128)(2,1)S(1)}, bf16[2,24,64,128]{3,2,1,0:T(8,128)(2,1)S(1)}, f32[2,24,64,128]{3,2,1,0:T(8,128)S(1)}, f32[64,128]{1,0:T(8,128)S(1)}) custom-call(bf16[2,24,64,128]{3,2,1,0:T(8,128)(2,1)S(1)} %bitcast.26, bf16[192,128]{1,0:T(8,128)(2,1)S(1)} %collective-permute-done.1.from_left_ref, ...), custom_call_target="tpu_custom_call" | custom-call | flops 10000000 | bytes 10000 | tf_op jit(solution)/shard_map/pallas_call | solution.py:235
  17.3 2.6 %collective-permute-done.refs_2_ = bf16[36,64,128]{2,1,0:T(8,128)(2,1)S(1)} collective-permute-done((bf16[36,64,128]{2,1,0:T(8,128)(2,1)}, bf16[36,64,128]{2,1,0:T(8,128)(2,1)S(1)}, u32[]{:S(2)}, u32[]{:S(2)}) %collective-permute-start) | collective-permute-done | bytes 589856 | tf_op jit(solution)/shard_map/ppermute | solution.py:269
  20.0 1.3 %shard_map.69 = (bf16[24,64,128]{2,1,0:T(8,128)(2,1)S(1)}, f32[2,192,128]{2,1,0:T(8,128)S(1)}) custom-call(bf16[24,64,128]{2,1,0:T(8,128)(2,1)S(1)} %get-tuple-element.57.c0_ref.refs_0_, bf16[24,64,128]{2,1,0:T(8,128)(2,1)S(1)} %get-tuple-element.56.c1_ref.refs_1_, bf16[36,64,128]{2,1,0:T(8,128)(2,1)S(1)} %collective-permute-done.refs_2_, ...), custom_call_target="tpu_custom_call" | custom-call | flops 4000000000 | bytes 4000000 | tf_op jit(solution)/shard_map/pallas_call | solution.py:235
  21.3 3.3 %collective-permute-done.3.refs_3_.far_ref = bf16[13,64,128]{2,1,0:T(8,128)(2,1)S(1)} collective-permute-done((bf16[13,64,128]{2,1,0:T(8,128)(2,1)S(1)}, bf16[13,64,128]{2,1,0:T(8,128)(2,1)S(1)}, u32[]{:S(2)}, u32[]{:S(2)}) %collective-permute-start.3) | collective-permute-done | bytes 213024 | tf_op jit(solution)/shard_map/ppermute | solution.py:269
  24.5 1.3 %shard_map.70 = (bf16[24,64,128]{2,1,0:T(8,128)(2,1)S(1)}, f32[2,192,128]{2,1,0:T(8,128)S(1)}) custom-call(bf16[24,64,128]{2,1,0:T(8,128)(2,1)S(1)} %get-tuple-element.57.c0_ref.refs_0_, bf16[24,64,128]{2,1,0:T(8,128)(2,1)S(1)} %get-tuple-element.56.c1_ref.refs_1_, bf16[36,64,128]{2,1,0:T(8,128)(2,1)S(1)} %collective-permute-done.refs_2_, ...), custom_call_target="tpu_custom_call" | custom-call | flops 4000000000 | bytes 4000000 | tf_op jit(solution)/shard_map/pallas_call | solution.py:235
  25.8 16.9 %all_to_all.15 = f32[16,24,128]{2,1,0:T(8,128)S(1)} all-to-all(f32[16,24,128]{2,1,0:T(8,128)S(1)} %bitcast.30), channel_id=1, replica_groups=mesh['y'=4,'xh'=2,'xl'=2,'z'=8,'c'=2] {'y','xh','xl'}, dimensions={0} | all-to-all | bytes 393216 | tf_op jit(solution)/shard_map/all_to_all | solution.py:247
  42.8 21.0 %all_to_all.16 = f32[16,24,128]{2,1,0:T(8,128)S(1)} all-to-all(f32[16,24,128]{2,1,0:T(8,128)S(1)} %broadcast_in_dim.7), channel_id=1, replica_groups=mesh['y'=4,'xh'=2,'xl'=2,'z'=8,'c'=2] {'z','c'}, dimensions={0} | all-to-all | bytes 393216 | tf_op jit(solution)/shard_map/all_to_all | solution.py:247
  63.8 0.7 broadcast_in_dim.8
  64.5 3.5 %all-to-all-start.2 = ((f32[16,24,128]{2,1,0:T(8,128)}), f32[16,24,128]{2,1,0:T(8,128)S(1)}, u32[]{:S(2)}, u32[]{:S(2)}) async-start(f32[16,24,128]{2,1,0:T(8,128)} %broadcast_in_dim.8), calls=%async_computation.2 | async-start | bytes 393216 | tf_op jit(solution)/shard_map/all_to_all | solution.py:247
  68.0 2.9 %shard_map.71 = (bf16[24,64,128]{2,1,0:T(8,128)(2,1)S(1)}, bf16[24,64,128]{2,1,0:T(8,128)(2,1)S(1)}) custom-call(bf16[24,64,128]{2,1,0:T(8,128)(2,1)S(1)} %get-tuple-element.31.d0_ref, bf16[24,64,128]{2,1,0:T(8,128)(2,1)S(1)} %get-tuple-element.33.d1_ref, bf16[64,128]{1,0:T(8,128)(2,1)S(1)} %slice_add_fusion.near_ref, ...), custom_call_target="tpu_custom_call" | custom-call | flops 4000000000 | bytes 4000000 | tf_op jit(solution)/shard_map/pallas_call | solution.py:235
  70.9 0.1 pad_maximum_fusion
  71.0 1.4 %copy.31 = bf16[64,2,24,128]{3,2,1,0:T(8,128)(2,1)} copy(bf16[64,2,24,128]{3,0,2,1:T(8,128)(2,1)S(1)} %pad_maximum_fusion) | data formatting | bytes 1572864
  72.4 3.7 %all-to-all-done.2 = f32[16,24,128]{2,1,0:T(8,128)S(1)} async-done(((f32[16,24,128]{2,1,0:T(8,128)}), f32[16,24,128]{2,1,0:T(8,128)S(1)}, u32[]{:S(2)}, u32[]{:S(2)}) %all-to-all-start.2) | async-done | bytes 196640 | tf_op jit(solution)/shard_map/all_to_all | solution.py:247
  76.1 0.8 %shard_map.72 = (f32[3,3,64,64]{3,2,1,0:T(8,128)}, f32[3,64,64]{2,1,0:T(8,128)}) custom-call(f32[2,192,128]{2,1,0:T(8,128)S(1)} %bitcast.27), custom_call_target="tpu_custom_call" | custom-call | flops 1000000 | bytes 1000 | tf_op jit(solution)/shard_map/pallas_call | solution.py:235
  (6 shorter events, 0.1 us)
Async XLA Ops:
  0.6 3.7 %copy-start = (bf16[64,2,24,128]{3,2,1,0:T(8,128)(2,1)S(1)}, bf16[64,2,24,128]{3,2,1,0:T(8,128)(2,1)}, u32[]{:S(2)}) copy-start(bf16[64,2,24,128]{3,2,1,0:T(8,128)(2,1)} %param.4) | copy-start | bytes 2359300
  2.1 7.2 %copy-start.1 = (bf16[3,3,64,64]{3,2,1,0:T(8,128)(2,1)S(1)}, bf16[3,3,64,64]{3,2,1,0:T(8,128)(2,1)}, u32[]{:S(2)}) copy-start(bf16[3,3,64,64]{3,2,1,0:T(8,128)(2,1)} %param.6) | copy-start | bytes 221188
  2.2 7.5 %copy-start.2 = (bf16[3,64,64]{2,1,0:T(8,128)(2,1)S(1)}, bf16[3,64,64]{2,1,0:T(8,128)(2,1)}, u32[]{:S(2)}) copy-start(bf16[3,64,64]{2,1,0:T(8,128)(2,1)} %param.7) | copy-start | bytes 73732
  3.0 16.9 %collective-permute-start = (bf16[36,64,128]{2,1,0:T(8,128)(2,1)}, bf16[36,64,128]{2,1,0:T(8,128)(2,1)S(1)}, u32[]{:S(2)}, u32[]{:S(2)}) collective-permute-start(bf16[36,64,128]{2,1,0:T(8,128)(2,1)} %pad_maximum_fusion.1), channel_id=1, source_target_pairs={{32,0},{33,1},{34,2},{35,3},{36,4},{37,5},{38,6},{39,7},{40,8},{41... | collective-permute-start | bytes 1769480 | tf_op jit(solution)/shard_map/ppermute | solution.py:269
  6.0 4.3 %collective-permute-start.1 = (bf16[192,128]{1,0:T(8,128)(2,1)S(1)}, bf16[192,128]{1,0:T(8,128)(2,1)S(1)}, u32[]{:S(2)}, u32[]{:S(2)}) collective-permute-start(bf16[192,128]{1,0:T(8,128)(2,1)S(1)} %get-tuple-element.25), channel_id=1, source_target_pairs={{31,0},{0,1},{1,2},{2,3},{3,4},{4,5},{5,6},{6,7},{7,8},{8,9},{9,10... | collective-permute-start | bytes 147464 | tf_op jit(solution)/shard_map/ppermute | solution.py:269
  9.1 3.5 %collective-permute-start.2 = (bf16[192,128]{1,0:T(8,128)(2,1)S(1)}, bf16[192,128]{1,0:T(8,128)(2,1)S(1)}, u32[]{:S(2)}, u32[]{:S(2)}) collective-permute-start(bf16[192,128]{1,0:T(8,128)(2,1)S(1)} %get-tuple-element.26), channel_id=1, source_target_pairs={{1,0},{2,1},{3,2},{4,3},{5,4},{6,5},{7,6},{8,7},{9,8},{10,9},{11,1... | collective-permute-start | bytes 147464 | tf_op jit(solution)/shard_map/ppermute | solution.py:269
  12.6 11.9 %collective-permute-start.3 = (bf16[13,64,128]{2,1,0:T(8,128)(2,1)S(1)}, bf16[13,64,128]{2,1,0:T(8,128)(2,1)S(1)}, u32[]{:S(2)}, u32[]{:S(2)}) collective-permute-start(bf16[13,64,128]{2,1,0:T(8,128)(2,1)S(1)} %pad_maximum_fusion.2), channel_id=1, source_target_pairs={{32,0},{33,1},{34,2},{35,3},{36,4},{37,5},{38,6},{39,7},{40,8},{41... | collective-permute-start | bytes 638984 | tf_op jit(solution)/shard_map/ppermute | solution.py:269
  64.5 11.5 %all-to-all-start.2 = ((f32[16,24,128]{2,1,0:T(8,128)}), f32[16,24,128]{2,1,0:T(8,128)S(1)}, u32[]{:S(2)}, u32[]{:S(2)}) async-start(f32[16,24,128]{2,1,0:T(8,128)} %broadcast_in_dim.8), calls=%async_computation.2 | async-start | bytes 393216 | tf_op jit(solution)/shard_map/all_to_all | solution.py:247

commit v4 on v2

--- a/solution.py
+++ b/solution.py
@@ -6,6 +6,7 @@
 import numpy as np
 from jax import lax
 from jax.experimental import pallas as pl
+from jax.experimental.layout import Layout, with_layout_constraint
 from jax.experimental.pallas import tpu as pltpu
 from jax.sharding import Mesh
 from jax.sharding import PartitionSpec as P
@@ -14,7 +15,6 @@
 TM = ("y", "xh")
 LON = ("xl", "z", "c")
 PLANE = ("y", "xh", "xl")
-LINE = ("z", "c")
 F32 = jnp.float32
 BF16 = jnp.bfloat16
 ROWS = 8
@@ -39,13 +39,13 @@
     return before.astype(BF16), slab, after.astype(BF16)
 
 
-def edge_kernel(x_ref, c0_ref, c1_ref, right_ref, left_ref, own_ref):
+def edge_kernel(x_ref, c_ref, right_ref, left_ref, own_ref):
     frames, rows, chans, cols = x_ref.shape
     lane = lax.broadcasted_iota(jnp.int32, (chans, cols), 1)
     sums = (jnp.zeros((chans, cols), F32),) * 6
-    for f, c_ref in enumerate((c0_ref, c1_ref)):
-
-        def step(g, sums, f=f, c_ref=c_ref):
+    for f in range(frames):
+
+        def step(g, sums, f=f):
             for r in range(ROWS):
                 h = g * ROWS + r
                 at = lane_of(f, h)
@@ -53,7 +53,7 @@
                 wide = x_ref[f, h].astype(F32)
                 low = pltpu.roll(wide, at, 1)
                 high = pltpu.roll(wide, at + 2, 1)
-                cot = c_ref[h].astype(F32)
+                cot = c_ref[f * rows + h].astype(F32)
                 vals = (low, low, high, high, pltpu.roll(cot, at, 1), pltpu.roll(cot, at + 1, 1))
                 masks = (here, beside, here, beside, here, here)
                 sums = tuple(jnp.where(m, v, s) for m, v, s in zip(masks, vals, sums))
@@ -129,50 +129,49 @@
                 slope_ref[f, h] = slope
 
 
-def grads_kernel(f, c0_ref, c1_ref, c2_ref, act_ref, slope_ref, x3_ref, w_ref, base_ref, d_ref, sum_ref, d_scr):
-    rows, chans, cols = d_ref.shape
+def grads_kernel(c_ref, later_ref, act_ref, slope_ref, x3_ref, w_ref, d_ref, sum_ref, d_scr):
+    frames, rows, chans, cols = d_ref.shape
     weight = w_ref[...]
-    d_scr[0] = jnp.zeros((chans, cols), BF16)
-    d_scr[rows + 1] = jnp.zeros((chans, cols), BF16)
     t_sum = jnp.zeros((3 * chans, chans), F32)
-    for g in range(rows // ROWS):
-        hs = range(g * ROWS, (g + 1) * ROWS)
-        cot = jnp.concatenate(
-            [jnp.concatenate([ref[h] for h in hs], axis=1) for ref in (c0_ref, c1_ref, c2_ref)], axis=0
-        )
-        up = jnp.dot(weight, cot, preferred_element_type=F32)
-        for r, h in enumerate(hs):
-            d = (up[:, r * cols : (r + 1) * cols] * slope_ref[f, h]).astype(BF16)
-            d_ref[h] = d
-            d_scr[h + 1] = d
-        act = jnp.concatenate([act_ref[f, h] for h in hs], axis=1)
-        t_sum = t_sum + dot_nt(cot, act)
     g_sum = jnp.zeros((3 * chans, 3 * chans), F32)
-    for g in range(rows // ROWS):
-        hs = range(g * ROWS, (g + 1) * ROWS)
-        d3 = jnp.concatenate(
-            [jnp.concatenate([d_scr[h - i + 2] for h in hs], axis=1) for i in range(3)], axis=0
-        )
-        x3 = jnp.concatenate([x3_ref[f, h] for h in hs], axis=1)
-        g_sum = g_sum + dot_nt(d3, x3)
+    for f in range(frames):
+        d_scr[f, 0] = jnp.zeros((chans, cols), BF16)
+        d_scr[f, rows + 1] = jnp.zeros((chans, cols), BF16)
+        for g in range(rows // ROWS):
+            hs = range(g * ROWS, (g + 1) * ROWS)
+            cot = jnp.concatenate(
+                [
+                    jnp.concatenate([ref[at * rows + h] for h in hs], axis=1)
+                    for ref, at in ((c_ref, f + k) if f + k < frames else (later_ref, f + k - frames) for k in range(3))
+                ],
+                axis=0,
+            )
+            up = jnp.dot(weight, cot, preferred_element_type=F32)
+            for r, h in enumerate(hs):
+                d = (up[:, r * cols : (r + 1) * cols] * slope_ref[f, h]).astype(BF16)
+                d_ref[f, h] = d
+                d_scr[f, h + 1] = d
+            act = jnp.concatenate([act_ref[f, h] for h in hs], axis=1)
+            t_sum = t_sum + dot_nt(cot, act)
+        for g in range(rows // ROWS):
+            hs = range(g * ROWS, (g + 1) * ROWS)
+            d3 = jnp.concatenate(
+                [jnp.concatenate([d_scr[f, h - i + 2] for h in hs], axis=1) for i in range(3)], axis=0
+            )
+            x3 = jnp.concatenate([x3_ref[f, h] for h in hs], axis=1)
+            g_sum = g_sum + dot_nt(d3, x3)
     both = jnp.concatenate([g_sum, t_sum], axis=1)
     half = both.shape[1] // 2
-    if f == 0:
-        sum_ref[0] = both[:, :half]
-        sum_ref[1] = both[:, half:]
-    else:
-        sum_ref[0] = base_ref[0] + both[:, :half]
-        sum_ref[1] = base_ref[1] + both[:, half:]
-
-
-def back_kernel(d0_ref, d1_ref, near_left_ref, near_right_ref, far_left_ref, far_right_ref, slope_ref, w_up_ref, w_ref,
-                out0_ref, out1_ref, z_ref):
-    rows, chans, cols = d0_ref.shape
+    sum_ref[0] = both[:, :half]
+    sum_ref[1] = both[:, half:]
+
+
+def back_kernel(d_ref, near_ref, far_ref, slope_ref, w_up_ref, w_ref, out_ref, z_ref):
+    frames, rows, chans, cols = d_ref.shape
     weight = w_ref[...]
     lane = lax.broadcasted_iota(jnp.int32, (chans, cols), 1)
-    left_half = lane < cols // 2
-    near = jnp.where(left_half, near_left_ref[...].astype(F32), near_right_ref[...].astype(F32))
-    far = jnp.where(left_half, far_left_ref[...].astype(F32), far_right_ref[...].astype(F32))
+    near = near_ref[...].astype(F32)
+    far = far_ref[...].astype(F32)
     mixed = jnp.where(lane % (2 * GAP) < GAP, pltpu.roll(near, cols - GAP, 1), pltpu.roll(far, GAP, 1))
     cot = jnp.concatenate([near, mixed, far], axis=0).astype(BF16)
     up = jnp.dot(w_up_ref[...], cot, preferred_element_type=F32)
@@ -180,14 +179,14 @@
     zero = jnp.zeros((3 * chans, cols), F32)
     z_ref[0] = zero
     z_ref[rows + 1] = zero
-    for f, (d_ref, out_ref) in enumerate(((d0_ref, out0_ref), (d1_ref, out1_ref))):
+    for f in range(frames):
 
         @pl.loop(0, rows // ROWS)
         def _(g):
             wide = []
             for r in range(ROWS):
                 h = g * ROWS + r
-                before, same, after = lane_taps(d_ref[h], edge, lane_of(f, h))
+                before, same, after = lane_taps(d_ref[f, h], edge, lane_of(f, h))
                 wide.append(jnp.concatenate([after, same, before], axis=0))
             z = jnp.dot(weight, jnp.concatenate(wide, axis=1), preferred_element_type=F32)
             for r in range(ROWS):
@@ -202,7 +201,7 @@
                     + z_ref[h + 1, chans : 2 * chans]
                     + z_ref[h, 2 * chans : 3 * chans]
                 )
-                out_ref[h] = out.astype(BF16)
+                out_ref[f, h] = out.astype(BF16)
 
 
 def finish_kernel(scale, sum_ref, space_ref, time_ref):
@@ -242,18 +241,21 @@
     return exchange(jnp.broadcast_to(cells[None], (count,) + cells.shape), axes)
 
 
-def sum_over_all(cells):
+def sum_over_all(cells, beside):
     count = lax.axis_size(PLANE)
-    parts = exchange(cells.reshape(count, -1, cells.shape[-1]), PLANE).sum(0)
-    parts = spread(parts, LINE).sum(0)
-    return spread(parts, PLANE).reshape(cells.shape)
+    parts = exchange(cells.reshape(count, -1, cells.shape[-1]), PLANE)
+    parts, beside = lax.optimization_barrier((parts, beside))
+    parts = parts.sum(0)
+    parts = parts + lax.ppermute(parts, "c", [(0, 1), (1, 0)])
+    parts = spread(parts, "z").sum(0)
+    return spread(parts, PLANE).reshape(cells.shape), beside
 
 
 def shifted(cells, tm_step, lon_step):
     blocks, sectors = lax.axis_size(TM), lax.axis_size(LON)
     pairs = [
-        ((t + tm_step) * sectors + (s + lon_step) % sectors, t * sectors + s)
-        for t in range(blocks - tm_step)
+        ((t + tm_step) % blocks * sectors + (s + lon_step) % sectors, t * sectors + s)
+        for t in range(blocks)
         for s in range(sectors)
     ]
     return lax.ppermute(cells, TM + LON, pairs)
@@ -266,15 +268,14 @@
     edge = shape((chans, cols), BF16)
     edges = shape((3 * chans, cols), BF16)
     sums = shape((2, 3 * chans, 2 * chans), F32)
-    cot = [jnp.transpose(cotangent[:, f], (1, 0, 2)) for f in range(nf)]
-    cot[0], cot[1], frames = lax.optimization_barrier((cot[0], cot[1], frames))
-    cot += [shifted(c, 1, 0) for c in cot]
-
-    field = jnp.transpose(frames, (1, 2, 0, 3))
-    to_right, to_left, own = call(edge_kernel, (field, cot[0], cot[1]), (edges, edges, edge), [], 10_000_000)
+    by_row = lambda field: jnp.transpose(field, (1, 2, 0, 3)).reshape(nf * rows, chans, cols)
+    keep = (lax.axis_index(TM) < lax.axis_size(TM) - 1).astype(BF16)
+    later = by_row(shifted(cotangent, 1, 0)) * keep
+    cot, field = by_row(cotangent), jnp.transpose(frames, (1, 2, 0, 3))
+    to_right, to_left, own = call(edge_kernel, (field, cot), (edges, edges, edge), [], 10_000_000)
     from_left, from_right = shifted(to_right, 0, -1), shifted(to_left, 0, 1)
-    far_left = shifted(to_right[2 * chans :], 1, -1)
-    far_right = shifted(to_left[2 * chans :], 1, 1)
+    near = from_left[2 * chans :] + from_right[2 * chans :]
+    far = shifted(near, 1, 0) * keep
     w_fwd = jnp.transpose(w_space, (0, 2, 1, 3)).reshape(3 * chans, 3 * chans)
     w_bwd = jnp.transpose(w_space, (0, 3, 1, 2)).reshape(3 * chans, 3 * chans)
     w_up = jnp.transpose(w_time, (2, 0, 1)).reshape(chans, 3 * chans)
@@ -290,29 +291,25 @@
         [pltpu.VMEM((rows + 2, 3 * chans, cols), F32)],
         10_000_000,
     )
-    total = jnp.zeros((1, 8, 128), F32)
-    dpre = []
-    for f in range(nf):
-        d, total = call(
-            functools.partial(grads_kernel, f),
-            (cot[f], cot[f + 1], cot[f + 2], act, slope, x3, w_up, total),
-            (shape(slabs, BF16), sums),
-            [pltpu.VMEM((rows + 2, chans, cols), BF16)],
-            4_000_000_000,
-        )
-        dpre.append(d)
-    total, far_left, far_right = lax.optimization_barrier((total, far_left, far_right))
-    near = (from_left[2 * chans :], from_right[2 * chans :])
-    out = call(
+    dpre, total = call(
+        grads_kernel,
+        (cot, later, act, slope, x3, w_up),
+        (shape((nf,) + slabs, BF16), sums),
+        [pltpu.VMEM((nf, rows + 2, chans, cols), BF16)],
+        4_000_000_000,
+    )
+    total, near, far, w_bwd = lax.optimization_barrier((total, near, far, w_bwd))
+    (out,) = call(
         back_kernel,
-        (dpre[0], dpre[1], *near, far_left, far_right, edge_slope, w_up, w_bwd),
-        (shape(slabs, BF16), shape(slabs, BF16)),
+        (dpre, near, far, edge_slope, w_up, w_bwd),
+        (shape((nf,) + slabs, BF16),),
         [pltpu.VMEM((rows + 2, 3 * chans, cols), F32)],
         4_000_000_000,
     )
-    grad_frames = jnp.stack([jnp.transpose(o, (1, 0, 2)) for o in out], axis=1)
+    grad_frames = with_layout_constraint(jnp.transpose(out, (2, 0, 1, 3)), Layout(major_to_minor=(0, 1, 2, 3)))
     cells = nf * lax.axis_size(TM) * rows * cols * lax.axis_size(LON)
-    total = sum_over_all(total.reshape(-1, 2 * chans)).reshape(sums.shape)
+    total, grad_frames = sum_over_all(total.reshape(-1, 2 * chans), grad_frames)
+    total = total.reshape(sums.shape)
     grad_sp, grad_tm = call(
         functools.partial(finish_kernel, 1.0 / math.sqrt(cells)),
         (total,),

time: 79.6 us -> 72.1 us (0.906)
  waiting for transfers between devices: 21.5 us -> 9.94 us
  blocking collectives: 16.9 us -> 24.8 us
  starting transfers between devices: 23.4 us -> 19.1 us
    all_to_all x2 -> x1, waiting for transfers between devices: 13.6 us -> 2.93 us  [exchange(): return lax.all_to_all(cells, axes, 0, 0, tiled=True)]
    all_to_all x1 -> x2, blocking collectives: 16.9 us -> 24.8 us  [exchange(): return lax.all_to_all(cells, axes, 0, 0, tiled=True)]
    all_to_all x2 -> x1, starting transfers between devices: 14.9 us -> 7.2 us  [exchange(): return lax.all_to_all(cells, axes, 0, 0, tiled=True)]
    ppermute x0 -> x1, starting transfers between devices: none -> 3.06 us  [sum_over_all(): parts = parts + lax.ppermute(parts, 'c', [(0, 1), (1, 0)])]
    ppermute x6 -> x4, waiting for transfers between devices: 7.81 us -> 6.17 us  [shifted(): return lax.ppermute(cells, TM + LON, pairs)]
    pallas_call x0 -> x1, local copies, waits for them, and re-layouts: none -> 1.39 us  [call(): pl.pallas_call(kernel, out_shape=outs, in_specs=in_vmem(len(args)), out_s...]
    broadcast_in_dim x2, local copies, waits for them, and re-layouts: 1.38 us -> 0.03 us  [spread(): return exchange(jnp.broadcast_to(cells[None], (count,) + cells.shape), axes)]
    slice x5 -> x0, local copies, waits for them, and re-layouts: 1.29 us -> none  [the longest x1 1.28 us: body(): cot = [jnp.transpose(cotangent[:, f], (1, 0, 2)) for f in range(nf)]]
  transfers between devices with their start and end apart: 8 -> 6, of which waited for: 4 -> 5; matrix products, arithmetic and copies ran while one was open for 3% -> 7% of each run, Pallas kernels for 13% -> 11%
where the time goes in v4:
time: 72.1 us; the launch traced here: 70.8 us
  blocking collectives  24.8 us (34%)
  starting transfers between devices  19.1 us (26%)
  Pallas kernels  11 us (15%)
  waiting for transfers between devices  9.94 us (14%)
  local copies, waits for them, and re-layouts  5.08 us (7%)
  between operations  0.73 us (1%)
    all_to_all x2, blocking collectives, exchange(): return lax.all_to_all(cells, axes, 0, 0, tiled=True)  24.8 us
    pallas_call x5, Pallas kernels, call(): pl.pallas_call(kernel, out_shape=outs, in_specs=in_vmem(len(args)), out_s...  11 us
    ppermute x4, starting transfers between devices, shifted(): return lax.ppermute(cells, TM + LON, pairs)  8.88 us
    all_to_all x1, starting transfers between devices, exchange(): return lax.all_to_all(cells, axes, 0, 0, tiled=True)  7.2 us
    ppermute x4, waiting for transfers between devices, shifted(): return lax.ppermute(cells, TM + LON, pairs)  6.17 us
    ppermute x1, starting transfers between devices, sum_over_all(): parts = parts + lax.ppermute(parts, 'c', [(0, 1), (1, 0)])  3.06 us
    all_to_all x1, waiting for transfers between devices, exchange(): return lax.all_to_all(cells, axes, 0, 0, tiled=True)  2.93 us
  transfers between devices with their start and end apart: 6, of which 5 were waited for; matrix products, arithmetic and copies ran while one was open for 7% of the time, Pallas kernels for 11%

profile of v4, /device:TPU:1, one launch (start us, length us, event | category | flops | bytes accessed | tf_op | source)
XLA Modules:
  0.0 70.8 jit_solution(13815140195796939456)
XLA Ops:
  0.6 6.1 %collective-permute-start = (bf16[64,2,24,128]{3,2,1,0:T(8,128)(2,1)}, bf16[64,2,24,128]{3,2,1,0:T(8,128)(2,1)S(1)}, u32[]{:S(2)}, u32[]{:S(2)}) collective-permute-start(bf16[64,2,24,128]{3,2,1,0:T(8,128)(2,1)} %param.5), channel_id=1, source_target_pairs={{32,0},{33,1},{34,2},{35,3},{36,4},{37,5},{38,6},{39,7},{40,8},{41... | collective-permute-start | bytes 2359304 | tf_op jit(solution)/shard_map/ppermute | solution.py:261
  6.7 0.0 copy-start
  6.7 0.0 copy-start.1
  6.7 1.4 %copy.22 = bf16[2,24,64,128]{3,2,1,0:T(8,128)(2,1)S(1)} copy(bf16[2,24,64,128]{3,1,0,2:T(8,128)(2,1)} %bitcast.24) | data formatting | bytes 1572864 | tf_op jit(solution)/shard_map/transpose | solution.py:271
  8.1 1.3 %copy.33 = bf16[64,2,24,128]{3,0,2,1:T(8,128)(2,1)S(1)} copy(bf16[64,2,24,128]{3,2,1,0:T(8,128)(2,1)} %param.4) | data formatting | bytes 1572864 | tf_op args[0]
  9.5 1.4 %shard_map.67 = (bf16[192,128]{1,0:T(8,128)(2,1)S(1)}, bf16[192,128]{1,0:T(8,128)(2,1)S(1)}, bf16[64,128]{1,0:T(8,128)(2,1)S(1)}) custom-call(bf16[2,24,64,128]{3,2,1,0:T(8,128)(2,1)S(1)} %bitcast.18, bf16[48,64,128]{2,1,0:T(8,128)(2,1)S(1)} %bitcast.20), custom_call_target="tpu_custom_call" | custom-call | flops 10000000 | bytes 10000 | tf_op jit(solution)/shard_map/pallas_call | solution.py:224
  10.9 2.5 %collective-permute-start.1 = (bf16[192,128]{1,0:T(8,128)(2,1)S(1)}, bf16[192,128]{1,0:T(8,128)(2,1)S(1)}, u32[]{:S(2)}, u32[]{:S(2)}) collective-permute-start(bf16[192,128]{1,0:T(8,128)(2,1)S(1)} %get-tuple-element.20), channel_id=1, source_target_pairs={{31,0},{0,1},{1,2},{2,3},{3,4},{4,5},{5,6},{6,7},{7,8},{8,9},{9,10... | collective-permute-start | bytes 147464 | tf_op jit(solution)/shard_map/ppermute | solution.py:261
  13.5 0.0 collective-permute-start.2
  13.5 1.2 %collective-permute-done.1.from_left_ref = bf16[192,128]{1,0:T(8,128)(2,1)S(1)} collective-permute-done((bf16[192,128]{1,0:T(8,128)(2,1)S(1)}, bf16[192,128]{1,0:T(8,128)(2,1)S(1)}, u32[]{:S(2)}, u32[]{:S(2)}) %collective-permute-start.1) | collective-permute-done | bytes 49184 | tf_op jit(solution)/shard_map/ppermute | solution.py:261
  14.7 2.6 %collective-permute-done.2.from_right_ref = bf16[192,128]{1,0:T(8,128)(2,1)S(1)} collective-permute-done((bf16[192,128]{1,0:T(8,128)(2,1)S(1)}, bf16[192,128]{1,0:T(8,128)(2,1)S(1)}, u32[]{:S(2)}, u32[]{:S(2)}) %collective-permute-start.2) | collective-permute-done | bytes 49184 | tf_op jit(solution)/shard_map/ppermute | solution.py:261
  17.3 0.2 collective-permute-start.3
  17.5 0.0 copy-done
  17.5 0.1 copy.25
  17.6 0.2 reshape.24.w_ref
  17.8 0.0 copy-done.1
  17.8 0.1 copy.26.w_ref.w_up_ref
  17.9 0.2 copy.27
  18.1 0.2 reshape.26.w_ref
  18.3 3.4 %shard_map.68 = (bf16[2,24,192,128]{3,2,1,0:T(8,128)(2,1)S(1)}, bf16[2,24,64,128]{3,2,1,0:T(8,128)(2,1)S(1)}, f32[2,24,64,128]{3,2,1,0:T(8,128)S(1)}, f32[64,128]{1,0:T(8,128)S(1)}) custom-call(bf16[2,24,64,128]{3,2,1,0:T(8,128)(2,1)S(1)} %bitcast.19, bf16[192,128]{1,0:T(8,128)(2,1)S(1)} %collective-permute-done.1.from_left_ref, ...), custom_call_target="tpu_custom_call" | custom-call | flops 10000000 | bytes 10000 | tf_op jit(solution)/shard_map/pallas_call | solution.py:224
  21.7 2.4 %collective-permute-done.3 = bf16[64,128]{1,0:T(8,128)(2,1)S(1)} collective-permute-done((bf16[64,128]{1,0:T(8,128)(2,1)S(1)}, bf16[64,128]{1,0:T(8,128)(2,1)S(1)}, u32[]{:S(2)}, u32[]{:S(2)}) %collective-permute-start.3) | collective-permute-done | bytes 16416 | tf_op jit(solution)/shard_map/ppermute | solution.py:261
  24.0 0.0 collective-permute-done
  24.0 0.1 multiply_bitcast_fusion
  24.1 0.2 copy.23
  24.3 2.5 %shard_map.69 = (bf16[2,24,64,128]{3,2,1,0:T(8,128)(2,1)S(1)}, f32[2,192,128]{2,1,0:T(8,128)}) custom-call(bf16[48,64,128]{2,1,0:T(8,128)(2,1)S(1)} %bitcast.21, bf16[48,64,128]{2,1,0:T(8,128)(2,1)S(1)} %bitcast.22, bf16[2,24,64,128]{3,2,1,0:T(8,128)(2,1)S(1)} %get-tuple-element.23.act_ref, f32[2,24,64,128]{3,2,1,0:T(8,128)S(1)} %get-tuple-element.24.slope_ref, ...), custom_call_target="tpu_custom_call" | custom-call | flops 4000000000 | bytes 4000000 | tf_op jit(solution)/shard_map/pallas_call | solution.py:224
  26.8 7.2 %all-to-all-start = ((f32[16,24,128]{2,1,0:T(8,128)}), f32[16,24,128]{2,1,0:T(8,128)S(1)}, u32[]{:S(2)}, u32[]{:S(2)}) async-start(f32[16,24,128]{2,1,0:T(8,128)} %bitcast.9), calls=%async_computation | async-start | bytes 393216 | tf_op jit(solution)/shard_map/all_to_all | solution.py:236
  34.0 2.9 %shard_map.70 = bf16[2,24,64,128]{3,2,1,0:T(8,128)(2,1)S(1)} custom-call(bf16[2,24,64,128]{3,2,1,0:T(8,128)(2,1)S(1)} %get-tuple-element.28.d_ref, bf16[64,128]{1,0:T(8,128)(2,1)S(1)} %slice_add_fusion.near_ref, bf16[64,128]{1,0:T(8,128)(2,1)S(1)} %broadcast_multiply_fusion.far_ref, f32[64,128]{1,0:T(8,128)S(1)} %get-tuple-element.31.slope_ref, ...), custom_call_target="tpu_custom_call" | custom-call | flops 4000000000 | bytes 4000000 | tf_op jit(solution)/shard_map/pallas_call | solution.py:224
  36.9 1.4 %copy.32 = bf16[2,24,64,128]{3,1,0,2:T(8,128)(2,1)} copy(bf16[2,24,64,128]{3,2,1,0:T(8,128)(2,1)S(1)} %shard_map.70) | data formatting | bytes 1572864 | tf_op jit(solution)/shard_map/pallas_call | solution.py:224
  38.3 2.9 %all-to-all-done = f32[16,24,128]{2,1,0:T(8,128)S(1)} async-done(((f32[16,24,128]{2,1,0:T(8,128)}), f32[16,24,128]{2,1,0:T(8,128)S(1)}, u32[]{:S(2)}, u32[]{:S(2)}) %all-to-all-start) | async-done | bytes 196640 | tf_op jit(solution)/shard_map/all_to_all | solution.py:236
  41.2 3.1 %collective-permute-start.4 = (f32[24,128]{1,0:T(8,128)S(1)}, f32[24,128]{1,0:T(8,128)S(1)}, u32[]{:S(2)}, u32[]{:S(2)}) collective-permute-start(f32[24,128]{1,0:T(8,128)S(1)} %reduce_sum.18), channel_id=1, source_target_pairs={{0,1},{1,0},{2,3},{3,2},{4,5},{5,4},{6,7},{7,6},{8,9},{9,8},{10,11... | collective-permute-start | bytes 36872 | tf_op jit(solution)/shard_map/ppermute | solution.py:249
  44.3 0.8 %collective-permute-done.4 = f32[24,128]{1,0:T(8,128)S(1)} collective-permute-done((f32[24,128]{1,0:T(8,128)S(1)}, f32[24,128]{1,0:T(8,128)S(1)}, u32[]{:S(2)}, u32[]{:S(2)}) %collective-permute-start.4) | collective-permute-done | bytes 12320 | tf_op jit(solution)/shard_map/ppermute | solution.py:249
  45.1 14.9 %all_to_all.15 = f32[8,24,128]{2,1,0:T(8,128)S(1)} all-to-all(f32[8,24,128]{2,1,0:T(8,128)S(1)} %broadcast_in_dim.4), channel_id=1, replica_groups=mesh['y'=4,'xh'=2,'xl'=2,'z'=8,'c'=2] {'z'}, dimensions={0} | all-to-all | bytes 196608 | tf_op jit(solution)/shard_map/all_to_all | solution.py:236
  60.1 9.9 %all_to_all.16 = f32[16,24,128]{2,1,0:T(8,128)S(1)} all-to-all(f32[16,24,128]{2,1,0:T(8,128)S(1)} %broadcast_in_dim.5), channel_id=1, replica_groups=mesh['y'=4,'xh'=2,'xl'=2,'z'=8,'c'=2] {'y','xh','xl'}, dimensions={0} | all-to-all | bytes 393216 | tf_op jit(solution)/shard_map/all_to_all | solution.py:236
  70.0 0.8 %shard_map.71 = (f32[3,3,64,64]{3,2,1,0:T(8,128)}, f32[3,64,64]{2,1,0:T(8,128)}) custom-call(f32[2,192,128]{2,1,0:T(8,128)S(1)} %bitcast.23), custom_call_target="tpu_custom_call" | custom-call | flops 1000000 | bytes 1000 | tf_op jit(solution)/shard_map/pallas_call | solution.py:224
  (7 shorter events, 0.1 us)
Async XLA Ops:
  0.6 23.4 %collective-permute-start = (bf16[64,2,24,128]{3,2,1,0:T(8,128)(2,1)}, bf16[64,2,24,128]{3,2,1,0:T(8,128)(2,1)S(1)}, u32[]{:S(2)}, u32[]{:S(2)}) collective-permute-start(bf16[64,2,24,128]{3,2,1,0:T(8,128)(2,1)} %param.5), channel_id=1, source_target_pairs={{32,0},{33,1},{34,2},{35,3},{36,4},{37,5},{38,6},{39,7},{40,8},{41... | collective-permute-start | bytes 2359304 | tf_op jit(solution)/shard_map/ppermute | solution.py:261
  6.7 10.8 %copy-start = (bf16[3,3,64,64]{3,2,1,0:T(8,128)(2,1)S(1)}, bf16[3,3,64,64]{3,2,1,0:T(8,128)(2,1)}, u32[]{:S(2)}) copy-start(bf16[3,3,64,64]{3,2,1,0:T(8,128)(2,1)} %param.6) | copy-start | bytes 221188
  6.7 11.1 %copy-start.1 = (bf16[3,64,64]{2,1,0:T(8,128)(2,1)S(1)}, bf16[3,64,64]{2,1,0:T(8,128)(2,1)}, u32[]{:S(2)}) copy-start(bf16[3,64,64]{2,1,0:T(8,128)(2,1)} %param.7) | copy-start | bytes 73732
  10.9 3.7 %collective-permute-start.1 = (bf16[192,128]{1,0:T(8,128)(2,1)S(1)}, bf16[192,128]{1,0:T(8,128)(2,1)S(1)}, u32[]{:S(2)}, u32[]{:S(2)}) collective-permute-start(bf16[192,128]{1,0:T(8,128)(2,1)S(1)} %get-tuple-element.20), channel_id=1, source_target_pairs={{31,0},{0,1},{1,2},{2,3},{3,4},{4,5},{5,6},{6,7},{7,8},{8,9},{9,10... | collective-permute-start | bytes 147464 | tf_op jit(solution)/shard_map/ppermute | solution.py:261
  13.5 3.8 %collective-permute-start.2 = (bf16[192,128]{1,0:T(8,128)(2,1)S(1)}, bf16[192,128]{1,0:T(8,128)(2,1)S(1)}, u32[]{:S(2)}, u32[]{:S(2)}) collective-permute-start(bf16[192,128]{1,0:T(8,128)(2,1)S(1)} %get-tuple-element.21), channel_id=1, source_target_pairs={{1,0},{2,1},{3,2},{4,3},{5,4},{6,5},{7,6},{8,7},{9,8},{10,9},{11,1... | collective-permute-start | bytes 147464 | tf_op jit(solution)/shard_map/ppermute | solution.py:261
  17.3 6.7 %collective-permute-start.3 = (bf16[64,128]{1,0:T(8,128)(2,1)S(1)}, bf16[64,128]{1,0:T(8,128)(2,1)S(1)}, u32[]{:S(2)}, u32[]{:S(2)}) collective-permute-start(bf16[64,128]{1,0:T(8,128)(2,1)S(1)} %slice_add_fusion.near_ref), channel_id=1, source_target_pairs={{32,0},{33,1},{34,2},{35,3},{36,4},{37,5},{38,6},{39,7},{40,8},{41... | collective-permute-start | bytes 49160 | tf_op jit(solution)/shard_map/ppermute | solution.py:261
  26.8 14.4 %all-to-all-start = ((f32[16,24,128]{2,1,0:T(8,128)}), f32[16,24,128]{2,1,0:T(8,128)S(1)}, u32[]{:S(2)}, u32[]{:S(2)}) async-start(f32[16,24,128]{2,1,0:T(8,128)} %bitcast.9), calls=%async_computation | async-start | bytes 393216 | tf_op jit(solution)/shard_map/all_to_all | solution.py:236
  41.2 3.9 %collective-permute-start.4 = (f32[24,128]{1,0:T(8,128)S(1)}, f32[24,128]{1,0:T(8,128)S(1)}, u32[]{:S(2)}, u32[]{:S(2)}) collective-permute-start(f32[24,128]{1,0:T(8,128)S(1)} %reduce_sum.18), channel_id=1, source_target_pairs={{0,1},{1,0},{2,3},{3,2},{4,5},{5,4},{6,7},{7,6},{8,9},{9,8},{10,11... | collective-permute-start | bytes 36872 | tf_op jit(solution)/shard_map/ppermute | solution.py:249

commit v5 on v4

--- a/solution.py
+++ b/solution.py
@@ -132,34 +132,37 @@
 def grads_kernel(c_ref, later_ref, act_ref, slope_ref, x3_ref, w_ref, d_ref, sum_ref, d_scr):
     frames, rows, chans, cols = d_ref.shape
     weight = w_ref[...]
-    t_sum = jnp.zeros((3 * chans, chans), F32)
-    g_sum = jnp.zeros((3 * chans, 3 * chans), F32)
+    wide = lambda ref, f, hs: jnp.concatenate([ref[f, h] for h in hs], axis=1)
     for f in range(frames):
         d_scr[f, 0] = jnp.zeros((chans, cols), BF16)
         d_scr[f, rows + 1] = jnp.zeros((chans, cols), BF16)
-        for g in range(rows // ROWS):
-            hs = range(g * ROWS, (g + 1) * ROWS)
-            cot = jnp.concatenate(
-                [
-                    jnp.concatenate([ref[at * rows + h] for h in hs], axis=1)
-                    for ref, at in ((c_ref, f + k) if f + k < frames else (later_ref, f + k - frames) for k in range(3))
-                ],
-                axis=0,
-            )
-            up = jnp.dot(weight, cot, preferred_element_type=F32)
+    t_sum = jnp.zeros((2 * frames * chans, frames * chans), F32)
+    for g in range(rows // ROWS):
+        hs = range(g * ROWS, (g + 1) * ROWS)
+        cot = jnp.concatenate(
+            [
+                jnp.concatenate([ref[f * rows + h] for h in hs], axis=1)
+                for ref in (c_ref, later_ref)
+                for f in range(frames)
+            ],
+            axis=0,
+        )
+        up = jnp.dot(weight, cot, preferred_element_type=F32)
+        for f in range(frames):
             for r, h in enumerate(hs):
-                d = (up[:, r * cols : (r + 1) * cols] * slope_ref[f, h]).astype(BF16)
+                d = (up[f * chans : (f + 1) * chans, r * cols : (r + 1) * cols] * slope_ref[f, h]).astype(BF16)
                 d_ref[f, h] = d
                 d_scr[f, h + 1] = d
-            act = jnp.concatenate([act_ref[f, h] for h in hs], axis=1)
-            t_sum = t_sum + dot_nt(cot, act)
+        t_sum = t_sum + dot_nt(cot, jnp.concatenate([wide(act_ref, f, hs) for f in range(frames)], axis=0))
+    g_sum = jnp.zeros((3 * chans, 3 * chans), F32)
+    for f in range(frames):
         for g in range(rows // ROWS):
             hs = range(g * ROWS, (g + 1) * ROWS)
             d3 = jnp.concatenate(
                 [jnp.concatenate([d_scr[f, h - i + 2] for h in hs], axis=1) for i in range(3)], axis=0
             )
-            x3 = jnp.concatenate([x3_ref[f, h] for h in hs], axis=1)
-            g_sum = g_sum + dot_nt(d3, x3)
+            g_sum = g_sum + dot_nt(d3, wide(x3_ref, f, hs))
+    t_sum = t_sum[: 3 * chans, :chans] + t_sum[chans:, chans:]
     both = jnp.concatenate([g_sum, t_sum], axis=1)
     half = both.shape[1] // 2
     sum_ref[0] = both[:, :half]
@@ -208,8 +211,8 @@
     taps, chans = time_ref.shape[:2]
     for i in range(taps):
         rows = slice(i * chans, (i + 1) * chans)
-        low = sum_ref[0, rows, :] * scale
-        high = sum_ref[1, rows, :] * scale
+        low = sum_ref[0, rows, :].astype(F32) * scale
+        high = sum_ref[1, rows, :].astype(F32) * scale
         space_ref[i, 0] = low[:, :chans]
         space_ref[i, 1] = low[:, chans:]
         space_ref[i, 2] = high[:, :chans]
@@ -248,7 +251,7 @@
     parts = parts.sum(0)
     parts = parts + lax.ppermute(parts, "c", [(0, 1), (1, 0)])
     parts = spread(parts, "z").sum(0)
-    return spread(parts, PLANE).reshape(cells.shape), beside
+    return spread(parts.astype(BF16), PLANE).reshape(cells.shape), beside
 
 
 def shifted(cells, tm_step, lon_step):
@@ -279,6 +282,7 @@
     w_fwd = jnp.transpose(w_space, (0, 2, 1, 3)).reshape(3 * chans, 3 * chans)
     w_bwd = jnp.transpose(w_space, (0, 3, 1, 2)).reshape(3 * chans, 3 * chans)
     w_up = jnp.transpose(w_time, (2, 0, 1)).reshape(chans, 3 * chans)
+    w_both = jnp.concatenate([jnp.pad(w_up, ((0, 0), (f * chans, (nf - 1 - f) * chans))) for f in range(nf)], axis=0)
     x3, act, slope, edge_slope = call(
         forward_kernel,
         (field, from_left, from_right, own, w_fwd),
@@ -293,7 +297,7 @@
     )
     dpre, total = call(
         grads_kernel,
-        (cot, later, act, slope, x3, w_up),
+        (cot, later, act, slope, x3, w_both),
         (shape((nf,) + slabs, BF16), sums),
         [pltpu.VMEM((nf, rows + 2, chans, cols), BF16)],
         4_000_000_000,

time: 72.1 us -> 71.2 us (0.988)
  no operation moved by 1% of the time
where the time goes in v5:
time: 71.2 us; the launch traced here: 69.9 us
  blocking collectives  24.3 us (34%)
  starting transfers between devices  19.1 us (27%)
  Pallas kernels  10.6 us (15%)
  waiting for transfers between devices  9.86 us (14%)
  local copies, waits for them, and re-layouts  5.08 us (7%)
  between operations  0.73 us (1%)
    all_to_all x2, blocking collectives, exchange(): return lax.all_to_all(cells, axes, 0, 0, tiled=True)  24.3 us
    pallas_call x5, Pallas kernels, call(): pl.pallas_call(kernel, out_shape=outs, in_specs=in_vmem(len(args)), out_s...  10.6 us
    ppermute x4, starting transfers between devices, shifted(): return lax.ppermute(cells, TM + LON, pairs)  8.88 us
    all_to_all x1, starting transfers between devices, exchange(): return lax.all_to_all(cells, axes, 0, 0, tiled=True)  7.2 us
    ppermute x4, waiting for transfers between devices, shifted(): return lax.ppermute(cells, TM + LON, pairs)  6.1 us
    ppermute x1, starting transfers between devices, sum_over_all(): parts = parts + lax.ppermute(parts, 'c', [(0, 1), (1, 0)])  3.06 us
    all_to_all x1, waiting for transfers between devices, exchange(): return lax.all_to_all(cells, axes, 0, 0, tiled=True)  2.93 us
  transfers between devices with their start and end apart: 6, of which 5 were waited for; matrix products, arithmetic and copies ran while one was open for 7% of the time, Pallas kernels for 11%

profile of v5, /device:TPU:1, one launch (start us, length us, event | category | flops | bytes accessed | tf_op | source)
XLA Modules:
  0.0 69.9 jit_solution(7935515866498948477)
XLA Ops:
  0.6 6.1 %collective-permute-start = (bf16[64,2,24,128]{3,2,1,0:T(8,128)(2,1)}, bf16[64,2,24,128]{3,2,1,0:T(8,128)(2,1)S(1)}, u32[]{:S(2)}, u32[]{:S(2)}) collective-permute-start(bf16[64,2,24,128]{3,2,1,0:T(8,128)(2,1)} %param.5), channel_id=1, source_target_pairs={{32,0},{33,1},{34,2},{35,3},{36,4},{37,5},{38,6},{39,7},{40,8},{41... | collective-permute-start | bytes 2359304 | tf_op jit(solution)/shard_map/ppermute | solution.py:264
  6.7 0.0 copy-start.1
  6.7 0.0 copy-start
  6.7 1.4 %copy.23 = bf16[2,24,64,128]{3,2,1,0:T(8,128)(2,1)S(1)} copy(bf16[2,24,64,128]{3,1,0,2:T(8,128)(2,1)} %bitcast.24) | data formatting | bytes 1572864 | tf_op jit(solution)/shard_map/transpose | solution.py:274
  8.1 1.3 %copy.35 = bf16[64,2,24,128]{3,0,2,1:T(8,128)(2,1)S(1)} copy(bf16[64,2,24,128]{3,2,1,0:T(8,128)(2,1)} %param.4) | data formatting | bytes 1572864 | tf_op args[0]
  9.5 1.4 %shard_map.67 = (bf16[192,128]{1,0:T(8,128)(2,1)S(1)}, bf16[192,128]{1,0:T(8,128)(2,1)S(1)}, bf16[64,128]{1,0:T(8,128)(2,1)S(1)}) custom-call(bf16[2,24,64,128]{3,2,1,0:T(8,128)(2,1)S(1)} %bitcast.18, bf16[48,64,128]{2,1,0:T(8,128)(2,1)S(1)} %bitcast.20), custom_call_target="tpu_custom_call" | custom-call | flops 10000000 | bytes 10000 | tf_op jit(solution)/shard_map/pallas_call | solution.py:227
  10.9 2.5 %collective-permute-start.1 = (bf16[192,128]{1,0:T(8,128)(2,1)S(1)}, bf16[192,128]{1,0:T(8,128)(2,1)S(1)}, u32[]{:S(2)}, u32[]{:S(2)}) collective-permute-start(bf16[192,128]{1,0:T(8,128)(2,1)S(1)} %get-tuple-element.20), channel_id=1, source_target_pairs={{31,0},{0,1},{1,2},{2,3},{3,4},{4,5},{5,6},{6,7},{7,8},{8,9},{9,10... | collective-permute-start | bytes 147464 | tf_op jit(solution)/shard_map/ppermute | solution.py:264
  13.5 0.0 collective-permute-start.2
  13.5 0.0 copy-done.1
  13.5 0.1 copy.27.w_up_ref
  13.6 1.1 %collective-permute-done.1.from_left_ref = bf16[192,128]{1,0:T(8,128)(2,1)S(1)} collective-permute-done((bf16[192,128]{1,0:T(8,128)(2,1)S(1)}, bf16[192,128]{1,0:T(8,128)(2,1)S(1)}, u32[]{:S(2)}, u32[]{:S(2)}) %collective-permute-start.1) | collective-permute-done | bytes 49184 | tf_op jit(solution)/shard_map/ppermute | solution.py:264
  14.7 2.6 %collective-permute-done.2.from_right_ref = bf16[192,128]{1,0:T(8,128)(2,1)S(1)} collective-permute-done((bf16[192,128]{1,0:T(8,128)(2,1)S(1)}, bf16[192,128]{1,0:T(8,128)(2,1)S(1)}, u32[]{:S(2)}, u32[]{:S(2)}) %collective-permute-start.2) | collective-permute-done | bytes 49184 | tf_op jit(solution)/shard_map/ppermute | solution.py:264
  17.3 0.2 collective-permute-start.3
  17.5 0.1 fusion.2.w_ref
  17.6 0.0 copy-done
  17.6 0.1 copy.26
  17.7 0.2 reshape.26.w_ref
  17.9 0.2 copy.29
  18.1 0.2 reshape.28.w_ref
  18.2 3.4 %shard_map.68 = (bf16[2,24,192,128]{3,2,1,0:T(8,128)(2,1)S(1)}, bf16[2,24,64,128]{3,2,1,0:T(8,128)(2,1)S(1)}, f32[2,24,64,128]{3,2,1,0:T(8,128)S(1)}, f32[64,128]{1,0:T(8,128)S(1)}) custom-call(bf16[2,24,64,128]{3,2,1,0:T(8,128)(2,1)S(1)} %bitcast.19, bf16[192,128]{1,0:T(8,128)(2,1)S(1)} %collective-permute-done.1.from_left_ref, ...), custom_call_target="tpu_custom_call" | custom-call | flops 10000000 | bytes 10000 | tf_op jit(solution)/shard_map/pallas_call | solution.py:227
  21.6 2.4 %collective-permute-done.3 = bf16[64,128]{1,0:T(8,128)(2,1)S(1)} collective-permute-done((bf16[64,128]{1,0:T(8,128)(2,1)S(1)}, bf16[64,128]{1,0:T(8,128)(2,1)S(1)}, u32[]{:S(2)}, u32[]{:S(2)}) %collective-permute-start.3) | collective-permute-done | bytes 16416 | tf_op jit(solution)/shard_map/ppermute | solution.py:264
  24.0 0.0 collective-permute-done
  24.0 0.1 multiply_bitcast_fusion
  24.1 0.2 copy.24
  24.3 2.1 %shard_map.69 = (bf16[2,24,64,128]{3,2,1,0:T(8,128)(2,1)S(1)}, f32[2,192,128]{2,1,0:T(8,128)}) custom-call(bf16[48,64,128]{2,1,0:T(8,128)(2,1)S(1)} %bitcast.21, bf16[48,64,128]{2,1,0:T(8,128)(2,1)S(1)} %bitcast.22, bf16[2,24,64,128]{3,2,1,0:T(8,128)(2,1)S(1)} %get-tuple-element.23.act_ref, f32[2,24,64,128]{3,2,1,0:T(8,128)S(1)} %get-tuple-element.24.slope_ref, ...), custom_call_target="tpu_custom_call" | custom-call | flops 4000000000 | bytes 4000000 | tf_op jit(solution)/shard_map/pallas_call | solution.py:227
  26.4 7.2 %all-to-all-start = ((f32[16,24,128]{2,1,0:T(8,128)}), f32[16,24,128]{2,1,0:T(8,128)S(1)}, u32[]{:S(2)}, u32[]{:S(2)}) async-start(f32[16,24,128]{2,1,0:T(8,128)} %bitcast.9), calls=%async_computation | async-start | bytes 393216 | tf_op jit(solution)/shard_map/all_to_all | solution.py:239
  33.6 2.9 %shard_map.70 = bf16[2,24,64,128]{3,2,1,0:T(8,128)(2,1)S(1)} custom-call(bf16[2,24,64,128]{3,2,1,0:T(8,128)(2,1)S(1)} %get-tuple-element.28.d_ref, bf16[64,128]{1,0:T(8,128)(2,1)S(1)} %slice_add_fusion.near_ref, bf16[64,128]{1,0:T(8,128)(2,1)S(1)} %broadcast_multiply_fusion.far_ref, f32[64,128]{1,0:T(8,128)S(1)} %get-tuple-element.31.slope_ref, ...), custom_call_target="tpu_custom_call" | custom-call | flops 4000000000 | bytes 4000000 | tf_op jit(solution)/shard_map/pallas_call | solution.py:227
  36.5 1.4 %copy.34 = bf16[2,24,64,128]{3,1,0,2:T(8,128)(2,1)} copy(bf16[2,24,64,128]{3,2,1,0:T(8,128)(2,1)S(1)} %shard_map.70) | data formatting | bytes 1572864 | tf_op jit(solution)/shard_map/pallas_call | solution.py:227
  37.9 2.9 %all-to-all-done = f32[16,24,128]{2,1,0:T(8,128)S(1)} async-done(((f32[16,24,128]{2,1,0:T(8,128)}), f32[16,24,128]{2,1,0:T(8,128)S(1)}, u32[]{:S(2)}, u32[]{:S(2)}) %all-to-all-start) | async-done | bytes 196640 | tf_op jit(solution)/shard_map/all_to_all | solution.py:239
  40.8 3.1 %collective-permute-start.4 = (f32[24,128]{1,0:T(8,128)S(1)}, f32[24,128]{1,0:T(8,128)S(1)}, u32[]{:S(2)}, u32[]{:S(2)}) collective-permute-start(f32[24,128]{1,0:T(8,128)S(1)} %reduce_sum.18), channel_id=1, source_target_pairs={{0,1},{1,0},{2,3},{3,2},{4,5},{5,4},{6,7},{7,6},{8,9},{9,8},{10,11... | collective-permute-start | bytes 36872 | tf_op jit(solution)/shard_map/ppermute | solution.py:252
  43.9 0.8 %collective-permute-done.4 = f32[24,128]{1,0:T(8,128)S(1)} collective-permute-done((f32[24,128]{1,0:T(8,128)S(1)}, f32[24,128]{1,0:T(8,128)S(1)}, u32[]{:S(2)}, u32[]{:S(2)}) %collective-permute-start.4) | collective-permute-done | bytes 12320 | tf_op jit(solution)/shard_map/ppermute | solution.py:252
  44.7 14.9 %all_to_all.15 = f32[8,24,128]{2,1,0:T(8,128)S(1)} all-to-all(f32[8,24,128]{2,1,0:T(8,128)S(1)} %broadcast_in_dim.4), channel_id=1, replica_groups=mesh['y'=4,'xh'=2,'xl'=2,'z'=8,'c'=2] {'z'}, dimensions={0} | all-to-all | bytes 196608 | tf_op jit(solution)/shard_map/all_to_all | solution.py:239
  59.7 9.4 %all_to_all.16 = bf16[16,24,128]{2,1,0:T(8,128)(2,1)S(1)} all-to-all(bf16[16,24,128]{2,1,0:T(8,128)(2,1)S(1)} %broadcast_in_dim.5), channel_id=1, replica_groups=mesh['y'=4,'xh'=2,'xl'=2,'z'=8,'c'=2] {'y','xh','xl'}, dimensions={0} | all-to-all | bytes 196608 | tf_op jit(solution)/shard_map/all_to_all | solution.py:239
  69.1 0.8 %shard_map.71 = (f32[3,3,64,64]{3,2,1,0:T(8,128)}, f32[3,64,64]{2,1,0:T(8,128)}) custom-call(bf16[2,192,128]{2,1,0:T(8,128)(2,1)S(1)} %bitcast.23), custom_call_target="tpu_custom_call" | custom-call | flops 1000000 | bytes 1000 | tf_op jit(solution)/shard_map/pallas_call | solution.py:227
  (7 shorter events, 0.1 us)
Async XLA Ops:
  0.6 23.4 %collective-permute-start = (bf16[64,2,24,128]{3,2,1,0:T(8,128)(2,1)}, bf16[64,2,24,128]{3,2,1,0:T(8,128)(2,1)S(1)}, u32[]{:S(2)}, u32[]{:S(2)}) collective-permute-start(bf16[64,2,24,128]{3,2,1,0:T(8,128)(2,1)} %param.5), channel_id=1, source_target_pairs={{32,0},{33,1},{34,2},{35,3},{36,4},{37,5},{38,6},{39,7},{40,8},{41... | collective-permute-start | bytes 2359304 | tf_op jit(solution)/shard_map/ppermute | solution.py:264
  6.7 6.7 %copy-start.1 = (bf16[3,64,64]{2,1,0:T(8,128)(2,1)S(1)}, bf16[3,64,64]{2,1,0:T(8,128)(2,1)}, u32[]{:S(2)}) copy-start(bf16[3,64,64]{2,1,0:T(8,128)(2,1)} %param.7) | copy-start | bytes 73732
  6.7 10.9 %copy-start = (bf16[3,3,64,64]{3,2,1,0:T(8,128)(2,1)S(1)}, bf16[3,3,64,64]{3,2,1,0:T(8,128)(2,1)}, u32[]{:S(2)}) copy-start(bf16[3,3,64,64]{3,2,1,0:T(8,128)(2,1)} %param.6) | copy-start | bytes 221188
  10.9 3.7 %collective-permute-start.1 = (bf16[192,128]{1,0:T(8,128)(2,1)S(1)}, bf16[192,128]{1,0:T(8,128)(2,1)S(1)}, u32[]{:S(2)}, u32[]{:S(2)}) collective-permute-start(bf16[192,128]{1,0:T(8,128)(2,1)S(1)} %get-tuple-element.20), channel_id=1, source_target_pairs={{31,0},{0,1},{1,2},{2,3},{3,4},{4,5},{5,6},{6,7},{7,8},{8,9},{9,10... | collective-permute-start | bytes 147464 | tf_op jit(solution)/shard_map/ppermute | solution.py:264
  13.5 3.8 %collective-permute-start.2 = (bf16[192,128]{1,0:T(8,128)(2,1)S(1)}, bf16[192,128]{1,0:T(8,128)(2,1)S(1)}, u32[]{:S(2)}, u32[]{:S(2)}) collective-permute-start(bf16[192,128]{1,0:T(8,128)(2,1)S(1)} %get-tuple-element.21), channel_id=1, source_target_pairs={{1,0},{2,1},{3,2},{4,3},{5,4},{6,5},{7,6},{8,7},{9,8},{10,9},{11,1... | collective-permute-start | bytes 147464 | tf_op jit(solution)/shard_map/ppermute | solution.py:264
  17.3 6.7 %collective-permute-start.3 = (bf16[64,128]{1,0:T(8,128)(2,1)S(1)}, bf16[64,128]{1,0:T(8,128)(2,1)S(1)}, u32[]{:S(2)}, u32[]{:S(2)}) collective-permute-start(bf16[64,128]{1,0:T(8,128)(2,1)S(1)} %slice_add_fusion.near_ref), channel_id=1, source_target_pairs={{32,0},{33,1},{34,2},{35,3},{36,4},{37,5},{38,6},{39,7},{40,8},{41... | collective-permute-start | bytes 49160 | tf_op jit(solution)/shard_map/ppermute | solution.py:264
  26.4 14.4 %all-to-all-start = ((f32[16,24,128]{2,1,0:T(8,128)}), f32[16,24,128]{2,1,0:T(8,128)S(1)}, u32[]{:S(2)}, u32[]{:S(2)}) async-start(f32[16,24,128]{2,1,0:T(8,128)} %bitcast.9), calls=%async_computation | async-start | bytes 393216 | tf_op jit(solution)/shard_map/all_to_all | solution.py:239
  40.8 3.9 %collective-permute-start.4 = (f32[24,128]{1,0:T(8,128)S(1)}, f32[24,128]{1,0:T(8,128)S(1)}, u32[]{:S(2)}, u32[]{:S(2)}) collective-permute-start(f32[24,128]{1,0:T(8,128)S(1)} %reduce_sum.18), channel_id=1, source_target_pairs={{0,1},{1,0},{2,3},{3,2},{4,5},{5,4},{6,7},{7,6},{8,9},{9,8},{10,11... | collective-permute-start | bytes 36872 | tf_op jit(solution)/shard_map/ppermute | solution.py:252

commit v6 on v5

--- a/solution.py
+++ b/solution.py
@@ -34,7 +34,7 @@
     width = slab.shape[1]
     lane = lax.broadcasted_iota(jnp.int32, slab.shape, 1)
     wide = slab.astype(F32)
-    before = jnp.where(lane == 0, pltpu.roll(edge, width - at, 1), pltpu.roll(wide, 1, 1))
+    before = jnp.where(lane == 0, pltpu.roll(edge, lax.rem(width - at, width), 1), pltpu.roll(wide, 1, 1))
     after = jnp.where(lane == width - 1, pltpu.roll(edge, width // 2 - 1 - at, 1), pltpu.roll(wide, width - 1, 1))
     return before.astype(BF16), slab, after.astype(BF16)
 

time: 71.2 us -> 71.2 us (level)
  no operation moved by 1% of the time
where the time goes in v6:
time: 71.2 us; the launch traced here: 69.9 us
  blocking collectives  24.3 us (34%)
  starting transfers between devices  19.1 us (27%)
  Pallas kernels  10.7 us (15%)
  waiting for transfers between devices  9.83 us (14%)
  local copies, waits for them, and re-layouts  5.08 us (7%)
  between operations  0.73 us (1%)
    all_to_all x2, blocking collectives, exchange(): return lax.all_to_all(cells, axes, 0, 0, tiled=True)  24.3 us
    pallas_call x5, Pallas kernels, call(): pl.pallas_call(kernel, out_shape=outs, in_specs=in_vmem(len(args)), out_s...  10.7 us
    ppermute x4, starting transfers between devices, shifted(): return lax.ppermute(cells, TM + LON, pairs)  8.88 us
    all_to_all x1, starting transfers between devices, exchange(): return lax.all_to_all(cells, axes, 0, 0, tiled=True)  7.2 us
    ppermute x4, waiting for transfers between devices, shifted(): return lax.ppermute(cells, TM + LON, pairs)  6.06 us
    ppermute x1, starting transfers between devices, sum_over_all(): parts = parts + lax.ppermute(parts, 'c', [(0, 1), (1, 0)])  3.06 us
    all_to_all x1, waiting for transfers between devices, exchange(): return lax.all_to_all(cells, axes, 0, 0, tiled=True)  2.93 us
  transfers between devices with their start and end apart: 6, of which 5 were waited for; matrix products, arithmetic and copies ran while one was open for 7% of the time, Pallas kernels for 11%

profile of v6, /device:TPU:1, one launch (start us, length us, event | category | flops | bytes accessed | tf_op | source)
XLA Modules:
  0.0 69.9 jit_solution(17850081263090255452)
XLA Ops:
  0.6 6.1 %collective-permute-start = (bf16[64,2,24,128]{3,2,1,0:T(8,128)(2,1)}, bf16[64,2,24,128]{3,2,1,0:T(8,128)(2,1)S(1)}, u32[]{:S(2)}, u32[]{:S(2)}) collective-permute-start(bf16[64,2,24,128]{3,2,1,0:T(8,128)(2,1)} %param.5), channel_id=1, source_target_pairs={{32,0},{33,1},{34,2},{35,3},{36,4},{37,5},{38,6},{39,7},{40,8},{41... | collective-permute-start | bytes 2359304 | tf_op jit(solution)/shard_map/ppermute | solution.py:264
  6.7 0.0 copy-start.1
  6.7 0.0 copy-start
  6.7 1.4 %copy.23 = bf16[2,24,64,128]{3,2,1,0:T(8,128)(2,1)S(1)} copy(bf16[2,24,64,128]{3,1,0,2:T(8,128)(2,1)} %bitcast.24) | data formatting | bytes 1572864 | tf_op jit(solution)/shard_map/transpose | solution.py:274
  8.1 1.3 %copy.35 = bf16[64,2,24,128]{3,0,2,1:T(8,128)(2,1)S(1)} copy(bf16[64,2,24,128]{3,2,1,0:T(8,128)(2,1)} %param.4) | data formatting | bytes 1572864 | tf_op args[0]
  9.5 1.4 %shard_map.67 = (bf16[192,128]{1,0:T(8,128)(2,1)S(1)}, bf16[192,128]{1,0:T(8,128)(2,1)S(1)}, bf16[64,128]{1,0:T(8,128)(2,1)S(1)}) custom-call(bf16[2,24,64,128]{3,2,1,0:T(8,128)(2,1)S(1)} %bitcast.18, bf16[48,64,128]{2,1,0:T(8,128)(2,1)S(1)} %bitcast.20), custom_call_target="tpu_custom_call" | custom-call | flops 10000000 | bytes 10000 | tf_op jit(solution)/shard_map/pallas_call | solution.py:227
  10.9 2.5 %collective-permute-start.1 = (bf16[192,128]{1,0:T(8,128)(2,1)S(1)}, bf16[192,128]{1,0:T(8,128)(2,1)S(1)}, u32[]{:S(2)}, u32[]{:S(2)}) collective-permute-start(bf16[192,128]{1,0:T(8,128)(2,1)S(1)} %get-tuple-element.20), channel_id=1, source_target_pairs={{31,0},{0,1},{1,2},{2,3},{3,4},{4,5},{5,6},{6,7},{7,8},{8,9},{9,10... | collective-permute-start | bytes 147464 | tf_op jit(solution)/shard_map/ppermute | solution.py:264
  13.5 0.0 collective-permute-start.2
  13.5 0.0 copy-done.1
  13.5 0.1 copy.27.w_up_ref
  13.6 1.1 %collective-permute-done.1.from_left_ref = bf16[192,128]{1,0:T(8,128)(2,1)S(1)} collective-permute-done((bf16[192,128]{1,0:T(8,128)(2,1)S(1)}, bf16[192,128]{1,0:T(8,128)(2,1)S(1)}, u32[]{:S(2)}, u32[]{:S(2)}) %collective-permute-start.1) | collective-permute-done | bytes 49184 | tf_op jit(solution)/shard_map/ppermute | solution.py:264
  14.7 2.6 %collective-permute-done.2.from_right_ref = bf16[192,128]{1,0:T(8,128)(2,1)S(1)} collective-permute-done((bf16[192,128]{1,0:T(8,128)(2,1)S(1)}, bf16[192,128]{1,0:T(8,128)(2,1)S(1)}, u32[]{:S(2)}, u32[]{:S(2)}) %collective-permute-start.2) | collective-permute-done | bytes 49184 | tf_op jit(solution)/shard_map/ppermute | solution.py:264
  17.3 0.2 collective-permute-start.3
  17.5 0.1 fusion.2.w_ref
  17.6 0.0 copy-done
  17.6 0.1 copy.26
  17.7 0.2 reshape.26.w_ref
  17.9 0.2 copy.29
  18.1 0.2 reshape.28.w_ref
  18.2 3.4 %shard_map.68 = (bf16[2,24,192,128]{3,2,1,0:T(8,128)(2,1)S(1)}, bf16[2,24,64,128]{3,2,1,0:T(8,128)(2,1)S(1)}, f32[2,24,64,128]{3,2,1,0:T(8,128)S(1)}, f32[64,128]{1,0:T(8,128)S(1)}) custom-call(bf16[2,24,64,128]{3,2,1,0:T(8,128)(2,1)S(1)} %bitcast.19, bf16[192,128]{1,0:T(8,128)(2,1)S(1)} %collective-permute-done.1.from_left_ref, ...), custom_call_target="tpu_custom_call" | custom-call | flops 10000000 | bytes 10000 | tf_op jit(solution)/shard_map/pallas_call | solution.py:227
  21.7 2.4 %collective-permute-done.3 = bf16[64,128]{1,0:T(8,128)(2,1)S(1)} collective-permute-done((bf16[64,128]{1,0:T(8,128)(2,1)S(1)}, bf16[64,128]{1,0:T(8,128)(2,1)S(1)}, u32[]{:S(2)}, u32[]{:S(2)}) %collective-permute-start.3) | collective-permute-done | bytes 16416 | tf_op jit(solution)/shard_map/ppermute | solution.py:264
  24.0 0.0 collective-permute-done
  24.0 0.1 multiply_bitcast_fusion
  24.1 0.2 copy.24
  24.3 2.1 %shard_map.69 = (bf16[2,24,64,128]{3,2,1,0:T(8,128)(2,1)S(1)}, f32[2,192,128]{2,1,0:T(8,128)}) custom-call(bf16[48,64,128]{2,1,0:T(8,128)(2,1)S(1)} %bitcast.21, bf16[48,64,128]{2,1,0:T(8,128)(2,1)S(1)} %bitcast.22, bf16[2,24,64,128]{3,2,1,0:T(8,128)(2,1)S(1)} %get-tuple-element.23.act_ref, f32[2,24,64,128]{3,2,1,0:T(8,128)S(1)} %get-tuple-element.24.slope_ref, ...), custom_call_target="tpu_custom_call" | custom-call | flops 4000000000 | bytes 4000000 | tf_op jit(solution)/shard_map/pallas_call | solution.py:227
  26.4 7.2 %all-to-all-start = ((f32[16,24,128]{2,1,0:T(8,128)}), f32[16,24,128]{2,1,0:T(8,128)S(1)}, u32[]{:S(2)}, u32[]{:S(2)}) async-start(f32[16,24,128]{2,1,0:T(8,128)} %bitcast.9), calls=%async_computation | async-start | bytes 393216 | tf_op jit(solution)/shard_map/all_to_all | solution.py:239
  33.6 2.9 %shard_map.70 = bf16[2,24,64,128]{3,2,1,0:T(8,128)(2,1)S(1)} custom-call(bf16[2,24,64,128]{3,2,1,0:T(8,128)(2,1)S(1)} %get-tuple-element.28.d_ref, bf16[64,128]{1,0:T(8,128)(2,1)S(1)} %slice_add_fusion.near_ref, bf16[64,128]{1,0:T(8,128)(2,1)S(1)} %broadcast_multiply_fusion.far_ref, f32[64,128]{1,0:T(8,128)S(1)} %get-tuple-element.31.slope_ref, ...), custom_call_target="tpu_custom_call" | custom-call | flops 4000000000 | bytes 4000000 | tf_op jit(solution)/shard_map/pallas_call | solution.py:227
  36.5 1.4 %copy.34 = bf16[2,24,64,128]{3,1,0,2:T(8,128)(2,1)} copy(bf16[2,24,64,128]{3,2,1,0:T(8,128)(2,1)S(1)} %shard_map.70) | data formatting | bytes 1572864 | tf_op jit(solution)/shard_map/pallas_call | solution.py:227
  37.9 2.9 %all-to-all-done = f32[16,24,128]{2,1,0:T(8,128)S(1)} async-done(((f32[16,24,128]{2,1,0:T(8,128)}), f32[16,24,128]{2,1,0:T(8,128)S(1)}, u32[]{:S(2)}, u32[]{:S(2)}) %all-to-all-start) | async-done | bytes 196640 | tf_op jit(solution)/shard_map/all_to_all | solution.py:239
  40.8 3.1 %collective-permute-start.4 = (f32[24,128]{1,0:T(8,128)S(1)}, f32[24,128]{1,0:T(8,128)S(1)}, u32[]{:S(2)}, u32[]{:S(2)}) collective-permute-start(f32[24,128]{1,0:T(8,128)S(1)} %reduce_sum.18), channel_id=1, source_target_pairs={{0,1},{1,0},{2,3},{3,2},{4,5},{5,4},{6,7},{7,6},{8,9},{9,8},{10,11... | collective-permute-start | bytes 36872 | tf_op jit(solution)/shard_map/ppermute | solution.py:252
  43.9 0.8 %collective-permute-done.4 = f32[24,128]{1,0:T(8,128)S(1)} collective-permute-done((f32[24,128]{1,0:T(8,128)S(1)}, f32[24,128]{1,0:T(8,128)S(1)}, u32[]{:S(2)}, u32[]{:S(2)}) %collective-permute-start.4) | collective-permute-done | bytes 12320 | tf_op jit(solution)/shard_map/ppermute | solution.py:252
  44.7 14.9 %all_to_all.15 = f32[8,24,128]{2,1,0:T(8,128)S(1)} all-to-all(f32[8,24,128]{2,1,0:T(8,128)S(1)} %broadcast_in_dim.4), channel_id=1, replica_groups=mesh['y'=4,'xh'=2,'xl'=2,'z'=8,'c'=2] {'z'}, dimensions={0} | all-to-all | bytes 196608 | tf_op jit(solution)/shard_map/all_to_all | solution.py:239
  59.7 9.4 %all_to_all.16 = bf16[16,24,128]{2,1,0:T(8,128)(2,1)S(1)} all-to-all(bf16[16,24,128]{2,1,0:T(8,128)(2,1)S(1)} %broadcast_in_dim.5), channel_id=1, replica_groups=mesh['y'=4,'xh'=2,'xl'=2,'z'=8,'c'=2] {'y','xh','xl'}, dimensions={0} | all-to-all | bytes 196608 | tf_op jit(solution)/shard_map/all_to_all | solution.py:239
  69.1 0.8 %shard_map.71 = (f32[3,3,64,64]{3,2,1,0:T(8,128)}, f32[3,64,64]{2,1,0:T(8,128)}) custom-call(bf16[2,192,128]{2,1,0:T(8,128)(2,1)S(1)} %bitcast.23), custom_call_target="tpu_custom_call" | custom-call | flops 1000000 | bytes 1000 | tf_op jit(solution)/shard_map/pallas_call | solution.py:227
  (7 shorter events, 0.1 us)
Async XLA Ops:
  0.6 23.4 %collective-permute-start = (bf16[64,2,24,128]{3,2,1,0:T(8,128)(2,1)}, bf16[64,2,24,128]{3,2,1,0:T(8,128)(2,1)S(1)}, u32[]{:S(2)}, u32[]{:S(2)}) collective-permute-start(bf16[64,2,24,128]{3,2,1,0:T(8,128)(2,1)} %param.5), channel_id=1, source_target_pairs={{32,0},{33,1},{34,2},{35,3},{36,4},{37,5},{38,6},{39,7},{40,8},{41... | collective-permute-start | bytes 2359304 | tf_op jit(solution)/shard_map/ppermute | solution.py:264
  6.7 6.7 %copy-start.1 = (bf16[3,64,64]{2,1,0:T(8,128)(2,1)S(1)}, bf16[3,64,64]{2,1,0:T(8,128)(2,1)}, u32[]{:S(2)}) copy-start(bf16[3,64,64]{2,1,0:T(8,128)(2,1)} %param.7) | copy-start | bytes 73732
  6.7 10.9 %copy-start = (bf16[3,3,64,64]{3,2,1,0:T(8,128)(2,1)S(1)}, bf16[3,3,64,64]{3,2,1,0:T(8,128)(2,1)}, u32[]{:S(2)}) copy-start(bf16[3,3,64,64]{3,2,1,0:T(8,128)(2,1)} %param.6) | copy-start | bytes 221188
  10.9 3.7 %collective-permute-start.1 = (bf16[192,128]{1,0:T(8,128)(2,1)S(1)}, bf16[192,128]{1,0:T(8,128)(2,1)S(1)}, u32[]{:S(2)}, u32[]{:S(2)}) collective-permute-start(bf16[192,128]{1,0:T(8,128)(2,1)S(1)} %get-tuple-element.20), channel_id=1, source_target_pairs={{31,0},{0,1},{1,2},{2,3},{3,4},{4,5},{5,6},{6,7},{7,8},{8,9},{9,10... | collective-permute-start | bytes 147464 | tf_op jit(solution)/shard_map/ppermute | solution.py:264
  13.5 3.8 %collective-permute-start.2 = (bf16[192,128]{1,0:T(8,128)(2,1)S(1)}, bf16[192,128]{1,0:T(8,128)(2,1)S(1)}, u32[]{:S(2)}, u32[]{:S(2)}) collective-permute-start(bf16[192,128]{1,0:T(8,128)(2,1)S(1)} %get-tuple-element.21), channel_id=1, source_target_pairs={{1,0},{2,1},{3,2},{4,3},{5,4},{6,5},{7,6},{8,7},{9,8},{10,9},{11,1... | collective-permute-start | bytes 147464 | tf_op jit(solution)/shard_map/ppermute | solution.py:264
  17.3 6.7 %collective-permute-start.3 = (bf16[64,128]{1,0:T(8,128)(2,1)S(1)}, bf16[64,128]{1,0:T(8,128)(2,1)S(1)}, u32[]{:S(2)}, u32[]{:S(2)}) collective-permute-start(bf16[64,128]{1,0:T(8,128)(2,1)S(1)} %slice_add_fusion.near_ref), channel_id=1, source_target_pairs={{32,0},{33,1},{34,2},{35,3},{36,4},{37,5},{38,6},{39,7},{40,8},{41... | collective-permute-start | bytes 49160 | tf_op jit(solution)/shard_map/ppermute | solution.py:264
  26.4 14.4 %all-to-all-start = ((f32[16,24,128]{2,1,0:T(8,128)}), f32[16,24,128]{2,1,0:T(8,128)S(1)}, u32[]{:S(2)}, u32[]{:S(2)}) async-start(f32[16,24,128]{2,1,0:T(8,128)} %bitcast.9), calls=%async_computation | async-start | bytes 393216 | tf_op jit(solution)/shard_map/all_to_all | solution.py:239
  40.8 3.9 %collective-permute-start.4 = (f32[24,128]{1,0:T(8,128)S(1)}, f32[24,128]{1,0:T(8,128)S(1)}, u32[]{:S(2)}, u32[]{:S(2)}) collective-permute-start(f32[24,128]{1,0:T(8,128)S(1)} %reduce_sum.18), channel_id=1, source_target_pairs={{0,1},{1,0},{2,3},{3,2},{4,5},{5,4},{6,7},{7,6},{8,9},{9,8},{10,11... | collective-permute-start | bytes 36872 | tf_op jit(solution)/shard_map/ppermute | solution.py:252

commit v7 on v6

--- a/solution.py
+++ b/solution.py
@@ -27,15 +27,16 @@
 
 
 def lane_of(f, h):
-    return f * GAP + h
+    return 2 * (f * GAP + h)
 
 
 def lane_taps(slab, edge, at):
     width = slab.shape[1]
     lane = lax.broadcasted_iota(jnp.int32, slab.shape, 1)
     wide = slab.astype(F32)
-    before = jnp.where(lane == 0, pltpu.roll(edge, lax.rem(width - at, width), 1), pltpu.roll(wide, 1, 1))
-    after = jnp.where(lane == width - 1, pltpu.roll(edge, width // 2 - 1 - at, 1), pltpu.roll(wide, width - 1, 1))
+    beside = pltpu.roll(edge, width - 1 - at, 1)
+    before = jnp.where(lane == 0, beside, pltpu.roll(wide, 1, 1))
+    after = jnp.where(lane == width - 1, beside, pltpu.roll(wide, width - 1, 1))
     return before.astype(BF16), slab, after.astype(BF16)
 
 
@@ -49,27 +50,23 @@
             for r in range(ROWS):
                 h = g * ROWS + r
                 at = lane_of(f, h)
-                here, beside = lane == at, lane == at + 1
+                right, left, past = (lane == at + k for k in range(3))
                 wide = x_ref[f, h].astype(F32)
                 low = pltpu.roll(wide, at, 1)
-                high = pltpu.roll(wide, at + 2, 1)
+                high = pltpu.roll(wide, at + 3, 1)
                 cot = c_ref[f * rows + h].astype(F32)
-                vals = (low, low, high, high, pltpu.roll(cot, at, 1), pltpu.roll(cot, at + 1, 1))
-                masks = (here, beside, here, beside, here, here)
+                vals = (low, low, high, high, pltpu.roll(cot, at, 1), pltpu.roll(cot, at + 2, 1))
+                masks = (right, left, left, past, right, left)
                 sums = tuple(jnp.where(m, v, s) for m, v, s in zip(masks, vals, sums))
             return sums
 
         sums = lax.fori_loop(0, rows // ROWS, step, sums)
     first, second, before_last, last, cot_first, cot_last = sums
-    half = cols // 2
-    last = pltpu.roll(last, cols - 1, 1)
-    right_ref[0:chans] = before_last.astype(BF16)
-    right_ref[chans : 2 * chans] = last.astype(BF16)
-    right_ref[2 * chans : 3 * chans] = cot_last.astype(BF16)
-    left_ref[0:chans] = pltpu.roll(first, half, 1).astype(BF16)
-    left_ref[chans : 2 * chans] = pltpu.roll(second, half - 1, 1).astype(BF16)
-    left_ref[2 * chans : 3 * chans] = pltpu.roll(cot_first, half, 1).astype(BF16)
-    own_ref[...] = (first + pltpu.roll(last, half, 1)).astype(BF16)
+    second, last = (pltpu.roll(cells, cols - 1, 1) for cells in (second, last))
+    for ref, cells in ((right_ref, (before_last, last, cot_last)), (left_ref, (first, second, cot_first))):
+        for i, part in enumerate(cells):
+            ref[i * chans : (i + 1) * chans] = part.astype(BF16)
+    own_ref[...] = (pltpu.roll(first, 1, 1) + pltpu.roll(last, cols - 1, 1)).astype(BF16)
 
 
 def silu_parts(pre):
@@ -80,10 +77,10 @@
 def forward_kernel(x_ref, from_left_ref, from_right_ref, own_ref, w_ref, x3_ref, act_ref, slope_ref, edge_slope_ref, y_ref):
     frames, rows, chans, cols = x_ref.shape
     weight = w_ref[...]
-    left_half = lax.broadcasted_iota(jnp.int32, (chans, cols), 1) < cols // 2
+    left = lax.broadcasted_iota(jnp.int32, (chans, cols), 1) % 2 == 1
     own = own_ref[...].astype(F32)
     taps = [
-        jnp.where(left_half, a.astype(F32), b.astype(F32))
+        jnp.where(left, a.astype(F32), b.astype(F32))
         for a, b in (
             (from_left_ref[0:chans], own),
             (from_left_ref[chans : 2 * chans], from_right_ref[0:chans]),
@@ -93,9 +90,9 @@
     edge = taps[1]
     ye = jnp.dot(weight, jnp.concatenate(taps, axis=0).astype(BF16), preferred_element_type=F32)
     pre = (
-        pltpu.roll(ye[0:chans], 1, 1)
+        pltpu.roll(ye[0:chans], 2, 1)
         + ye[chans : 2 * chans]
-        + pltpu.roll(ye[2 * chans : 3 * chans], cols - 1, 1)
+        + pltpu.roll(ye[2 * chans : 3 * chans], cols - 2, 1)
     )
     edge_slope_ref[...] = silu_parts(pre)[1]
     zero = jnp.zeros((3 * chans, cols), F32)
@@ -175,7 +172,7 @@
     lane = lax.broadcasted_iota(jnp.int32, (chans, cols), 1)
     near = near_ref[...].astype(F32)
     far = far_ref[...].astype(F32)
-    mixed = jnp.where(lane % (2 * GAP) < GAP, pltpu.roll(near, cols - GAP, 1), pltpu.roll(far, GAP, 1))
+    mixed = jnp.where(lane < 2 * GAP, pltpu.roll(near, cols - 2 * GAP, 1), pltpu.roll(far, 2 * GAP, 1))
     cot = jnp.concatenate([near, mixed, far], axis=0).astype(BF16)
     up = jnp.dot(w_up_ref[...], cot, preferred_element_type=F32)
     edge = (up * slope_ref[...]).astype(BF16).astype(F32)
@@ -246,11 +243,10 @@
 
 def sum_over_all(cells, beside):
     count = lax.axis_size(PLANE)
-    parts = exchange(cells.reshape(count, -1, cells.shape[-1]), PLANE)
-    parts, beside = lax.optimization_barrier((parts, beside))
+    parts = exchange(cells.reshape(count, -1, cells.shape[-1]), PLANE).sum(0)
+    parts = parts + lax.ppermute(parts, "c", [(0, 1), (1, 0)])
+    parts, beside = lax.optimization_barrier((spread(parts, "z"), beside))
     parts = parts.sum(0)
-    parts = parts + lax.ppermute(parts, "c", [(0, 1), (1, 0)])
-    parts = spread(parts, "z").sum(0)
     return spread(parts.astype(BF16), PLANE).reshape(cells.shape), beside
 
 

time: 71.2 us -> 71.2 us (level)
  Pallas kernels: 10.7 us -> 9.43 us
  waiting for transfers between devices: 9.83 us -> 10.7 us
    pallas_call x5, Pallas kernels: 10.7 us -> 9.43 us  [call(): pl.pallas_call(kernel, out_shape=outs, in_specs=in_vmem(len(args)), out_s...]
    all_to_all x2, blocking collectives: 24.3 us -> 23.6 us  [exchange(): return lax.all_to_all(cells, axes, 0, 0, tiled=True)]
  transfers between devices with their start and end apart: 6 -> 6, of which waited for: 5 -> 5; matrix products, arithmetic and copies ran while one was open for 7% -> 7% of each run, Pallas kernels for 11% -> 10%
where the time goes in v7:
time: 71.2 us; the launch traced here: 69.9 us
  blocking collectives  23.6 us (33%)
  starting transfers between devices  19.6 us (28%)
  waiting for transfers between devices  10.7 us (15%)
  Pallas kernels  9.43 us (13%)
  local copies, waits for them, and re-layouts  5.72 us (8%)
  between operations  0.73 us (1%)
    all_to_all x2, blocking collectives, exchange(): return lax.all_to_all(cells, axes, 0, 0, tiled=True)  23.6 us
    pallas_call x5, Pallas kernels, call(): pl.pallas_call(kernel, out_shape=outs, in_specs=in_vmem(len(args)), out_s...  9.43 us
    ppermute x4, starting transfers between devices, shifted(): return lax.ppermute(cells, TM + LON, pairs)  8.88 us
    all_to_all x1, starting transfers between devices, exchange(): return lax.all_to_all(cells, axes, 0, 0, tiled=True)  7.66 us
    ppermute x4, waiting for transfers between devices, shifted(): return lax.ppermute(cells, TM + LON, pairs)  6.34 us
    all_to_all x1, waiting for transfers between devices, exchange(): return lax.all_to_all(cells, axes, 0, 0, tiled=True)  3.47 us
    ppermute x1, starting transfers between devices, sum_over_all(): parts = parts + lax.ppermute(parts, 'c', [(0, 1), (1, 0)])  3.06 us
  transfers between devices with their start and end apart: 6, of which 5 were waited for; matrix products, arithmetic and copies ran while one was open for 7% of the time, Pallas kernels for 10%

profile of v7, /device:TPU:1, one launch (start us, length us, event | category | flops | bytes accessed | tf_op | source)
XLA Modules:
  0.0 69.9 jit_solution(10670614501246927217)
XLA Ops:
  0.6 6.1 %collective-permute-start = (bf16[64,2,24,128]{3,2,1,0:T(8,128)(2,1)}, bf16[64,2,24,128]{3,2,1,0:T(8,128)(2,1)S(1)}, u32[]{:S(2)}, u32[]{:S(2)}) collective-permute-start(bf16[64,2,24,128]{3,2,1,0:T(8,128)(2,1)} %param.5), channel_id=1, source_target_pairs={{32,0},{33,1},{34,2},{35,3},{36,4},{37,5},{38,6},{39,7},{40,8},{41... | collective-permute-start | bytes 2359304 | tf_op jit(solution)/shard_map/ppermute | solution.py:260
  6.7 0.0 copy-start.1
  6.7 0.0 copy-start
  6.7 1.4 %copy.14 = bf16[2,24,64,128]{3,2,1,0:T(8,128)(2,1)S(1)} copy(bf16[2,24,64,128]{3,1,0,2:T(8,128)(2,1)} %bitcast.25) | data formatting | bytes 1572864 | tf_op jit(solution)/shard_map/transpose | solution.py:270
  8.1 1.3 %copy.26 = bf16[64,2,24,128]{3,0,2,1:T(8,128)(2,1)S(1)} copy(bf16[64,2,24,128]{3,2,1,0:T(8,128)(2,1)} %param.4) | data formatting | bytes 1572864 | tf_op args[0]
  9.5 1.4 %shard_map.67 = (bf16[192,128]{1,0:T(8,128)(2,1)S(1)}, bf16[192,128]{1,0:T(8,128)(2,1)S(1)}, bf16[64,128]{1,0:T(8,128)(2,1)S(1)}) custom-call(bf16[2,24,64,128]{3,2,1,0:T(8,128)(2,1)S(1)} %bitcast.18, bf16[48,64,128]{2,1,0:T(8,128)(2,1)S(1)} %bitcast.20), custom_call_target="tpu_custom_call" | custom-call | flops 10000000 | bytes 10000 | tf_op jit(solution)/shard_map/pallas_call | solution.py:224
  10.9 2.6 %collective-permute-start.1 = (bf16[192,128]{1,0:T(8,128)(2,1)S(1)}, bf16[192,128]{1,0:T(8,128)(2,1)S(1)}, u32[]{:S(2)}, u32[]{:S(2)}) collective-permute-start(bf16[192,128]{1,0:T(8,128)(2,1)S(1)} %get-tuple-element.20), channel_id=1, source_target_pairs={{31,0},{0,1},{1,2},{2,3},{3,4},{4,5},{5,6},{6,7},{7,8},{8,9},{9,10... | collective-permute-start | bytes 147464 | tf_op jit(solution)/shard_map/ppermute | solution.py:260
  13.5 0.0 collective-permute-start.2
  13.5 0.0 copy-done.1
  13.5 0.1 copy.18.w_up_ref
  13.6 1.1 %collective-permute-done.1.from_left_ref = bf16[192,128]{1,0:T(8,128)(2,1)S(1)} collective-permute-done((bf16[192,128]{1,0:T(8,128)(2,1)S(1)}, bf16[192,128]{1,0:T(8,128)(2,1)S(1)}, u32[]{:S(2)}, u32[]{:S(2)}) %collective-permute-start.1) | collective-permute-done | bytes 49184 | tf_op jit(solution)/shard_map/ppermute | solution.py:260
  14.7 2.6 %collective-permute-done.2.from_right_ref = bf16[192,128]{1,0:T(8,128)(2,1)S(1)} collective-permute-done((bf16[192,128]{1,0:T(8,128)(2,1)S(1)}, bf16[192,128]{1,0:T(8,128)(2,1)S(1)}, u32[]{:S(2)}, u32[]{:S(2)}) %collective-permute-start.2) | collective-permute-done | bytes 49184 | tf_op jit(solution)/shard_map/ppermute | solution.py:260
  17.3 0.2 collective-permute-start.3
  17.5 0.1 fusion.2.w_ref
  17.6 0.0 copy-done
  17.6 0.1 copy.17
  17.7 0.2 reshape.26.w_ref
  17.9 0.2 copy.20
  18.1 0.2 reshape.28.w_ref
  18.3 3.1 %shard_map.68 = (bf16[2,24,192,128]{3,2,1,0:T(8,128)(2,1)S(1)}, bf16[2,24,64,128]{3,2,1,0:T(8,128)(2,1)S(1)}, f32[2,24,64,128]{3,2,1,0:T(8,128)S(1)}, f32[64,128]{1,0:T(8,128)S(1)}) custom-call(bf16[2,24,64,128]{3,2,1,0:T(8,128)(2,1)S(1)} %bitcast.19, bf16[192,128]{1,0:T(8,128)(2,1)S(1)} %collective-permute-done.1.from_left_ref, ...), custom_call_target="tpu_custom_call" | custom-call | flops 10000000 | bytes 10000 | tf_op jit(solution)/shard_map/pallas_call | solution.py:224
  21.4 2.6 %collective-permute-done.3 = bf16[64,128]{1,0:T(8,128)(2,1)S(1)} collective-permute-done((bf16[64,128]{1,0:T(8,128)(2,1)S(1)}, bf16[64,128]{1,0:T(8,128)(2,1)S(1)}, u32[]{:S(2)}, u32[]{:S(2)}) %collective-permute-start.3) | collective-permute-done | bytes 16416 | tf_op jit(solution)/shard_map/ppermute | solution.py:260
  24.0 0.0 collective-permute-done
  24.0 0.1 multiply_bitcast_fusion
  24.1 0.2 copy.15
  24.3 1.4 %shard_map.69 = (bf16[2,24,64,128]{3,2,1,0:T(8,128)(2,1)S(1)}, f32[2,192,128]{2,1,0:T(8,128)S(1)}) custom-call(bf16[48,64,128]{2,1,0:T(8,128)(2,1)S(1)} %bitcast.21, bf16[48,64,128]{2,1,0:T(8,128)(2,1)S(1)} %bitcast.22, bf16[2,24,64,128]{3,2,1,0:T(8,128)(2,1)S(1)} %get-tuple-element.23.act_ref, f32[2,24,64,128]{3,2,1,0:T(8,128)S(1)} %get-tuple-element.24.slope_ref, ...), custom_call_target="tpu_custom_call" | custom-call | flops 4000000000 | bytes 4000000 | tf_op jit(solution)/shard_map/pallas_call | solution.py:224
  25.7 14.2 %all_to_all.15 = f32[16,24,128]{2,1,0:T(8,128)S(1)} all-to-all(f32[16,24,128]{2,1,0:T(8,128)S(1)} %bitcast.24), channel_id=1, replica_groups=mesh['y'=4,'xh'=2,'xl'=2,'z'=8,'c'=2] {'y','xh','xl'}, dimensions={0} | all-to-all | bytes 393216 | tf_op jit(solution)/shard_map/all_to_all | solution.py:236
  39.9 3.1 %collective-permute-start.4 = (f32[24,128]{1,0:T(8,128)S(1)}, f32[24,128]{1,0:T(8,128)S(1)}, u32[]{:S(2)}, u32[]{:S(2)}) collective-permute-start(f32[24,128]{1,0:T(8,128)S(1)} %reduce_sum.18), channel_id=1, source_target_pairs={{0,1},{1,0},{2,3},{3,2},{4,5},{5,4},{6,7},{7,6},{8,9},{9,8},{10,11... | collective-permute-start | bytes 36872 | tf_op jit(solution)/shard_map/ppermute | solution.py:247
  43.0 0.8 %collective-permute-done.4 = f32[24,128]{1,0:T(8,128)S(1)} collective-permute-done((f32[24,128]{1,0:T(8,128)S(1)}, f32[24,128]{1,0:T(8,128)S(1)}, u32[]{:S(2)}, u32[]{:S(2)}) %collective-permute-start.4) | collective-permute-done | bytes 12320 | tf_op jit(solution)/shard_map/ppermute | solution.py:247
  43.8 0.7 broadcast_in_dim.4
  44.5 7.7 %all-to-all-start.1 = ((f32[8,24,128]{2,1,0:T(8,128)}), f32[8,24,128]{2,1,0:T(8,128)S(1)}, u32[]{:S(2)}, u32[]{:S(2)}) async-start(f32[8,24,128]{2,1,0:T(8,128)} %broadcast_in_dim.4), calls=%async_computation.1 | async-start | bytes 196608 | tf_op jit(solution)/shard_map/all_to_all | solution.py:236
  52.2 2.6 %shard_map.70 = bf16[2,24,64,128]{3,2,1,0:T(8,128)(2,1)S(1)} custom-call(bf16[2,24,64,128]{3,2,1,0:T(8,128)(2,1)S(1)} %get-tuple-element.28.d_ref, bf16[64,128]{1,0:T(8,128)(2,1)S(1)} %slice_add_fusion.near_ref, bf16[64,128]{1,0:T(8,128)(2,1)S(1)} %broadcast_multiply_fusion.far_ref, f32[64,128]{1,0:T(8,128)S(1)} %get-tuple-element.31.slope_ref, ...), custom_call_target="tpu_custom_call" | custom-call | flops 4000000000 | bytes 4000000 | tf_op jit(solution)/shard_map/pallas_call | solution.py:224
  54.7 1.4 %copy.25 = bf16[2,24,64,128]{3,1,0,2:T(8,128)(2,1)} copy(bf16[2,24,64,128]{3,2,1,0:T(8,128)(2,1)S(1)} %shard_map.70) | data formatting | bytes 1572864 | tf_op jit(solution)/shard_map/pallas_call | solution.py:224
  56.1 3.5 %all-to-all-done.1 = f32[8,24,128]{2,1,0:T(8,128)S(1)} async-done(((f32[8,24,128]{2,1,0:T(8,128)}), f32[8,24,128]{2,1,0:T(8,128)S(1)}, u32[]{:S(2)}, u32[]{:S(2)}) %all-to-all-start.1) | async-done | bytes 98336 | tf_op jit(solution)/shard_map/all_to_all | solution.py:236
  59.7 9.4 %all_to_all.16 = bf16[16,24,128]{2,1,0:T(8,128)(2,1)S(1)} all-to-all(bf16[16,24,128]{2,1,0:T(8,128)(2,1)S(1)} %broadcast_in_dim.5), channel_id=1, replica_groups=mesh['y'=4,'xh'=2,'xl'=2,'z'=8,'c'=2] {'y','xh','xl'}, dimensions={0} | all-to-all | bytes 196608 | tf_op jit(solution)/shard_map/all_to_all | solution.py:236
  69.0 0.8 %shard_map.71 = (f32[3,3,64,64]{3,2,1,0:T(8,128)}, f32[3,64,64]{2,1,0:T(8,128)}) custom-call(bf16[2,192,128]{2,1,0:T(8,128)(2,1)S(1)} %bitcast.23), custom_call_target="tpu_custom_call" | custom-call | flops 1000000 | bytes 1000 | tf_op jit(solution)/shard_map/pallas_call | solution.py:224
  (6 shorter events, 0.1 us)
Async XLA Ops:
  0.6 23.4 %collective-permute-start = (bf16[64,2,24,128]{3,2,1,0:T(8,128)(2,1)}, bf16[64,2,24,128]{3,2,1,0:T(8,128)(2,1)S(1)}, u32[]{:S(2)}, u32[]{:S(2)}) collective-permute-start(bf16[64,2,24,128]{3,2,1,0:T(8,128)(2,1)} %param.5), channel_id=1, source_target_pairs={{32,0},{33,1},{34,2},{35,3},{36,4},{37,5},{38,6},{39,7},{40,8},{41... | collective-permute-start | bytes 2359304 | tf_op jit(solution)/shard_map/ppermute | solution.py:260
  6.7 6.8 %copy-start.1 = (bf16[3,64,64]{2,1,0:T(8,128)(2,1)S(1)}, bf16[3,64,64]{2,1,0:T(8,128)(2,1)}, u32[]{:S(2)}) copy-start(bf16[3,64,64]{2,1,0:T(8,128)(2,1)} %param.7) | copy-start | bytes 73732
  6.7 10.9 %copy-start = (bf16[3,3,64,64]{3,2,1,0:T(8,128)(2,1)S(1)}, bf16[3,3,64,64]{3,2,1,0:T(8,128)(2,1)}, u32[]{:S(2)}) copy-start(bf16[3,3,64,64]{3,2,1,0:T(8,128)(2,1)} %param.6) | copy-start | bytes 221188
  10.9 3.7 %collective-permute-start.1 = (bf16[192,128]{1,0:T(8,128)(2,1)S(1)}, bf16[192,128]{1,0:T(8,128)(2,1)S(1)}, u32[]{:S(2)}, u32[]{:S(2)}) collective-permute-start(bf16[192,128]{1,0:T(8,128)(2,1)S(1)} %get-tuple-element.20), channel_id=1, source_target_pairs={{31,0},{0,1},{1,2},{2,3},{3,4},{4,5},{5,6},{6,7},{7,8},{8,9},{9,10... | collective-permute-start | bytes 147464 | tf_op jit(solution)/shard_map/ppermute | solution.py:260
  13.5 3.8 %collective-permute-start.2 = (bf16[192,128]{1,0:T(8,128)(2,1)S(1)}, bf16[192,128]{1,0:T(8,128)(2,1)S(1)}, u32[]{:S(2)}, u32[]{:S(2)}) collective-permute-start(bf16[192,128]{1,0:T(8,128)(2,1)S(1)} %get-tuple-element.21), channel_id=1, source_target_pairs={{1,0},{2,1},{3,2},{4,3},{5,4},{6,5},{7,6},{8,7},{9,8},{10,9},{11,1... | collective-permute-start | bytes 147464 | tf_op jit(solution)/shard_map/ppermute | solution.py:260
  17.3 6.7 %collective-permute-start.3 = (bf16[64,128]{1,0:T(8,128)(2,1)S(1)}, bf16[64,128]{1,0:T(8,128)(2,1)S(1)}, u32[]{:S(2)}, u32[]{:S(2)}) collective-permute-start(bf16[64,128]{1,0:T(8,128)(2,1)S(1)} %slice_add_fusion.near_ref), channel_id=1, source_target_pairs={{32,0},{33,1},{34,2},{35,3},{36,4},{37,5},{38,6},{39,7},{40,8},{41... | collective-permute-start | bytes 49160 | tf_op jit(solution)/shard_map/ppermute | solution.py:260
  39.9 3.9 %collective-permute-start.4 = (f32[24,128]{1,0:T(8,128)S(1)}, f32[24,128]{1,0:T(8,128)S(1)}, u32[]{:S(2)}, u32[]{:S(2)}) collective-permute-start(f32[24,128]{1,0:T(8,128)S(1)} %reduce_sum.18), channel_id=1, source_target_pairs={{0,1},{1,0},{2,3},{3,2},{4,5},{5,4},{6,7},{7,6},{8,9},{9,8},{10,11... | collective-permute-start | bytes 36872 | tf_op jit(solution)/shard_map/ppermute | solution.py:247
  44.5 15.1 %all-to-all-start.1 = ((f32[8,24,128]{2,1,0:T(8,128)}), f32[8,24,128]{2,1,0:T(8,128)S(1)}, u32[]{:S(2)}, u32[]{:S(2)}) async-start(f32[8,24,128]{2,1,0:T(8,128)} %broadcast_in_dim.4), calls=%async_computation.1 | async-start | bytes 196608 | tf_op jit(solution)/shard_map/all_to_all | solution.py:236
